TPU v7x, 128 devices: a whole 4x4x4 slice. The times are simulated.
128 devices in a mesh: pair: 8 (over y, z_lo), virt: 16 (over z_hi, x, core).
Axes of the slice: x: 4, y: 4, z: 4 (z_hi: 2, z_lo: 2; z = z_hi * 2 + z_lo), core: 2. Of those that a mesh axis runs over, the one named last changes fastest.
Arguments:
- amplitudes: float32 [4096, 16384], P('pair', 'virt'), may hold values from -6 to 6
- integrals: bfloat16 [16384, 16384], P('pair', 'virt'), may hold values from -0.046875 to 0.046875
- occ_energy: float32 [4096], P('pair'), may hold values from 0.5 to 4
- vir_energy: float32 [16384], P('virt'), may hold values from 0.5 to 4
- tile_mask: int32 [512, 128], P('pair', 'virt'), may hold values 0 or 1
- partner_slot: int32 [512, 128], P('pair', 'virt'), may hold values from 0 to 127, as said below
Outputs:
- new_amplitudes: float32 [4096, 16384], P('pair', 'virt')
Inputs may be any that keep to these rules, and one draw needn't show every extreme that they name: `partner_slot`: within the block of tiles of each device (tile rows of one pair index by tile columns of one virt index), every device number 0 to 127 stands exactly 4 times, in an order drawn from the seed.
All inputs are finite; a program needn't handle non-finite values. No bound on the sum of `tile_mask` on one device may be relied on, other than what follows from the above.
Results may differ from a plain program's by a relative error of at most 0.0012.
Values may be sent and summed in bfloat16 or wider, within the bound.
No kernel may reach another device: no remote copies, remote signals or barrier semaphores. Data moves between devices by JAX's collectives and lax.ppermute only.
A program may use at most 128 MiB of HBM per device.

v0:
```python
import functools
import jax
import jax.numpy as jnp
from jax import lax
from jax.experimental import pallas as pl
from jax.experimental.pallas import tpu as pltpu
from jax.sharding import PartitionSpec as P

AXES = ("pair", "virt")
BF = jnp.bfloat16
F32 = jnp.float32


def decode(device):
    p, v = divmod(device, 16)
    y, zl = divmod(p, 2)
    zh, r = divmod(v, 8)
    x, c = divmod(r, 2)
    return x, y, zl, zh, c


def encode(x, y, zl, zh, c):
    return ((y % 4) * 2 + zl % 2) * 16 + (zh % 2) * 8 + (x % 4) * 2 + c % 2


def permutation(move):
    return [(d, encode(*move(*decode(d)))) for d in range(128)]


def shift(dx=0, dy=0, dzl=0, dzh=0, dc=0):
    return permutation(lambda x, y, zl, zh, c: (x + dx, y + dy, zl + dzl, zh + dzh, c + dc))


def spread(a):
    def move(x, y, zl, zh, c):
        fy, fzl = 2 * zh + x // 2, x % 2
        return (y - fy + a, fy, fzl, zl ^ fzl, c)

    return permutation(move)


def send(value, pairs):
    return lax.ppermute(value, AXES, pairs)


VMEM = pl.BlockSpec(memory_space=pltpu.VMEM)
SMEM = pl.BlockSpec(memory_space=pltpu.SMEM)


def params(megabytes=56):
    return pltpu.CompilerParams(vmem_limit_bytes=megabytes << 20)


def cost(flops, moved):
    return pl.CostEstimate(flops=flops, bytes_accessed=moved, transcendentals=0)


def split_kernel(where, amp, keep, give):
    for k, out in enumerate((keep, give)):
        for a in range(4):
            row = pl.multiple_of(where[2 * a + k] * 64, 64)
            out[a * 64 : a * 64 + 64, :] = amp[pl.ds(row, 64), :].astype(BF)


def split(amp, where):
    return pl.pallas_call(
        split_kernel,
        out_shape=[jax.ShapeDtypeStruct((256, 1024), BF)] * 2,
        in_specs=[SMEM, VMEM],
        out_specs=[VMEM] * 2,
        compiler_params=params(),
        cost_estimate=cost(0, 3 << 20),
        name="split",
    )(where, amp)


def weave_kernel(where, keep, got, *outs):
    own = pl.multiple_of(where[0] * 1024, 1024)
    oth = pl.multiple_of(1024 - where[0] * 1024, 1024)
    for a, out in enumerate(outs):
        out[:, pl.ds(own, 1024)] = keep[a * 64 : a * 64 + 64, :]
        out[:, pl.ds(oth, 1024)] = got[a * 64 : a * 64 + 64, :]


def weave(where, keep, got):
    return pl.pallas_call(
        weave_kernel,
        out_shape=[jax.ShapeDtypeStruct((64, 2048), BF)] * 4,
        in_specs=[SMEM] + [VMEM] * 2,
        out_specs=[VMEM] * 4,
        compiler_params=params(),
        cost_estimate=cost(0, 2 << 20),
        name="weave",
    )(where, keep, got)


def join_kernel(where, *refs):
    out = refs[-1]
    for a in range(4):
        out[pl.ds(pl.multiple_of(where[a] * 64, 64), 64), :] = refs[a][...]


def join(where, pieces):
    return pl.pallas_call(
        join_kernel,
        out_shape=jax.ShapeDtypeStruct((256, 2048), BF),
        in_specs=[SMEM] + [VMEM] * 4,
        out_specs=VMEM,
        compiler_params=params(),
        cost_estimate=cost(0, 2 << 20),
        name="join",
    )(where, *pieces)


def product_kernel(counts, *refs):
    n_in = sum(counts)
    n = len(counts)
    blocks = refs[:n_in]
    own, oth = refs[n_in : n_in + 2]
    p0, p1, p2, p3 = refs[n_in + 2 : n_in + 6]
    held = refs[n_in + 6]
    step = pl.program_id(0)

    @pl.when(step == 0)
    def _():
        at = 0
        for ref in blocks:
            rows = ref.shape[0]
            held[at : at + rows, :] = ref[...]
            at += rows

    def run(b):
        r = jnp.dot(held[...], b[...], preferred_element_type=F32)
        for i in range(n):
            base = i * 256
            p0[i * 64 : i * 64 + 64, :] = r[base : base + 64]
            p1[i * 64 : i * 64 + 64, :] = r[base + 64 : base + 128].astype(BF)
            p2[i * 64 : i * 64 + 64, :] = r[base + 128 : base + 192].astype(BF)
            p3[i * 64 : i * 64 + 64, :] = r[base + 192 : base + 256].astype(BF)

    @pl.when(step < 2)
    def _():
        run(own)

    @pl.when(step >= 2)
    def _():
        run(oth)


def product(groups, own, oth):
    flat = [a for g in groups for a in g]
    counts = tuple(len(g) for g in groups)
    n = len(groups)
    whole = lambda a: pl.BlockSpec(a.shape, lambda s: (0, 0))
    return pl.pallas_call(
        functools.partial(product_kernel, counts),
        out_shape=[jax.ShapeDtypeStruct((n * 64, 2048), F32)]
        + [jax.ShapeDtypeStruct((n * 64, 2048), BF)] * 3,
        grid=(4,),
        in_specs=[whole(a) for a in flat]
        + [
            pl.BlockSpec((2048, 512), lambda s: (0, jnp.minimum(s, 1))),
            pl.BlockSpec((2048, 512), lambda s: (0, jnp.maximum(s - 2, 0))),
        ],
        out_specs=[pl.BlockSpec((n * 64, 512), lambda s: (0, s))] * 4,
        scratch_shapes=[pltpu.VMEM((n * 256, 2048), BF)],
        compiler_params=params(),
        cost_estimate=cost(2 * n * 256 * 2048 * 2048, (9 << 20) + n * (3 << 20)),
        name="product",
    )(*flat, own, oth)


def outgoing_kernel(place, mask, order, *refs):
    parts = refs[:8]
    masked, out = refs[8:]
    x = place[0]
    c = place[1]
    for i in range(4):
        for other in range(2):
            part = parts[other * 4 + i]
            chunk = lax.rem(x + i, 4) * 2 + (1 - c if other else c)
            for t in range(8):
                for k in range(8):
                    w = mask[(chunk * 8 + t) * 8 + k].astype(F32)
                    masked[pl.ds(pl.multiple_of(chunk * 64 + t * 8, 8), 8), k * 128 : k * 128 + 128] = (
                        part[t * 8 : t * 8 + 8, k * 128 : k * 128 + 128] * w
                    )

    def gather(s, carry):
        rows = []
        for j in range(4):
            t = order[s * 4 + j]
            row = pl.multiple_of(lax.shift_right_logical(t, 3) * 8, 8)
            col = pl.multiple_of(lax.bitwise_and(t, 7) * 128, 128)
            rows.append(masked[pl.ds(row, 8), pl.ds(col, 128)])
        out[s] = jnp.concatenate(rows, axis=0).astype(BF)
        return carry

    lax.fori_loop(0, 128, gather, 0, unroll=4)


def outgoing(place, mask, order, kept, swapped):
    return pl.pallas_call(
        outgoing_kernel,
        out_shape=[
            jax.ShapeDtypeStruct((512, 1024), F32),
            jax.ShapeDtypeStruct((128, 32, 128), BF),
        ],
        in_specs=[SMEM] * 3 + [VMEM] * 8,
        out_specs=[VMEM] * 2,
        compiler_params=params(),
        cost_estimate=cost(0, 5 << 20),
        name="outgoing",
    )(place, mask, order, *kept, *swapped)


def update_kernel(inverse, incoming, masked, amp, occ, vir, out, wide):
    wide[...] = incoming[...].astype(F32)

    def row(r, carry):
        at = pl.multiple_of(r * 8, 8)
        e = occ[pl.ds(at, 8), :]
        for k in range(8):
            q = inverse[r * 8 + k]
            partner = wide[pl.ds(pl.multiple_of(q * 8, 8), 8), :]
            cols = slice(k * 128, k * 128 + 128)
            symmetric = masked[pl.ds(at, 8), cols] + partner
            out[pl.ds(at, 8), cols] = amp[pl.ds(at, 8), cols] - symmetric / (e + vir[:, cols])
        return carry

    lax.fori_loop(0, 64, row, 0, unroll=2)


def update(inverse, incoming, masked, amp, occ, vir):
    return pl.pallas_call(
        update_kernel,
        out_shape=jax.ShapeDtypeStruct((512, 1024), F32),
        in_specs=[SMEM] + [VMEM] * 5,
        out_specs=VMEM,
        scratch_shapes=[pltpu.VMEM((4096, 128), F32)],
        compiler_params=params(),
        cost_estimate=cost(0, 7 << 20),
        name="update",
    )(inverse, incoming, masked, amp, occ, vir)


GROUPS = (((0, 0),), ((0, 1), (1, 0), (3, 0)), ((1, 1), (3, 1)), ((2, 0), (2, 1)))
LAST = ((0,), (1, 3), (2,))


def compute(amplitudes, integrals, occ_energy, vir_energy, tile_mask, partner_slot):
    device = lax.axis_index(AXES)
    c, x, zh = device & 1, (device >> 1) & 3, (device >> 3) & 1
    y = (device >> 5) & 3
    fy = 2 * zh + (x >> 1)

    where = jnp.stack([((y - fy + a) & 3) * 2 + (c ^ b) for a in range(4) for b in range(2)])
    keep, give = split(amplitudes, where)
    got = send(give, shift(dc=1))
    pieces = weave(c[None], keep, got)
    moved = [send(pieces[a], spread(a)) for a in range(4)]
    own = integrals
    oth = send(integrals, shift(dc=1))
    block = {}
    block[0, 0] = join(jnp.stack([(x - a) & 3 for a in range(4)]), moved)

    block[1, 0] = send(block[0, 0], shift(dx=-1))
    block[3, 0] = send(block[0, 0], shift(dx=1))
    block[0, 1] = send(block[0, 0], shift(dzh=1))
    block[1, 1] = send(block[0, 1], shift(dx=-1))
    block[3, 1] = send(block[0, 1], shift(dx=1))
    parts = {k: (b,) for k, b in block.items()}
    for j in range(2):
        parts[2, j] = (
            send(block[1, j][:128], shift(dx=-1)), send(block[3, j][128:], shift(dx=1))
        )

    summed = {}
    for group in GROUPS:
        p0, p1, p2, p3 = product([parts[k] for k in group], own, oth)
        q2 = send(p2, shift(dy=2))
        q1 = send(p1, shift(dy=1))
        q3 = send(p3, shift(dy=-1))
        total = p0 + q1.astype(F32) + q3.astype(F32) + q2.astype(F32)
        for n, k in enumerate(group):
            summed[k] = total[n * 64 : n * 64 + 64]

    kept, swapped = [None] * 4, [None] * 4
    low = zh == 0
    for group in LAST:
        stay = [jnp.where(low, summed[i, 0], summed[i, 1]) for i in group]
        leave = [jnp.where(low, summed[i, 1], summed[i, 0]).astype(BF) for i in group]
        got = send(jnp.concatenate(leave, axis=0), shift(dzl=1)).astype(F32)
        done = jnp.concatenate(stay, axis=0) + got
        crossed = send(done[:, 1024:], shift(dc=1))
        for n, i in enumerate(group):
            kept[i] = done[n * 64 : n * 64 + 64, :1024]
            swapped[i] = crossed[n * 64 : n * 64 + 64]

    slots = partner_slot.reshape(-1)
    order = jnp.argsort(slots, stable=True).astype(jnp.int32)
    inverse = jnp.argsort(order, stable=True).astype(jnp.int32)
    place = jnp.stack([x, c])
    masked, out = outgoing(place, tile_mask.reshape(-1), order, kept, swapped)
    incoming = lax.all_to_all(out, AXES, split_axis=0, concat_axis=0, tiled=True)
    return update(
        inverse,
        incoming.reshape(4096, 128),
        masked,
        amplitudes,
        occ_energy[:, None],
        vir_energy[None, :],
    )


def solution(mesh):
    in_specs = (
        P("pair", "virt"),
        P("pair", "virt"),
        P("pair"),
        P("virt"),
        P("pair", "virt"),
        P("pair", "virt"),
    )
    out_specs = P("pair", "virt")
    return jax.shard_map(compute, mesh=mesh, in_specs=in_specs, out_specs=out_specs, check_vma=False)
```

profile of v0, /device:TPU:1, one launch (start us, length us, event | category | flops | bytes accessed | tf_op | source)
XLA Modules:
  0.0 310.4 jit_solution(4191225276885829423)
XLA Ops:
  4.7 4.4 %collective-permute-done.got = bf16[256,1024]{1,0:T(8,128)(2,1)S(1)} collective-permute-done((bf16[256,1024]{1,0:T(8,128)(2,1)}, bf16[256,1024]{1,0:T(8,128)(2,1)S(1)}, u32[]{:S(2)}, u32[]{:S(2)}) %collective-permute-start) | collective-permute-done | bytes 524320 | tf_op jit(solution)/shard_map/ppermute | solution.py:43
  13.7 7.3 %collective-permute-start.2 = (bf16[64,2048]{1,0:T(8,128)(2,1)}, bf16[64,2048]{1,0:T(8,128)(2,1)S(1)}, u32[]{:S(2)}, u32[]{:S(2)}) collective-permute-start(bf16[64,2048]{1,0:T(8,128)(2,1)} %get-tuple-element.36), channel_id=1, source_target_pairs={{0,2},{1,3},{2,26},{3,27},{4,32},{5,33},{6,56},{7,57},{8,70},{9,71... | collective-permute-start | bytes 786440 | tf_op jit(solution)/shard_map/ppermute | solution.py:43
  23.1 10.0 %collective-permute-start.4 = (bf16[64,2048]{1,0:T(8,128)(2,1)}, bf16[64,2048]{1,0:T(8,128)(2,1)S(1)}, u32[]{:S(2)}, u32[]{:S(2)}) collective-permute-start(bf16[64,2048]{1,0:T(8,128)(2,1)} %get-tuple-element.38), channel_id=1, source_target_pairs={{0,6},{1,7},{2,30},{3,31},{4,36},{5,37},{6,60},{7,61},{8,66},{9,67... | collective-permute-start | bytes 786440 | tf_op jit(solution)/shard_map/ppermute | solution.py:43
  44.2 15.2 %collective-permute-start.9 = (bf16[256,2048]{1,0:T(8,128)(2,1)}, bf16[256,2048]{1,0:T(8,128)(2,1)S(1)}, u32[]{:S(2)}, u32[]{:S(2)}) collective-permute-start(bf16[256,2048]{1,0:T(8,128)(2,1)} %join.1.refs_0_), channel_id=1, source_target_pairs={{0,8},{1,9},{2,10},{3,11},{4,12},{5,13},{6,14},{7,15},{8,0},{9,1},... | collective-permute-start | bytes 3145736 | tf_op jit(solution)/shard_map/ppermute | solution.py:43
  59.4 6.1 %collective-permute-start.10 = (bf16[256,2048]{1,0:T(8,128)(2,1)}, bf16[256,2048]{1,0:T(8,128)(2,1)S(1)}, u32[]{:S(2)}, u32[]{:S(2)}) collective-permute-start(bf16[256,2048]{1,0:T(8,128)(2,1)} %join.1.refs_0_), channel_id=1, source_target_pairs={{0,6},{1,7},{2,0},{3,1},{4,2},{5,3},{6,4},{7,5},{8,14},{9,15},{10,... | collective-permute-start | bytes 3145736 | tf_op jit(solution)/shard_map/ppermute | solution.py:43
  65.5 16.4 %collective-permute-done.9.refs_0_ = bf16[256,2048]{1,0:T(8,128)(2,1)S(1)} collective-permute-done((bf16[256,2048]{1,0:T(8,128)(2,1)}, bf16[256,2048]{1,0:T(8,128)(2,1)S(1)}, u32[]{:S(2)}, u32[]{:S(2)}) %collective-permute-start.9) | collective-permute-done | bytes 1048608 | tf_op jit(solution)/shard_map/ppermute | solution.py:43
  88.1 19.7 %collective-permute-done.16.refs_0_ = bf16[256,2048]{1,0:T(8,128)(2,1)S(1)} collective-permute-done((bf16[256,2048]{1,0:T(8,128)(2,1)S(1)}, bf16[256,2048]{1,0:T(8,128)(2,1)S(1)}, u32[]{:S(2)}, u32[]{:S(2)}) %collective-permute-start.16) | collective-permute-done | bytes 1048608 | tf_op jit(solution)/shard_map/ppermute | solution.py:43
  122.7 7.6 %collective-permute-done.24.refs_2_ = bf16[128,2048]{1,0:T(8,128)(2,1)} collective-permute-done((bf16[128,2048]{1,0:T(8,128)(2,1)S(1)}, bf16[128,2048]{1,0:T(8,128)(2,1)}, u32[]{:S(2)}, u32[]{:S(2)}) %collective-permute-start.24) | collective-permute-done | bytes 524320 | tf_op jit(solution)/shard_map/ppermute | solution.py:43
  133.9 9.5 %product.7 = (f32[128,2048]{1,0:T(8,128)}, bf16[128,2048]{1,0:T(8,128)(2,1)}, bf16[128,2048]{1,0:T(8,128)(2,1)}, bf16[128,2048]{1,0:T(8,128)(2,1)}) custom-call(bf16[128,2048]{1,0:T(8,128)(2,1)} %collective-permute-done.22.refs_0_, bf16[128,2048]{1,0:T(8,128)(2,1)} %collective-permute-done.23.refs_1_, bf16[128,2048]{1,0:T(8,128)(2,1)} %collective-permute-done.24.refs_2_, ...), custom_call_target="tpu_custom_call" | custom-call | flops 4294967296 | bytes 15728640 | tf_op jit(solution)/shard_map/product/pallas_call | solution.py:155
  143.4 5.0 %collective-permute-start.26 = (bf16[128,2048]{1,0:T(8,128)(2,1)}, bf16[128,2048]{1,0:T(8,128)(2,1)S(1)}, u32[]{:S(2)}, u32[]{:S(2)}) collective-permute-start(bf16[128,2048]{1,0:T(8,128)(2,1)} %get-tuple-element.52), channel_id=1, source_target_pairs={{0,32},{1,33},{2,34},{3,35},{4,36},{5,37},{6,38},{7,39},{8,40},{9,... | collective-permute-start | bytes 1572872 | tf_op jit(solution)/shard_map/ppermute | solution.py:43
  148.4 6.9 %collective-permute-start.27 = (bf16[128,2048]{1,0:T(8,128)(2,1)}, bf16[128,2048]{1,0:T(8,128)(2,1)S(1)}, u32[]{:S(2)}, u32[]{:S(2)}) collective-permute-start(bf16[128,2048]{1,0:T(8,128)(2,1)} %get-tuple-element.53), channel_id=1, source_target_pairs={{0,96},{1,97},{2,98},{3,99},{4,100},{5,101},{6,102},{7,103},{8,104... | collective-permute-start | bytes 1572872 | tf_op jit(solution)/shard_map/ppermute | solution.py:43
  157.7 11.7 %product.5 = (f32[192,2048]{1,0:T(8,128)}, bf16[192,2048]{1,0:T(8,128)(2,1)}, bf16[192,2048]{1,0:T(8,128)(2,1)}, bf16[192,2048]{1,0:T(8,128)(2,1)}) custom-call(bf16[256,2048]{1,0:T(8,128)(2,1)} %copy-done.20, bf16[256,2048]{1,0:T(8,128)(2,1)} %copy-done.14, bf16[256,2048]{1,0:T(8,128)(2,1)} %copy-done.15, bf16[2048,1024]{1,0:T(8,128)(2,1)} %refs_4_.1, ...), custom_call_target="tpu_custom_call" | custom-call | flops 6442450944 | bytes 18874368 | tf_op jit(solution)/shard_map/product/pallas_call | solution.py:155
  172.1 7.2 %product.4 = (f32[64,2048]{1,0:T(8,128)}, bf16[64,2048]{1,0:T(8,128)(2,1)}, bf16[64,2048]{1,0:T(8,128)(2,1)}, bf16[64,2048]{1,0:T(8,128)(2,1)}) custom-call(bf16[256,2048]{1,0:T(8,128)(2,1)} %join.1.refs_0_, bf16[2048,1024]{1,0:T(8,128)(2,1)} %refs_4_.1, bf16[2048,1024]{1,0:T(8,128)(2,1)} %collective-permute-done.5.refs_2_.refs_4_.refs_3_.refs_5_), custom_call_target="tpu_custom_call" | custom-call | flops 2147483648 | bytes 12582912 | tf_op jit(solution)/shard_map/product/pallas_call | solution.py:155
  179.3 9.6 %product.6 = (f32[128,2048]{1,0:T(8,128)}, bf16[128,2048]{1,0:T(8,128)(2,1)}, bf16[128,2048]{1,0:T(8,128)(2,1)}, bf16[128,2048]{1,0:T(8,128)(2,1)}) custom-call(bf16[256,2048]{1,0:T(8,128)(2,1)} %copy-done.12, bf16[256,2048]{1,0:T(8,128)(2,1)} %copy-done.13, bf16[2048,1024]{1,0:T(8,128)(2,1)} %refs_4_.1, ...), custom_call_target="tpu_custom_call" | custom-call | flops 4294967296 | bytes 15728640 | tf_op jit(solution)/shard_map/product/pallas_call | solution.py:155
  192.0 18.0 %collective-permute-done.18 = bf16[128,2048]{1,0:T(8,128)(2,1)S(1)} collective-permute-done((bf16[128,2048]{1,0:T(8,128)(2,1)}, bf16[128,2048]{1,0:T(8,128)(2,1)S(1)}, u32[]{:S(2)}, u32[]{:S(2)}) %collective-permute-start.18) | collective-permute-done | bytes 524320 | tf_op jit(solution)/shard_map/ppermute | solution.py:43
  210.0 7.9 %collective-permute-start.14 = (bf16[192,2048]{1,0:T(8,128)(2,1)S(1)}, bf16[192,2048]{1,0:T(8,128)(2,1)S(1)}, u32[]{:S(2)}, u32[]{:S(2)}) collective-permute-start(bf16[192,2048]{1,0:T(8,128)(2,1)S(1)} %copy-done.21), channel_id=1, source_target_pairs={{0,64},{1,65},{2,66},{3,67},{4,68},{5,69},{6,70},{7,71},{8,72},{9,... | collective-permute-start | bytes 2359304 | tf_op jit(solution)/shard_map/ppermute | solution.py:43
  221.7 11.5 %collective-permute-done.14 = bf16[192,2048]{1,0:T(8,128)(2,1)S(1)} collective-permute-done((bf16[192,2048]{1,0:T(8,128)(2,1)S(1)}, bf16[192,2048]{1,0:T(8,128)(2,1)S(1)}, u32[]{:S(2)}, u32[]{:S(2)}) %collective-permute-start.14) | collective-permute-done | bytes 786464 | tf_op jit(solution)/shard_map/ppermute | solution.py:43
  233.7 11.2 %collective-permute-done.6 = bf16[64,2048]{1,0:T(8,128)(2,1)S(1)} collective-permute-done((bf16[64,2048]{1,0:T(8,128)(2,1)S(1)}, bf16[64,2048]{1,0:T(8,128)(2,1)S(1)}, u32[]{:S(2)}, u32[]{:S(2)}) %collective-permute-start.6) | collective-permute-done | bytes 262176 | tf_op jit(solution)/shard_map/ppermute | solution.py:43
  246.9 15.2 %collective-permute-done.15 = bf16[64,2048]{1,0:T(8,128)(2,1)S(1)} collective-permute-done((bf16[64,2048]{1,0:T(8,128)(2,1)S(1)}, bf16[64,2048]{1,0:T(8,128)(2,1)S(1)}, u32[]{:S(2)}, u32[]{:S(2)}) %collective-permute-start.15) | collective-permute-done | bytes 262176 | tf_op jit(solution)/shard_map/ppermute | solution.py:43
  262.7 6.1 %collective-permute-start.31 = (f32[128,1024]{1,0:T(8,128)S(1)}, f32[128,1024]{1,0:T(8,128)S(1)}, u32[]{:S(2)}, u32[]{:S(2)}) collective-permute-start(f32[128,1024]{1,0:T(8,128)S(1)} %slice.96), channel_id=1, source_target_pairs={{0,1},{1,0},{2,3},{3,2},{4,5},{5,4},{6,7},{7,6},{8,9},{9,8},{10,11... | collective-permute-start | bytes 1572872 | tf_op jit(solution)/shard_map/ppermute | solution.py:43
  273.3 5.6 %outgoing.1 = (f32[512,1024]{1,0:T(8,128)}, bf16[128,32,128]{2,1,0:T(8,128)(2,1)}) custom-call(s32[2]{0:T(128)} %pad_add_fusion.place, s32[512]{0:T(512)} %reshape.10.mask, s32[512]{0:T(512)} %get-tuple-element.31.order, f32[64,1024]{1,0:T(8,128)} %get-tuple-element.70.refs_0_, f32[64,1024]{1,0:T(8,128)} %get-tuple-element.64.refs_1_, ...), custom_call_target="tpu_custom_call" | custom-call | bytes 5242880 | tf_op jit(solution)/shard_map/outgoing/pallas_call | solution.py:203
  278.8 4.8 %all-to-all-start = ((bf16[128,32,128]{2,1,0:T(8,128)(2,1)}), bf16[128,32,128]{2,1,0:T(8,128)(2,1)S(1)}, u32[]{:S(2)}, u32[]{:S(2)}) async-start(bf16[128,32,128]{2,1,0:T(8,128)(2,1)} %get-tuple-element.55), calls=%async_computation | async-start | bytes 2097152 | tf_op jit(solution)/shard_map/all_to_all | solution.py:305
  288.3 14.3 %all-to-all-done = bf16[128,32,128]{2,1,0:T(8,128)(2,1)S(1)} async-done(((bf16[128,32,128]{2,1,0:T(8,128)(2,1)}), bf16[128,32,128]{2,1,0:T(8,128)(2,1)S(1)}, u32[]{:S(2)}, u32[]{:S(2)}) %all-to-all-start) | async-done | bytes 1048608 | tf_op jit(solution)/shard_map/all_to_all | solution.py:305
  303.5 6.9 %update.1 = f32[512,1024]{1,0:T(8,128)} custom-call(s32[512]{0:T(512)} %get-tuple-element.32.inverse, bf16[4096,128]{1,0:T(8,128)(2,1)} %bitcast.17, f32[512,1024]{1,0:T(8,128)} %get-tuple-element.56.masked, f32[512,1024]{1,0:T(8,128)} %amp.3, f32[512,1]{1,0:T(8,128)} %copy.9.occ, f32[1,1024]{1,0:T(1,128)} %bitcast.18), custom_call_target="tpu_custom_call" | custom-call | bytes 7340032 | tf_op jit(solution)/shard_map/update/pallas_call | solution.py:235
  (133 shorter events, 72.1 us)
Async XLA Ops:
  0.0 133.9 %collective-permute-start.5 = (bf16[2048,1024]{1,0:T(8,128)(2,1)}, bf16[2048,1024]{1,0:T(8,128)(2,1)}, u32[]{:S(2)}, u32[]{:S(2)}) collective-permute-start(bf16[2048,1024]{1,0:T(8,128)(2,1)} %refs_4_.1), channel_id=1, source_target_pairs={{0,1},{1,0},{2,3},{3,2},{4,5},{5,4},{6,7},{7,6},{8,9},{9,8},{10,11... | collective-permute-start | bytes 12582920 | tf_op jit(solution)/shard_map/ppermute | solution.py:43
  12.2 21.6 %collective-permute-start.1 = (bf16[64,2048]{1,0:T(8,128)(2,1)}, bf16[64,2048]{1,0:T(8,128)(2,1)S(1)}, u32[]{:S(2)}, u32[]{:S(2)}) collective-permute-start(bf16[64,2048]{1,0:T(8,128)(2,1)} %get-tuple-element.35), channel_id=1, source_target_pairs={{0,0},{1,1},{2,24},{3,25},{4,38},{5,39},{6,62},{7,63},{8,68},{9,69... | collective-permute-start | bytes 786440 | tf_op jit(solution)/shard_map/ppermute | solution.py:43
  44.2 37.7 %collective-permute-start.9 = (bf16[256,2048]{1,0:T(8,128)(2,1)}, bf16[256,2048]{1,0:T(8,128)(2,1)S(1)}, u32[]{:S(2)}, u32[]{:S(2)}) collective-permute-start(bf16[256,2048]{1,0:T(8,128)(2,1)} %join.1.refs_0_), channel_id=1, source_target_pairs={{0,8},{1,9},{2,10},{3,11},{4,12},{5,13},{6,14},{7,15},{8,0},{9,1},... | collective-permute-start | bytes 3145736 | tf_op jit(solution)/shard_map/ppermute | solution.py:43
  59.4 25.5 %collective-permute-start.10 = (bf16[256,2048]{1,0:T(8,128)(2,1)}, bf16[256,2048]{1,0:T(8,128)(2,1)S(1)}, u32[]{:S(2)}, u32[]{:S(2)}) collective-permute-start(bf16[256,2048]{1,0:T(8,128)(2,1)} %join.1.refs_0_), channel_id=1, source_target_pairs={{0,6},{1,7},{2,0},{3,1},{4,2},{5,3},{6,4},{7,5},{8,14},{9,15},{10,... | collective-permute-start | bytes 3145736 | tf_op jit(solution)/shard_map/ppermute | solution.py:43
  65.5 22.3 %collective-permute-start.11 = (bf16[256,2048]{1,0:T(8,128)(2,1)}, bf16[256,2048]{1,0:T(8,128)(2,1)S(1)}, u32[]{:S(2)}, u32[]{:S(2)}) collective-permute-start(bf16[256,2048]{1,0:T(8,128)(2,1)} %join.1.refs_0_), channel_id=1, source_target_pairs={{0,2},{1,3},{2,4},{3,5},{4,6},{5,7},{6,0},{7,1},{8,10},{9,11},{10,... | collective-permute-start | bytes 3145736 | tf_op jit(solution)/shard_map/ppermute | solution.py:43
  81.9 25.9 %collective-permute-start.16 = (bf16[256,2048]{1,0:T(8,128)(2,1)S(1)}, bf16[256,2048]{1,0:T(8,128)(2,1)S(1)}, u32[]{:S(2)}, u32[]{:S(2)}) collective-permute-start(bf16[256,2048]{1,0:T(8,128)(2,1)S(1)} %collective-permute-done.9.refs_0_), channel_id=1, source_target_pairs={{0,6},{1,7},{2,0},{3,1},{4,2},{5,3},{6,4},{7,5},{8,14},{9,15},{10,... | collective-permute-start | bytes 3145736 | tf_op jit(solution)/shard_map/ppermute | solution.py:43
  84.9 26.5 %collective-permute-start.17 = (bf16[256,2048]{1,0:T(8,128)(2,1)S(1)}, bf16[256,2048]{1,0:T(8,128)(2,1)S(1)}, u32[]{:S(2)}, u32[]{:S(2)}) collective-permute-start(bf16[256,2048]{1,0:T(8,128)(2,1)S(1)} %collective-permute-done.9.refs_0_), channel_id=1, source_target_pairs={{0,2},{1,3},{2,4},{3,5},{4,6},{5,7},{6,0},{7,1},{8,10},{9,11},{10,... | collective-permute-start | bytes 3145736 | tf_op jit(solution)/shard_map/ppermute | solution.py:43
  84.9 34.1 %collective-permute-start.22 = (bf16[128,2048]{1,0:T(8,128)(2,1)S(1)}, bf16[128,2048]{1,0:T(8,128)(2,1)}, u32[]{:S(2)}, u32[]{:S(2)}) collective-permute-start(bf16[128,2048]{1,0:T(8,128)(2,1)S(1)} %slice.87), channel_id=1, source_target_pairs={{0,6},{1,7},{2,0},{3,1},{4,2},{5,3},{6,4},{7,5},{8,14},{9,15},{10,... | collective-permute-start | bytes 1572872 | tf_op jit(solution)/shard_map/ppermute | solution.py:43
  87.9 34.8 %collective-permute-start.23 = (bf16[128,2048]{1,0:T(8,128)(2,1)S(1)}, bf16[128,2048]{1,0:T(8,128)(2,1)}, u32[]{:S(2)}, u32[]{:S(2)}) collective-permute-start(bf16[128,2048]{1,0:T(8,128)(2,1)S(1)} %slice.88), channel_id=1, source_target_pairs={{0,2},{1,3},{2,4},{3,5},{4,6},{5,7},{6,0},{7,1},{8,10},{9,11},{10,... | collective-permute-start | bytes 1572872 | tf_op jit(solution)/shard_map/ppermute | solution.py:43
  107.9 22.4 %collective-permute-start.24 = (bf16[128,2048]{1,0:T(8,128)(2,1)S(1)}, bf16[128,2048]{1,0:T(8,128)(2,1)}, u32[]{:S(2)}, u32[]{:S(2)}) collective-permute-start(bf16[128,2048]{1,0:T(8,128)(2,1)S(1)} %slice.89), channel_id=1, source_target_pairs={{0,6},{1,7},{2,0},{3,1},{4,2},{5,3},{6,4},{7,5},{8,14},{9,15},{10,... | collective-permute-start | bytes 1572872 | tf_op jit(solution)/shard_map/ppermute | solution.py:43
  112.4 21.5 %collective-permute-start.25 = (bf16[128,2048]{1,0:T(8,128)(2,1)S(1)}, bf16[128,2048]{1,0:T(8,128)(2,1)}, u32[]{:S(2)}, u32[]{:S(2)}) collective-permute-start(bf16[128,2048]{1,0:T(8,128)(2,1)S(1)} %slice.90), channel_id=1, source_target_pairs={{0,2},{1,3},{2,4},{3,5},{4,6},{5,7},{6,0},{7,1},{8,10},{9,11},{10,... | collective-permute-start | bytes 1572872 | tf_op jit(solution)/shard_map/ppermute | solution.py:43
  143.4 45.5 %collective-permute-start.26 = (bf16[128,2048]{1,0:T(8,128)(2,1)}, bf16[128,2048]{1,0:T(8,128)(2,1)S(1)}, u32[]{:S(2)}, u32[]{:S(2)}) collective-permute-start(bf16[128,2048]{1,0:T(8,128)(2,1)} %get-tuple-element.52), channel_id=1, source_target_pairs={{0,32},{1,33},{2,34},{3,35},{4,36},{5,37},{6,38},{7,39},{8,40},{9,... | collective-permute-start | bytes 1572872 | tf_op jit(solution)/shard_map/ppermute | solution.py:43
  148.4 40.6 %collective-permute-start.27 = (bf16[128,2048]{1,0:T(8,128)(2,1)}, bf16[128,2048]{1,0:T(8,128)(2,1)S(1)}, u32[]{:S(2)}, u32[]{:S(2)}) collective-permute-start(bf16[128,2048]{1,0:T(8,128)(2,1)} %get-tuple-element.53), channel_id=1, source_target_pairs={{0,96},{1,97},{2,98},{3,99},{4,100},{5,101},{6,102},{7,103},{8,104... | collective-permute-start | bytes 1572872 | tf_op jit(solution)/shard_map/ppermute | solution.py:43
  155.3 36.4 %collective-permute-start.28 = (bf16[128,2048]{1,0:T(8,128)(2,1)}, bf16[128,2048]{1,0:T(8,128)(2,1)S(1)}, u32[]{:S(2)}, u32[]{:S(2)}) collective-permute-start(bf16[128,2048]{1,0:T(8,128)(2,1)} %get-tuple-element.54), channel_id=1, source_target_pairs={{0,64},{1,65},{2,66},{3,67},{4,68},{5,69},{6,70},{7,71},{8,72},{9,... | collective-permute-start | bytes 1572872 | tf_op jit(solution)/shard_map/ppermute | solution.py:43
  169.4 51.6 %collective-permute-start.12 = (bf16[192,2048]{1,0:T(8,128)(2,1)}, bf16[192,2048]{1,0:T(8,128)(2,1)S(1)}, u32[]{:S(2)}, u32[]{:S(2)}) collective-permute-start(bf16[192,2048]{1,0:T(8,128)(2,1)} %get-tuple-element.44), channel_id=1, source_target_pairs={{0,32},{1,33},{2,34},{3,35},{4,36},{5,37},{6,38},{7,39},{8,40},{9,... | collective-permute-start | bytes 2359304 | tf_op jit(solution)/shard_map/ppermute | solution.py:43
  169.4 52.2 %collective-permute-start.13 = (bf16[192,2048]{1,0:T(8,128)(2,1)}, bf16[192,2048]{1,0:T(8,128)(2,1)S(1)}, u32[]{:S(2)}, u32[]{:S(2)}) collective-permute-start(bf16[192,2048]{1,0:T(8,128)(2,1)} %get-tuple-element.45), channel_id=1, source_target_pairs={{0,96},{1,97},{2,98},{3,99},{4,100},{5,101},{6,102},{7,103},{8,104... | collective-permute-start | bytes 2359304 | tf_op jit(solution)/shard_map/ppermute | solution.py:43
  189.0 28.9 %collective-permute-start.19 = (bf16[128,2048]{1,0:T(8,128)(2,1)}, bf16[128,2048]{1,0:T(8,128)(2,1)S(1)}, u32[]{:S(2)}, u32[]{:S(2)}) collective-permute-start(bf16[128,2048]{1,0:T(8,128)(2,1)} %get-tuple-element.49), channel_id=1, source_target_pairs={{0,96},{1,97},{2,98},{3,99},{4,100},{5,101},{6,102},{7,103},{8,104... | collective-permute-start | bytes 1572872 | tf_op jit(solution)/shard_map/ppermute | solution.py:43
  191.7 26.4 %collective-permute-start.20 = (bf16[128,2048]{1,0:T(8,128)(2,1)}, bf16[128,2048]{1,0:T(8,128)(2,1)S(1)}, u32[]{:S(2)}, u32[]{:S(2)}) collective-permute-start(bf16[128,2048]{1,0:T(8,128)(2,1)} %get-tuple-element.50), channel_id=1, source_target_pairs={{0,64},{1,65},{2,66},{3,67},{4,68},{5,69},{6,70},{7,71},{8,72},{9,... | collective-permute-start | bytes 1572872 | tf_op jit(solution)/shard_map/ppermute | solution.py:43
  210.0 23.2 %collective-permute-start.14 = (bf16[192,2048]{1,0:T(8,128)(2,1)S(1)}, bf16[192,2048]{1,0:T(8,128)(2,1)S(1)}, u32[]{:S(2)}, u32[]{:S(2)}) collective-permute-start(bf16[192,2048]{1,0:T(8,128)(2,1)S(1)} %copy-done.21), channel_id=1, source_target_pairs={{0,64},{1,65},{2,66},{3,67},{4,68},{5,69},{6,70},{7,71},{8,72},{9,... | collective-permute-start | bytes 2359304 | tf_op jit(solution)/shard_map/ppermute | solution.py:43
  218.0 26.9 %collective-permute-start.6 = (bf16[64,2048]{1,0:T(8,128)(2,1)S(1)}, bf16[64,2048]{1,0:T(8,128)(2,1)S(1)}, u32[]{:S(2)}, u32[]{:S(2)}) collective-permute-start(bf16[64,2048]{1,0:T(8,128)(2,1)S(1)} %copy-done.24), channel_id=1, source_target_pairs={{0,32},{1,33},{2,34},{3,35},{4,36},{5,37},{6,38},{7,39},{8,40},{9,... | collective-permute-start | bytes 786440 | tf_op jit(solution)/shard_map/ppermute | solution.py:43
  218.1 26.8 %collective-permute-start.7 = (bf16[64,2048]{1,0:T(8,128)(2,1)S(1)}, bf16[64,2048]{1,0:T(8,128)(2,1)S(1)}, u32[]{:S(2)}, u32[]{:S(2)}) collective-permute-start(bf16[64,2048]{1,0:T(8,128)(2,1)S(1)} %copy-done.23), channel_id=1, source_target_pairs={{0,96},{1,97},{2,98},{3,99},{4,100},{5,101},{6,102},{7,103},{8,104... | collective-permute-start | bytes 786440 | tf_op jit(solution)/shard_map/ppermute | solution.py:43
  221.7 23.2 %collective-permute-start.8 = (bf16[64,2048]{1,0:T(8,128)(2,1)S(1)}, bf16[64,2048]{1,0:T(8,128)(2,1)S(1)}, u32[]{:S(2)}, u32[]{:S(2)}) collective-permute-start(bf16[64,2048]{1,0:T(8,128)(2,1)S(1)} %copy-done.22), channel_id=1, source_target_pairs={{0,64},{1,65},{2,66},{3,67},{4,68},{5,69},{6,70},{7,71},{8,72},{9,... | collective-permute-start | bytes 786440 | tf_op jit(solution)/shard_map/ppermute | solution.py:43
  221.7 25.1 %collective-permute-start.29 = (bf16[64,2048]{1,0:T(8,128)(2,1)S(1)}, bf16[64,2048]{1,0:T(8,128)(2,1)S(1)}, u32[]{:S(2)}, u32[]{:S(2)}) collective-permute-start(bf16[64,2048]{1,0:T(8,128)(2,1)S(1)} %select_convert_fusion), channel_id=1, source_target_pairs={{0,16},{1,17},{2,18},{3,19},{4,20},{5,21},{6,22},{7,23},{8,24},{9,... | collective-permute-start | bytes 786440 | tf_op jit(solution)/shard_map/ppermute | solution.py:43
  278.8 23.7 %all-to-all-start = ((bf16[128,32,128]{2,1,0:T(8,128)(2,1)}), bf16[128,32,128]{2,1,0:T(8,128)(2,1)S(1)}, u32[]{:S(2)}, u32[]{:S(2)}) async-start(bf16[128,32,128]{2,1,0:T(8,128)(2,1)} %get-tuple-element.55), calls=%async_computation | async-start | bytes 2097152 | tf_op jit(solution)/shard_map/all_to_all | solution.py:305
  (35 other events, 451.6 us)
where the time goes:
time: 311 us; the launch traced here: 310 us
  waiting for transfers between devices  134 us (43%)
  starting transfers between devices  96.5 us (31%)
  Pallas kernels  57.6 us (19%)
  local copies, waits for them, and re-layouts  10.8 us (3%)
  other arithmetic  10.8 us (3%)
    ppermute x33, waiting for transfers between devices, send(): return lax.ppermute(value, AXES, pairs)  120 us
    ppermute x33, starting transfers between devices, send(): return lax.ppermute(value, AXES, pairs)  91.7 us
    pallas_call x4, Pallas kernels, product(): pl.pallas_call(functools.partial(product_kernel, counts), out_shape=[jax....  38 us
    all_to_all x1, waiting for transfers between devices, compute(): lax.all_to_all(out, AXES, split_axis=0, concat_axis=0, tiled=True)  14.3 us
    pallas_call x1, Pallas kernels, update(): pl.pallas_call(update_kernel, out_shape=jax.ShapeDtypeStruct((512, 1024),...  6.87 us
  transfers between devices with their start and end apart: 34, of which 14 were waited for; matrix products, arithmetic and copies ran while one was open for 5% of the time, Pallas kernels for 11%

commit v1 on v0

v1 whole, which is shorter than its diff:
```python
import functools
import jax
import jax.numpy as jnp
from jax import lax
from jax.experimental import pallas as pl
from jax.experimental.pallas import tpu as pltpu
from jax.sharding import PartitionSpec as P

AXES = ("pair", "virt")
BF = jnp.bfloat16
F32 = jnp.float32


def decode(device):
    p, v = divmod(device, 16)
    y, zl = divmod(p, 2)
    zh, r = divmod(v, 8)
    x, c = divmod(r, 2)
    return x, y, zl, zh, c


def encode(x, y, zl, zh, c):
    return ((y % 4) * 2 + zl % 2) * 16 + (zh % 2) * 8 + (x % 4) * 2 + c % 2


def permutation(move):
    return [(d, encode(*move(*decode(d)))) for d in range(128)]


def shift(dx=0, dy=0, dzl=0, dzh=0, dc=0):
    return permutation(lambda x, y, zl, zh, c: (x + dx, y + dy, zl + dzl, zh + dzh, c + dc))


def spread(a):
    def move(x, y, zl, zh, c):
        fy, fzl = 2 * zh + x // 2, x % 2
        return (y - fy + a, y, fzl, zl ^ fzl, c)

    return permutation(move)


def settle(a):
    return permutation(lambda x, y, zl, zh, c: (x, y - x + a, zl, zh, c))


def send(value, pairs):
    return lax.ppermute(value, AXES, pairs)


VMEM = pl.BlockSpec(memory_space=pltpu.VMEM)
SMEM = pl.BlockSpec(memory_space=pltpu.SMEM)


def params(megabytes=56):
    return pltpu.CompilerParams(vmem_limit_bytes=megabytes << 20)


def cost(flops, moved):
    return pl.CostEstimate(flops=flops, bytes_accessed=moved, transcendentals=0)


def split_kernel(where, amp, keep, give):
    for k, out in enumerate((keep, give)):
        for a in range(4):
            row = pl.multiple_of(where[2 * a + k] * 64, 64)
            out[a * 64 : a * 64 + 64, :] = amp[pl.ds(row, 64), :].astype(BF)


def split(amp, where):
    return pl.pallas_call(
        split_kernel,
        out_shape=[jax.ShapeDtypeStruct((256, 1024), BF)] * 2,
        in_specs=[SMEM, VMEM],
        out_specs=[VMEM] * 2,
        compiler_params=params(),
        cost_estimate=cost(0, 3 << 20),
        name="split",
    )(where, amp)


def weave_kernel(where, keep, got, *outs):
    own = pl.multiple_of(where[0] * 1024, 1024)
    oth = pl.multiple_of(1024 - where[0] * 1024, 1024)
    for a, out in enumerate(outs):
        out[:, pl.ds(own, 1024)] = keep[a * 64 : a * 64 + 64, :]
        out[:, pl.ds(oth, 1024)] = got[a * 64 : a * 64 + 64, :]


def weave(where, keep, got):
    return pl.pallas_call(
        weave_kernel,
        out_shape=[jax.ShapeDtypeStruct((64, 2048), BF)] * 4,
        in_specs=[SMEM] + [VMEM] * 2,
        out_specs=[VMEM] * 4,
        compiler_params=params(),
        cost_estimate=cost(0, 2 << 20),
        name="weave",
    )(where, keep, got)


def join_kernel(where, *refs):
    out = refs[-1]
    for a in range(4):
        out[pl.ds(pl.multiple_of(where[a] * 64, 64), 64), :] = refs[a][...]


def join(where, pieces):
    return pl.pallas_call(
        join_kernel,
        out_shape=jax.ShapeDtypeStruct((256, 2048), BF),
        in_specs=[SMEM] + [VMEM] * 4,
        out_specs=VMEM,
        compiler_params=params(),
        cost_estimate=cost(0, 2 << 20),
        name="join",
    )(where, *pieces)


def product_kernel(counts, *refs):
    n_in = sum(counts)
    n = len(counts)
    blocks = refs[:n_in]
    own, oth = refs[n_in : n_in + 2]
    zero_a, zero_b, one_a, three_b, up, down = refs[n_in + 2 : n_in + 8]
    held = refs[n_in + 8]
    step = pl.program_id(0)

    @pl.when(step == 0)
    def _():
        at = 0
        for ref in blocks:
            rows = ref.shape[0]
            held[at : at + rows, :] = ref[...]
            at += rows

    def rows_of(r, i, k):
        return r[i * 256 + k * 64 : i * 256 + k * 64 + 64]

    @pl.when(step < 2)
    def _():
        r = jnp.dot(held[...], own[...], preferred_element_type=F32)
        for i in range(n):
            at = slice(i * 64, i * 64 + 64)
            zero_a[at, :] = rows_of(r, i, 0)
            one_a[at, :] = rows_of(r, i, 1)
            up[at, :] = rows_of(r, i, 2).astype(BF)
            down[at, :] = rows_of(r, i, 3).astype(BF)

    @pl.when(step >= 2)
    def _():
        r = jnp.dot(held[...], oth[...], preferred_element_type=F32)
        for i in range(n):
            at = slice(i * 64, i * 64 + 64)
            zero_b[at, :] = rows_of(r, i, 0)
            up[at, :] = rows_of(r, i, 1).astype(BF)
            down[at, :] = rows_of(r, i, 2).astype(BF)
            three_b[at, :] = rows_of(r, i, 3)


def product(groups, own, oth):
    flat = [a for g in groups for a in g]
    counts = tuple(len(g) for g in groups)
    n = len(groups)
    whole = lambda a: pl.BlockSpec(a.shape, lambda s: (0, 0))
    first = lambda s: (0, jnp.minimum(s, 1))
    second = lambda s: (0, jnp.maximum(s - 2, 0))
    half = jax.ShapeDtypeStruct((n * 64, 1024), F32)
    full = jax.ShapeDtypeStruct((n * 64, 2048), BF)
    out = lambda at: pl.BlockSpec((n * 64, 512), at)
    return pl.pallas_call(
        functools.partial(product_kernel, counts),
        out_shape=[half] * 4 + [full] * 2,
        grid=(4,),
        in_specs=[whole(a) for a in flat]
        + [pl.BlockSpec((2048, 512), first), pl.BlockSpec((2048, 512), second)],
        out_specs=[out(first), out(second), out(first), out(second)]
        + [out(lambda s: (0, s))] * 2,
        scratch_shapes=[pltpu.VMEM((n * 256, 2048), BF)],
        compiler_params=params(),
        cost_estimate=cost(2 * n * 256 * 2048 * 2048, (9 << 20) + n * (3 << 20)),
        name="product",
    )(*flat, own, oth)


def settle_kernel(n_groups, members, low, *refs):
    ins, outs = refs[: 6 * n_groups], refs[6 * n_groups :]
    stay_a, stay_b, leave_a, leave_b = outs

    def total(g, n):
        za, zb, up, down, nup, ndown = ins[6 * g : 6 * g + 6]
        at = slice(n * 64, n * 64 + 64)
        a = za[at, :] + down[at, :1024].astype(F32) + nup[at, :].astype(F32)
        b = zb[at, :] + up[at, 1024:].astype(F32) + ndown[at, :].astype(F32)
        return a, b

    def write(swap):
        for k, (c0, c1) in enumerate(members):
            at = slice(k * 64, k * 64 + 64)
            a, b = total(*(c1 if swap else c0))
            stay_a[at, :] = a
            stay_b[at, :] = b
            a, b = total(*(c0 if swap else c1))
            leave_a[at, :] = a.astype(BF)
            leave_b[at, :] = b.astype(BF)

    @pl.when(low[0] == 1)
    def _():
        write(False)

    @pl.when(low[0] == 0)
    def _():
        write(True)


def collect(low, groups, members):
    rows = 64 * len(members)
    flat = [a for g in groups for a in g]
    return pl.pallas_call(
        functools.partial(settle_kernel, len(groups), members),
        out_shape=[jax.ShapeDtypeStruct((rows, 1024), F32)] * 2
        + [jax.ShapeDtypeStruct((rows, 1024), BF)] * 2,
        in_specs=[SMEM] + [VMEM] * len(flat),
        out_specs=[VMEM] * 4,
        compiler_params=params(),
        cost_estimate=cost(0, rows * 1024 * 24),
        name="collect",
    )(low, *flat)


def outgoing_kernel(code, *refs):
    full, out = refs[-2:]
    at = 0
    for k in (0, 2):
        for g in range(2):
            stay, got = refs[4 * g + k : 4 * g + k + 2]
            rows = stay.shape[0]
            full[at : at + rows, :] = stay[...] + got[...].astype(F32)
            at += rows

    def gather(s, carry):
        rows = []
        for j in range(4):
            q = code[s * 4 + j]
            row = pl.multiple_of(lax.shift_right_logical(q, 4) * 8, 8)
            col = pl.multiple_of(lax.bitwise_and(lax.shift_right_logical(q, 1), 7) * 128, 128)
            w = lax.bitwise_and(q, 1).astype(F32)
            rows.append(full[pl.ds(row, 8), pl.ds(col, 128)] * w)
        out[s] = jnp.concatenate(rows, axis=0).astype(BF)
        return carry

    lax.fori_loop(0, 128, gather, 0, unroll=4)


def outgoing(code, *parts):
    return pl.pallas_call(
        outgoing_kernel,
        out_shape=[
            jax.ShapeDtypeStruct((512, 1024), F32),
            jax.ShapeDtypeStruct((128, 32, 128), BF),
        ],
        in_specs=[SMEM] + [VMEM] * 8,
        out_specs=[VMEM] * 2,
        compiler_params=params(),
        cost_estimate=cost(0, 6 << 20),
        name="outgoing",
    )(code, *parts)


def base_kernel(row_of, mask, full, amp, occ, vir, base, scale):
    def row(r, carry):
        at = pl.multiple_of(r * 8, 8)
        src = pl.multiple_of(row_of[r], 8)
        e = occ[pl.ds(at, 8), :]
        for k in range(8):
            w = mask[r * 8 + k].astype(F32)
            cols = slice(k * 128, k * 128 + 128)
            q = 1.0 / (e + vir[:, cols])
            scale[pl.ds(at, 8), cols] = q
            base[pl.ds(at, 8), cols] = amp[pl.ds(at, 8), cols] - full[pl.ds(src, 8), cols] * w * q
        return carry

    lax.fori_loop(0, 64, row, 0, unroll=2)


def make_base(row_of, mask, full, amp, occ, vir):
    return pl.pallas_call(
        base_kernel,
        out_shape=[jax.ShapeDtypeStruct((512, 1024), F32)] * 2,
        in_specs=[SMEM] * 2 + [VMEM] * 4,
        out_specs=[VMEM] * 2,
        compiler_params=params(),
        cost_estimate=cost(0, 8 << 20),
        name="base",
    )(row_of, mask, full, amp, occ, vir)


def update_kernel(inverse, incoming, base, scale, out, wide):
    wide[...] = incoming[...].astype(F32)

    def row(r, carry):
        at = pl.multiple_of(r * 8, 8)
        for k in range(8):
            q = inverse[r * 8 + k]
            partner = wide[pl.ds(pl.multiple_of(q * 8, 8), 8), :]
            cols = slice(k * 128, k * 128 + 128)
            out[pl.ds(at, 8), cols] = base[pl.ds(at, 8), cols] - partner * scale[pl.ds(at, 8), cols]
        return carry

    lax.fori_loop(0, 64, row, 0, unroll=4)


def update(inverse, incoming, base, scale):
    return pl.pallas_call(
        update_kernel,
        out_shape=jax.ShapeDtypeStruct((512, 1024), F32),
        in_specs=[SMEM] + [VMEM] * 3,
        out_specs=VMEM,
        scratch_shapes=[pltpu.VMEM((4096, 128), F32)],
        compiler_params=params(),
        cost_estimate=cost(0, 7 << 20),
        name="update",
    )(inverse, incoming, base, scale)


GROUPS = (((0, 0),), ((0, 1), (1, 0), (3, 0)), ((1, 1), (3, 1)), ((2, 0), (2, 1)))
LAST = (
    ((0, 1, 2), (((0, 0), (1, 0)), ((1, 1), (2, 0)), ((1, 2), (2, 1)))),
    ((3,), (((0, 0), (0, 1)),)),
)


def compute(amplitudes, integrals, occ_energy, vir_energy, tile_mask, partner_slot):
    device = lax.axis_index(AXES)
    c, x, zh = device & 1, (device >> 1) & 3, (device >> 3) & 1
    y = (device >> 5) & 3
    fy = 2 * zh + (x >> 1)

    where = jnp.stack([((y - fy + a) & 3) * 2 + (c ^ b) for a in range(4) for b in range(2)])
    keep, give = split(amplitudes, where)
    got = send(give, shift(dc=1))
    pieces = weave(c[None], keep, got)
    moved = [send(pieces[a], spread(a)) for a in range(4)]
    moved = [send(moved[a], settle(a)) for a in range(4)]
    own = integrals
    oth = send(integrals, shift(dc=1))
    block = {}
    block[0, 0] = join(jnp.stack([(x - a) & 3 for a in range(4)]), moved)

    block[1, 0] = send(block[0, 0], shift(dx=-1))
    block[3, 0] = send(block[0, 0], shift(dx=1))
    block[0, 1] = send(block[0, 0], shift(dzh=1))
    block[1, 1] = send(block[0, 1], shift(dx=-1))
    block[3, 1] = send(block[0, 1], shift(dx=1))
    parts = {k: (b,) for k, b in block.items()}
    for j in range(2):
        parts[2, j] = (send(block[1, j][:128], shift(dx=-1)), send(block[3, j][128:], shift(dx=1)))

    sums = []
    for group in GROUPS:
        za, zb, one_a, three_b, up, down = product([parts[k] for k in group], own, oth)
        up = send(up, shift(dy=1))
        down = send(down, shift(dy=-1))
        nup = (one_a + up[:, :1024].astype(F32)).astype(BF)
        ndown = (three_b + down[:, 1024:].astype(F32)).astype(BF)
        nup = send(nup, shift(dy=1))
        ndown = send(ndown, shift(dy=-1))
        sums.append((za, zb, up, down, nup, ndown))

    low = (zh == 0).astype(jnp.int32)[None]
    last = []
    for groups, members in LAST:
        stay_a, stay_b, leave_a, leave_b = collect(low, [sums[k] for k in groups], members)
        got_a = send(leave_a, shift(dzl=1))
        got_b = send(leave_b, shift(dzl=1, dc=1))
        stay_b = send(stay_b, shift(dc=1))
        last += [stay_a, got_a, stay_b, got_b]

    slots = partner_slot.reshape(-1)
    mask = tile_mask.reshape(-1)
    order = jnp.argsort(slots, stable=True).astype(jnp.int32)
    inverse = jnp.argsort(order, stable=True).astype(jnp.int32)
    tile_row = jnp.arange(64, dtype=jnp.int32)
    part = ((tile_row >> 4) - x) & 3
    part = (((tile_row >> 3) & 1) ^ c) * 4 + (part ^ (part >> 1))
    row_of = part * 64 + (tile_row & 7) * 8
    tile = jnp.arange(512, dtype=jnp.int32)
    code = ((jnp.repeat(row_of, 8) >> 3) << 4) + ((tile & 7) << 1) + mask
    code = jnp.take(code, order)
    full, out = outgoing(code, *last)
    incoming = lax.all_to_all(out, AXES, split_axis=0, concat_axis=0, tiled=True)
    base, scale = make_base(
        row_of, mask, full, amplitudes, occ_energy[:, None], vir_energy[None, :]
    )
    return update(inverse, incoming.reshape(4096, 128), base, scale)


def solution(mesh):
    in_specs = (
        P("pair", "virt"),
        P("pair", "virt"),
        P("pair"),
        P("virt"),
        P("pair", "virt"),
        P("pair", "virt"),
    )
    out_specs = P("pair", "virt")
    return jax.shard_map(compute, mesh=mesh, in_specs=in_specs, out_specs=out_specs, check_vma=False)
```

time: 311 us -> 313 us (level)
  starting transfers between devices: 96.5 us -> 69.6 us
  waiting for transfers between devices: 134 us -> 148 us
  Pallas kernels: 57.6 us -> 71.5 us
    ppermute x33 -> x41, starting transfers between devices: 91.7 us -> 65.8 us  [send(): return lax.ppermute(value, AXES, pairs)]
    ppermute x33 -> x41, waiting for transfers between devices: 120 us -> 140 us  [send(): return lax.ppermute(value, AXES, pairs)]
    pallas_call x4 -> x7, Pallas kernels: 38 us -> 53.9 us  [the longest x4 38.8 us: product(): pl.pallas_call(functools.partial(product_kernel, counts), out_shape=[half...]
    all_to_all x1, waiting for transfers between devices: 14.3 us -> 7.43 us  [compute(): lax.all_to_all(out, AXES, split_axis=0, concat_axis=0, tiled=True)]
    gather x0 -> x1, local copies, waits for them, and re-layouts: none -> 3.49 us  [compute(): code = jnp.take(code, order)]
    slice x5 -> x0, local copies, waits for them, and re-layouts: 3.2 us -> none  [the longest x3 1.53 us: compute(): crossed = send(done[:, 1024:], shift(dc=1))]
    unnamed x52 -> x100, local copies, waits for them, and re-layouts: 5.17 us -> 7.75 us
  transfers between devices with their start and end apart: 34 -> 42, of which waited for: 14 -> 17; matrix products, arithmetic and copies ran while one was open for 5% -> 5% of each run, Pallas kernels for 11% -> 16%
where the time goes in v1:
time: 313 us
  waiting for transfers between devices  148 us (47%)
  Pallas kernels  71.5 us (23%)
  starting transfers between devices  69.6 us (22%)
  local copies, waits for them, and re-layouts  13.2 us (4%)
  other arithmetic  9.85 us (3%)
    ppermute x41, waiting for transfers between devices, send(): return lax.ppermute(value, AXES, pairs)  140 us
    ppermute x41, starting transfers between devices, send(): return lax.ppermute(value, AXES, pairs)  65.8 us
    pallas_call x4, Pallas kernels, product(): pl.pallas_call(functools.partial(product_kernel, counts), out_shape=[half...  38.8 us
    pallas_call x2, Pallas kernels, collect(): pl.pallas_call(functools.partial(settle_kernel, len(groups), members), ou...  8.08 us
    unnamed x100, local copies, waits for them, and re-layouts  7.75 us
    all_to_all x1, waiting for transfers between devices, compute(): lax.all_to_all(out, AXES, split_axis=0, concat_axis=0, tiled=True)  7.43 us
    pallas_call x1, Pallas kernels, make_base(): pl.pallas_call(base_kernel, out_shape=[jax.ShapeDtypeStruct((512, 1024),...  7.01 us
  transfers between devices with their start and end apart: 42, of which 17 were waited for; matrix products, arithmetic and copies ran while one was open for 5% of the time, Pallas kernels for 16%

profile of v1, /device:TPU:1, one launch (start us, length us, event | category | flops | bytes accessed | tf_op | source)
XLA Modules:
  0.0 312.6 jit_solution(8197144878880087690)
XLA Ops:
  4.7 4.5 %collective-permute-done.got = bf16[256,1024]{1,0:T(8,128)(2,1)S(1)} collective-permute-done((bf16[256,1024]{1,0:T(8,128)(2,1)}, bf16[256,1024]{1,0:T(8,128)(2,1)S(1)}, u32[]{:S(2)}, u32[]{:S(2)}) %collective-permute-start) | collective-permute-done | bytes 524320 | tf_op jit(solution)/shard_map/ppermute | solution.py:47
  13.7 7.3 %collective-permute-start.3 = (bf16[64,2048]{1,0:T(8,128)(2,1)}, bf16[64,2048]{1,0:T(8,128)(2,1)S(1)}, u32[]{:S(2)}, u32[]{:S(2)}) collective-permute-start(bf16[64,2048]{1,0:T(8,128)(2,1)} %get-tuple-element.54), channel_id=1, source_target_pairs={{0,2},{1,3},{2,26},{3,27},{4,0},{5,1},{6,24},{7,25},{8,6},{9,7},{1... | collective-permute-start | bytes 786440 | tf_op jit(solution)/shard_map/ppermute | solution.py:47
  22.9 5.7 %collective-permute-start.7 = (bf16[64,2048]{1,0:T(8,128)(2,1)}, bf16[64,2048]{1,0:T(8,128)(2,1)S(1)}, u32[]{:S(2)}, u32[]{:S(2)}) collective-permute-start(bf16[64,2048]{1,0:T(8,128)(2,1)} %get-tuple-element.56), channel_id=1, source_target_pairs={{0,6},{1,7},{2,30},{3,31},{4,4},{5,5},{6,28},{7,29},{8,2},{9,3},{1... | collective-permute-start | bytes 786440 | tf_op jit(solution)/shard_map/ppermute | solution.py:47
  32.4 17.3 %collective-permute-done.5 = bf16[64,2048]{1,0:T(8,128)(2,1)S(1)} collective-permute-done((bf16[64,2048]{1,0:T(8,128)(2,1)}, bf16[64,2048]{1,0:T(8,128)(2,1)S(1)}, u32[]{:S(2)}, u32[]{:S(2)}) %collective-permute-start.5) | collective-permute-done | bytes 262176 | tf_op jit(solution)/shard_map/ppermute | solution.py:47
  54.3 5.2 %collective-permute-done.6.refs_2_ = bf16[64,2048]{1,0:T(8,128)(2,1)S(1)} collective-permute-done((bf16[64,2048]{1,0:T(8,128)(2,1)S(1)}, bf16[64,2048]{1,0:T(8,128)(2,1)S(1)}, u32[]{:S(2)}, u32[]{:S(2)}) %collective-permute-start.6) | collective-permute-done | bytes 262176 | tf_op jit(solution)/shard_map/ppermute | solution.py:47
  67.2 20.0 %collective-permute-done.14.refs_0_ = bf16[256,2048]{1,0:T(8,128)(2,1)S(1)} collective-permute-done((bf16[256,2048]{1,0:T(8,128)(2,1)}, bf16[256,2048]{1,0:T(8,128)(2,1)S(1)}, u32[]{:S(2)}, u32[]{:S(2)}) %collective-permute-start.14) | collective-permute-done | bytes 1048608 | tf_op jit(solution)/shard_map/ppermute | solution.py:47
  91.4 19.7 %collective-permute-done.21.refs_0_ = bf16[256,2048]{1,0:T(8,128)(2,1)S(1)} collective-permute-done((bf16[256,2048]{1,0:T(8,128)(2,1)S(1)}, bf16[256,2048]{1,0:T(8,128)(2,1)S(1)}, u32[]{:S(2)}, u32[]{:S(2)}) %collective-permute-start.21) | collective-permute-done | bytes 1048608 | tf_op jit(solution)/shard_map/ppermute | solution.py:47
  113.8 8.7 %collective-permute-done.30.refs_0_ = bf16[128,2048]{1,0:T(8,128)(2,1)} collective-permute-done((bf16[128,2048]{1,0:T(8,128)(2,1)S(1)}, bf16[128,2048]{1,0:T(8,128)(2,1)}, u32[]{:S(2)}, u32[]{:S(2)}) %collective-permute-start.30) | collective-permute-done | bytes 524320 | tf_op jit(solution)/shard_map/ppermute | solution.py:47
  123.7 10.0 %collective-permute-done.32.refs_2_ = bf16[128,2048]{1,0:T(8,128)(2,1)} collective-permute-done((bf16[128,2048]{1,0:T(8,128)(2,1)S(1)}, bf16[128,2048]{1,0:T(8,128)(2,1)}, u32[]{:S(2)}, u32[]{:S(2)}) %collective-permute-start.32) | collective-permute-done | bytes 524320 | tf_op jit(solution)/shard_map/ppermute | solution.py:47
  134.9 9.7 %product.7 = (f32[128,1024]{1,0:T(8,128)}, f32[128,1024]{1,0:T(8,128)}, f32[128,1024]{1,0:T(8,128)}, f32[128,1024]{1,0:T(8,128)}, bf16[128,2048]{1,0:T(8,128)(2,1)}, /*index=5*/bf16[128,2048]{1,0:T(8,128)(2,1)}) custom-call(bf16[128,2048]{1,0:T(8,128)(2,1)} %collective-permute-done.30.refs_0_, bf16[128,2048]{1,0:T(8,128)(2,1)} %collective-permute-done.31.refs_1_, ...), custom_call_target="tpu_custom_call" | custom-call | flops 4294967296 | bytes 15728640 | tf_op jit(solution)/shard_map/product/pallas_call | solution.py:170
  147.7 9.6 %product.6 = (f32[128,1024]{1,0:T(8,128)}, f32[128,1024]{1,0:T(8,128)}, f32[128,1024]{1,0:T(8,128)}, f32[128,1024]{1,0:T(8,128)}, bf16[128,2048]{1,0:T(8,128)(2,1)}, /*index=5*/bf16[128,2048]{1,0:T(8,128)(2,1)}) custom-call(bf16[256,2048]{1,0:T(8,128)(2,1)} %copy-done.29, bf16[256,2048]{1,0:T(8,128)(2,1)} %copy-done.30, bf16[2048,1024]{1,0:T(8,128)(2,1)} %refs_4_.1, ...), custom_call_target="tpu_custom_call" | custom-call | flops 4294967296 | bytes 15728640 | tf_op jit(solution)/shard_map/product/pallas_call | solution.py:170
  159.5 7.4 %product.4 = (f32[64,1024]{1,0:T(8,128)}, f32[64,1024]{1,0:T(8,128)}, f32[64,1024]{1,0:T(8,128)}, f32[64,1024]{1,0:T(8,128)}, bf16[64,2048]{1,0:T(8,128)(2,1)}, /*index=5*/bf16[64,2048]{1,0:T(8,128)(2,1)}) custom-call(bf16[256,2048]{1,0:T(8,128)(2,1)} %join.1.refs_0_, bf16[2048,1024]{1,0:T(8,128)(2,1)} %refs_4_.1, ...), custom_call_target="tpu_custom_call" | custom-call | flops 2147483648 | bytes 12582912 | tf_op jit(solution)/shard_map/product/pallas_call | solution.py:170
  169.1 12.2 %product.5 = (f32[192,1024]{1,0:T(8,128)}, f32[192,1024]{1,0:T(8,128)}, f32[192,1024]{1,0:T(8,128)}, f32[192,1024]{1,0:T(8,128)}, bf16[192,2048]{1,0:T(8,128)(2,1)}, /*index=5*/bf16[192,2048]{1,0:T(8,128)(2,1)}) custom-call(bf16[256,2048]{1,0:T(8,128)(2,1)} %copy-done.44, bf16[256,2048]{1,0:T(8,128)(2,1)} %copy-done.27, bf16[256,2048]{1,0:T(8,128)(2,1)} %copy-done.28, ...), custom_call_target="tpu_custom_call" | custom-call | flops 6442450944 | bytes 18874368 | tf_op jit(solution)/shard_map/product/pallas_call | solution.py:170
  187.1 10.3 %collective-permute-done.18.refs_9_ = bf16[192,2048]{1,0:T(8,128)(2,1)S(1)} collective-permute-done((bf16[192,2048]{1,0:T(8,128)(2,1)}, bf16[192,2048]{1,0:T(8,128)(2,1)S(1)}, u32[]{:S(2)}, u32[]{:S(2)}) %collective-permute-start.18) | collective-permute-done | bytes 786464 | tf_op jit(solution)/shard_map/ppermute | solution.py:47
  203.8 7.9 %collective-permute-done.34.refs_2_ = bf16[128,2048]{1,0:T(8,128)(2,1)S(1)} collective-permute-done((bf16[128,2048]{1,0:T(8,128)(2,1)S(1)}, bf16[128,2048]{1,0:T(8,128)(2,1)S(1)}, u32[]{:S(2)}, u32[]{:S(2)}) %collective-permute-start.34) | collective-permute-done | bytes 524320 | tf_op jit(solution)/shard_map/ppermute | solution.py:47
  211.8 16.8 %collective-permute-done.12.refs_4_ = bf16[64,1024]{1,0:T(8,128)(2,1)S(1)} collective-permute-done((bf16[64,1024]{1,0:T(8,128)(2,1)S(1)}, bf16[64,1024]{1,0:T(8,128)(2,1)S(1)}, u32[]{:S(2)}, u32[]{:S(2)}) %collective-permute-start.12) | collective-permute-done | bytes 131104 | tf_op jit(solution)/shard_map/ppermute | solution.py:47
  231.1 5.3 %collect.2 = (f32[192,1024]{1,0:T(8,128)}, f32[192,1024]{1,0:T(8,128)}, bf16[192,1024]{1,0:T(8,128)(2,1)}, bf16[192,1024]{1,0:T(8,128)(2,1)}) custom-call(s32[1]{0:T(128)} %bitcast.low, f32[64,1024]{1,0:T(8,128)} %get-tuple-element.57.refs_0_, f32[64,1024]{1,0:T(8,128)} %get-tuple-element.58.refs_1_, bf16[64,2048]{1,0:T(8,128)(2,1)} %copy-done.11, ...), custom_call_target="tpu_custom_call" | custom-call | bytes 4718592 | tf_op jit(solution)/shard_map/collect/pallas_call | solution.py:218
  236.4 6.1 %collective-permute-start.28 = (f32[192,1024]{1,0:T(8,128)}, f32[192,1024]{1,0:T(8,128)S(1)}, u32[]{:S(2)}, u32[]{:S(2)}) collective-permute-start(f32[192,1024]{1,0:T(8,128)} %get-tuple-element.77), channel_id=1, source_target_pairs={{0,1},{1,0},{2,3},{3,2},{4,5},{5,4},{6,7},{7,6},{8,9},{9,8},{10,11... | collective-permute-start | bytes 2359304 | tf_op jit(solution)/shard_map/ppermute | solution.py:47
  260.3 16.7 %collective-permute-done.40.refs_7_ = bf16[64,1024]{1,0:T(8,128)(2,1)S(1)} collective-permute-done((bf16[64,1024]{1,0:T(8,128)(2,1)S(1)}, bf16[64,1024]{1,0:T(8,128)(2,1)S(1)}, u32[]{:S(2)}, u32[]{:S(2)}) %collective-permute-start.40) | collective-permute-done | bytes 131104 | tf_op jit(solution)/shard_map/ppermute | solution.py:47
  278.3 5.6 %outgoing.1 = (f32[512,1024]{1,0:T(8,128)}, bf16[128,32,128]{2,1,0:T(8,128)(2,1)}) custom-call(s32[512]{0:T(512)} %and_select_fusion.code, f32[192,1024]{1,0:T(8,128)} %get-tuple-element.75.refs_0_, bf16[192,1024]{1,0:T(8,128)(2,1)} %copy-done.19, f32[192,1024]{1,0:T(8,128)} %copy-done.9, bf16[192,1024]{1,0:T(8,128)(2,1)} %copy-done.20, ...), custom_call_target="tpu_custom_call" | custom-call | bytes 6291456 | tf_op jit(solution)/shard_map/outgoing/pallas_call | solution.py:255
  283.9 3.8 %all-to-all-start = ((bf16[128,32,128]{2,1,0:T(8,128)(2,1)}), bf16[128,32,128]{2,1,0:T(8,128)(2,1)S(1)}, u32[]{:S(2)}, u32[]{:S(2)}) async-start(bf16[128,32,128]{2,1,0:T(8,128)(2,1)} %get-tuple-element.89), calls=%async_computation | async-start | bytes 2097152 | tf_op jit(solution)/shard_map/all_to_all | solution.py:390
  292.4 7.0 %base.1 = (f32[512,1024]{1,0:T(8,128)}, f32[512,1024]{1,0:T(8,128)}) custom-call(s32[64]{0:T(128)} %get-tuple-element.94.row_of, s32[512]{0:T(512)} %copy-done.40, f32[512,1024]{1,0:T(8,128)} %get-tuple-element.90.full, f32[512,1024]{1,0:T(8,128)} %amp.3, f32[512,1]{1,0:T(8,128)} %copy.9.occ, f32[1,1024]{1,0:T(1,128)} %bitcast.18), custom_call_target="tpu_custom_call" | custom-call | bytes 8388608 | tf_op jit(solution)/shard_map/base/pallas_call | solution.py:286
  299.4 7.4 %all-to-all-done = bf16[128,32,128]{2,1,0:T(8,128)(2,1)S(1)} async-done(((bf16[128,32,128]{2,1,0:T(8,128)(2,1)}), bf16[128,32,128]{2,1,0:T(8,128)(2,1)S(1)}, u32[]{:S(2)}, u32[]{:S(2)}) %all-to-all-start) | async-done | bytes 1048608 | tf_op jit(solution)/shard_map/all_to_all | solution.py:390
  307.8 4.8 %update.1 = f32[512,1024]{1,0:T(8,128)} custom-call(s32[512]{0:T(512)} %get-tuple-element.50.inverse, bf16[4096,128]{1,0:T(8,128)(2,1)} %bitcast.17, f32[512,1024]{1,0:T(8,128)} %get-tuple-element.91.base, f32[512,1024]{1,0:T(8,128)} %get-tuple-element.92.scale), custom_call_target="tpu_custom_call" | custom-call | bytes 7340032 | tf_op jit(solution)/shard_map/update/pallas_call | solution.py:313
  (201 shorter events, 83.1 us)
Async XLA Ops:
  0.0 134.9 %collective-permute-start.9 = (bf16[2048,1024]{1,0:T(8,128)(2,1)}, bf16[2048,1024]{1,0:T(8,128)(2,1)}, u32[]{:S(2)}, u32[]{:S(2)}) collective-permute-start(bf16[2048,1024]{1,0:T(8,128)(2,1)} %refs_4_.1), channel_id=1, source_target_pairs={{0,1},{1,0},{2,3},{3,2},{4,5},{5,4},{6,7},{7,6},{8,9},{9,8},{10,11... | collective-permute-start | bytes 12582920 | tf_op jit(solution)/shard_map/ppermute | solution.py:47
  21.0 28.7 %collective-permute-start.5 = (bf16[64,2048]{1,0:T(8,128)(2,1)}, bf16[64,2048]{1,0:T(8,128)(2,1)S(1)}, u32[]{:S(2)}, u32[]{:S(2)}) collective-permute-start(bf16[64,2048]{1,0:T(8,128)(2,1)} %get-tuple-element.55), channel_id=1, source_target_pairs={{0,4},{1,5},{2,28},{3,29},{4,2},{5,3},{6,26},{7,27},{8,0},{9,1},{1... | collective-permute-start | bytes 786440 | tf_op jit(solution)/shard_map/ppermute | solution.py:47
  22.9 28.7 %collective-permute-start.7 = (bf16[64,2048]{1,0:T(8,128)(2,1)}, bf16[64,2048]{1,0:T(8,128)(2,1)S(1)}, u32[]{:S(2)}, u32[]{:S(2)}) collective-permute-start(bf16[64,2048]{1,0:T(8,128)(2,1)} %get-tuple-element.56), channel_id=1, source_target_pairs={{0,6},{1,7},{2,30},{3,31},{4,4},{5,5},{6,28},{7,29},{8,2},{9,3},{1... | collective-permute-start | bytes 786440 | tf_op jit(solution)/shard_map/ppermute | solution.py:47
  28.7 25.6 %collective-permute-start.2 = (bf16[64,2048]{1,0:T(8,128)(2,1)S(1)}, bf16[64,2048]{1,0:T(8,128)(2,1)S(1)}, u32[]{:S(2)}, u32[]{:S(2)}) collective-permute-start(bf16[64,2048]{1,0:T(8,128)(2,1)S(1)} %collective-permute-done.1), channel_id=1, source_target_pairs={{0,0},{1,1},{2,98},{3,99},{4,68},{5,69},{6,38},{7,39},{8,8},{9,9},... | collective-permute-start | bytes 786440 | tf_op jit(solution)/shard_map/ppermute | solution.py:47
  29.7 24.5 %collective-permute-start.4 = (bf16[64,2048]{1,0:T(8,128)(2,1)S(1)}, bf16[64,2048]{1,0:T(8,128)(2,1)S(1)}, u32[]{:S(2)}, u32[]{:S(2)}) collective-permute-start(bf16[64,2048]{1,0:T(8,128)(2,1)S(1)} %collective-permute-done.3), channel_id=1, source_target_pairs={{0,32},{1,33},{2,2},{3,3},{4,100},{5,101},{6,70},{7,71},{8,40},{9,... | collective-permute-start | bytes 786440 | tf_op jit(solution)/shard_map/ppermute | solution.py:47
  63.1 24.1 %collective-permute-start.14 = (bf16[256,2048]{1,0:T(8,128)(2,1)}, bf16[256,2048]{1,0:T(8,128)(2,1)S(1)}, u32[]{:S(2)}, u32[]{:S(2)}) collective-permute-start(bf16[256,2048]{1,0:T(8,128)(2,1)} %join.1.refs_0_), channel_id=1, source_target_pairs={{0,8},{1,9},{2,10},{3,11},{4,12},{5,13},{6,14},{7,15},{8,0},{9,1},... | collective-permute-start | bytes 3145736 | tf_op jit(solution)/shard_map/ppermute | solution.py:47
  65.7 23.0 %collective-permute-start.15 = (bf16[256,2048]{1,0:T(8,128)(2,1)}, bf16[256,2048]{1,0:T(8,128)(2,1)S(1)}, u32[]{:S(2)}, u32[]{:S(2)}) collective-permute-start(bf16[256,2048]{1,0:T(8,128)(2,1)} %join.1.refs_0_), channel_id=1, source_target_pairs={{0,6},{1,7},{2,0},{3,1},{4,2},{5,3},{6,4},{7,5},{8,14},{9,15},{10,... | collective-permute-start | bytes 3145736 | tf_op jit(solution)/shard_map/ppermute | solution.py:47
  65.7 24.6 %collective-permute-start.16 = (bf16[256,2048]{1,0:T(8,128)(2,1)}, bf16[256,2048]{1,0:T(8,128)(2,1)S(1)}, u32[]{:S(2)}, u32[]{:S(2)}) collective-permute-start(bf16[256,2048]{1,0:T(8,128)(2,1)} %join.1.refs_0_), channel_id=1, source_target_pairs={{0,2},{1,3},{2,4},{3,5},{4,6},{5,7},{6,0},{7,1},{8,10},{9,11},{10,... | collective-permute-start | bytes 3145736 | tf_op jit(solution)/shard_map/ppermute | solution.py:47
  87.1 24.0 %collective-permute-start.21 = (bf16[256,2048]{1,0:T(8,128)(2,1)S(1)}, bf16[256,2048]{1,0:T(8,128)(2,1)S(1)}, u32[]{:S(2)}, u32[]{:S(2)}) collective-permute-start(bf16[256,2048]{1,0:T(8,128)(2,1)S(1)} %collective-permute-done.14.refs_0_), channel_id=1, source_target_pairs={{0,6},{1,7},{2,0},{3,1},{4,2},{5,3},{6,4},{7,5},{8,14},{9,15},{10,... | collective-permute-start | bytes 3145736 | tf_op jit(solution)/shard_map/ppermute | solution.py:47
  87.1 25.6 %collective-permute-start.22 = (bf16[256,2048]{1,0:T(8,128)(2,1)S(1)}, bf16[256,2048]{1,0:T(8,128)(2,1)S(1)}, u32[]{:S(2)}, u32[]{:S(2)}) collective-permute-start(bf16[256,2048]{1,0:T(8,128)(2,1)S(1)} %collective-permute-done.14.refs_0_), channel_id=1, source_target_pairs={{0,2},{1,3},{2,4},{3,5},{4,6},{5,7},{6,0},{7,1},{8,10},{9,11},{10,... | collective-permute-start | bytes 3145736 | tf_op jit(solution)/shard_map/ppermute | solution.py:47
  88.7 33.7 %collective-permute-start.30 = (bf16[128,2048]{1,0:T(8,128)(2,1)S(1)}, bf16[128,2048]{1,0:T(8,128)(2,1)}, u32[]{:S(2)}, u32[]{:S(2)}) collective-permute-start(bf16[128,2048]{1,0:T(8,128)(2,1)S(1)} %slice.56), channel_id=1, source_target_pairs={{0,6},{1,7},{2,0},{3,1},{4,2},{5,3},{6,4},{7,5},{8,14},{9,15},{10,... | collective-permute-start | bytes 1572872 | tf_op jit(solution)/shard_map/ppermute | solution.py:47
  90.4 33.3 %collective-permute-start.31 = (bf16[128,2048]{1,0:T(8,128)(2,1)S(1)}, bf16[128,2048]{1,0:T(8,128)(2,1)}, u32[]{:S(2)}, u32[]{:S(2)}) collective-permute-start(bf16[128,2048]{1,0:T(8,128)(2,1)S(1)} %slice.57), channel_id=1, source_target_pairs={{0,2},{1,3},{2,4},{3,5},{4,6},{5,7},{6,0},{7,1},{8,10},{9,11},{10,... | collective-permute-start | bytes 1572872 | tf_op jit(solution)/shard_map/ppermute | solution.py:47
  144.6 59.2 %collective-permute-start.35 = (bf16[128,2048]{1,0:T(8,128)(2,1)}, bf16[128,2048]{1,0:T(8,128)(2,1)S(1)}, u32[]{:S(2)}, u32[]{:S(2)}) collective-permute-start(bf16[128,2048]{1,0:T(8,128)(2,1)} %get-tuple-element.82), channel_id=1, source_target_pairs={{0,96},{1,97},{2,98},{3,99},{4,100},{5,101},{6,102},{7,103},{8,104... | collective-permute-start | bytes 1572872 | tf_op jit(solution)/shard_map/ppermute | solution.py:47
  157.3 26.8 %collective-permute-start.24 = (bf16[128,2048]{1,0:T(8,128)(2,1)}, bf16[128,2048]{1,0:T(8,128)(2,1)S(1)}, u32[]{:S(2)}, u32[]{:S(2)}) collective-permute-start(bf16[128,2048]{1,0:T(8,128)(2,1)} %get-tuple-element.72), channel_id=1, source_target_pairs={{0,96},{1,97},{2,98},{3,99},{4,100},{5,101},{6,102},{7,103},{8,104... | collective-permute-start | bytes 1572872 | tf_op jit(solution)/shard_map/ppermute | solution.py:47
  158.7 25.6 %collective-permute-start.23 = (bf16[128,2048]{1,0:T(8,128)(2,1)}, bf16[128,2048]{1,0:T(8,128)(2,1)S(1)}, u32[]{:S(2)}, u32[]{:S(2)}) collective-permute-start(bf16[128,2048]{1,0:T(8,128)(2,1)} %get-tuple-element.71), channel_id=1, source_target_pairs={{0,32},{1,33},{2,34},{3,35},{4,36},{5,37},{6,38},{7,39},{8,40},{9,... | collective-permute-start | bytes 1572872 | tf_op jit(solution)/shard_map/ppermute | solution.py:47
  184.1 27.6 %collective-permute-start.34 = (bf16[128,2048]{1,0:T(8,128)(2,1)S(1)}, bf16[128,2048]{1,0:T(8,128)(2,1)S(1)}, u32[]{:S(2)}, u32[]{:S(2)}) collective-permute-start(bf16[128,2048]{1,0:T(8,128)(2,1)S(1)} %copy-done.45), channel_id=1, source_target_pairs={{0,32},{1,33},{2,34},{3,35},{4,36},{5,37},{6,38},{7,39},{8,40},{9,... | collective-permute-start | bytes 1572872 | tf_op jit(solution)/shard_map/ppermute | solution.py:47
  197.3 31.2 %collective-permute-start.26 = (bf16[128,1024]{1,0:T(8,128)(2,1)S(1)}, bf16[128,1024]{1,0:T(8,128)(2,1)S(1)}, u32[]{:S(2)}, u32[]{:S(2)}) collective-permute-start(bf16[128,1024]{1,0:T(8,128)(2,1)S(1)} %add_convert_fusion.4), channel_id=1, source_target_pairs={{0,96},{1,97},{2,98},{3,99},{4,100},{5,101},{6,102},{7,103},{8,104... | collective-permute-start | bytes 786440 | tf_op jit(solution)/shard_map/ppermute | solution.py:47
  200.8 29.3 %collective-permute-start.25 = (bf16[128,1024]{1,0:T(8,128)(2,1)S(1)}, bf16[128,1024]{1,0:T(8,128)(2,1)S(1)}, u32[]{:S(2)}, u32[]{:S(2)}) collective-permute-start(bf16[128,1024]{1,0:T(8,128)(2,1)S(1)} %add_convert_fusion.5), channel_id=1, source_target_pairs={{0,32},{1,33},{2,34},{3,35},{4,36},{5,37},{6,38},{7,39},{8,40},{9,... | collective-permute-start | bytes 786440 | tf_op jit(solution)/shard_map/ppermute | solution.py:47
  201.0 29.0 %collective-permute-start.20 = (bf16[192,1024]{1,0:T(8,128)(2,1)S(1)}, bf16[192,1024]{1,0:T(8,128)(2,1)S(1)}, u32[]{:S(2)}, u32[]{:S(2)}) collective-permute-start(bf16[192,1024]{1,0:T(8,128)(2,1)S(1)} %add_convert_fusion), channel_id=1, source_target_pairs={{0,96},{1,97},{2,98},{3,99},{4,100},{5,101},{6,102},{7,103},{8,104... | collective-permute-start | bytes 1179656 | tf_op jit(solution)/shard_map/ppermute | solution.py:47
  203.7 26.3 %collective-permute-start.19 = (bf16[192,1024]{1,0:T(8,128)(2,1)S(1)}, bf16[192,1024]{1,0:T(8,128)(2,1)S(1)}, u32[]{:S(2)}, u32[]{:S(2)}) collective-permute-start(bf16[192,1024]{1,0:T(8,128)(2,1)S(1)} %add_convert_fusion.1), channel_id=1, source_target_pairs={{0,32},{1,33},{2,34},{3,35},{4,36},{5,37},{6,38},{7,39},{8,40},{9,... | collective-permute-start | bytes 1179656 | tf_op jit(solution)/shard_map/ppermute | solution.py:47
  236.4 40.6 %collective-permute-start.28 = (f32[192,1024]{1,0:T(8,128)}, f32[192,1024]{1,0:T(8,128)S(1)}, u32[]{:S(2)}, u32[]{:S(2)}) collective-permute-start(f32[192,1024]{1,0:T(8,128)} %get-tuple-element.77), channel_id=1, source_target_pairs={{0,1},{1,0},{2,3},{3,2},{4,5},{5,4},{6,7},{7,6},{8,9},{9,8},{10,11... | collective-permute-start | bytes 2359304 | tf_op jit(solution)/shard_map/ppermute | solution.py:47
  253.3 23.7 %collective-permute-start.27 = (bf16[192,1024]{1,0:T(8,128)(2,1)S(1)}, bf16[192,1024]{1,0:T(8,128)(2,1)S(1)}, u32[]{:S(2)}, u32[]{:S(2)}) collective-permute-start(bf16[192,1024]{1,0:T(8,128)(2,1)S(1)} %copy-done.47), channel_id=1, source_target_pairs={{0,16},{1,17},{2,18},{3,19},{4,20},{5,21},{6,22},{7,23},{8,24},{9,... | collective-permute-start | bytes 1179656 | tf_op jit(solution)/shard_map/ppermute | solution.py:47
  253.4 23.7 %collective-permute-start.29 = (bf16[192,1024]{1,0:T(8,128)(2,1)S(1)}, bf16[192,1024]{1,0:T(8,128)(2,1)S(1)}, u32[]{:S(2)}, u32[]{:S(2)}) collective-permute-start(bf16[192,1024]{1,0:T(8,128)(2,1)S(1)} %copy-done.46), channel_id=1, source_target_pairs={{0,17},{1,16},{2,19},{3,18},{4,21},{5,20},{6,23},{7,22},{8,25},{9,... | collective-permute-start | bytes 1179656 | tf_op jit(solution)/shard_map/ppermute | solution.py:47
  283.9 22.9 %all-to-all-start = ((bf16[128,32,128]{2,1,0:T(8,128)(2,1)}), bf16[128,32,128]{2,1,0:T(8,128)(2,1)S(1)}, u32[]{:S(2)}, u32[]{:S(2)}) async-start(bf16[128,32,128]{2,1,0:T(8,128)(2,1)} %get-tuple-element.89), calls=%async_computation | async-start | bytes 2097152 | tf_op jit(solution)/shard_map/all_to_all | solution.py:390
  (67 other events, 791.2 us)

commit v2 on v1

--- a/solution.py
+++ b/solution.py
@@ -51,7 +51,7 @@
 SMEM = pl.BlockSpec(memory_space=pltpu.SMEM)
 
 
-def params(megabytes=56):
+def params(megabytes):
     return pltpu.CompilerParams(vmem_limit_bytes=megabytes << 20)
 
 
@@ -72,7 +72,7 @@
         out_shape=[jax.ShapeDtypeStruct((256, 1024), BF)] * 2,
         in_specs=[SMEM, VMEM],
         out_specs=[VMEM] * 2,
-        compiler_params=params(),
+        compiler_params=params(8),
         cost_estimate=cost(0, 3 << 20),
         name="split",
     )(where, amp)
@@ -92,7 +92,7 @@
         out_shape=[jax.ShapeDtypeStruct((64, 2048), BF)] * 4,
         in_specs=[SMEM] + [VMEM] * 2,
         out_specs=[VMEM] * 4,
-        compiler_params=params(),
+        compiler_params=params(6),
         cost_estimate=cost(0, 2 << 20),
         name="weave",
     )(where, keep, got)
@@ -110,7 +110,7 @@
         out_shape=jax.ShapeDtypeStruct((256, 2048), BF),
         in_specs=[SMEM] + [VMEM] * 4,
         out_specs=VMEM,
-        compiler_params=params(),
+        compiler_params=params(6),
         cost_estimate=cost(0, 2 << 20),
         name="join",
     )(where, *pieces)
@@ -176,7 +176,7 @@
         out_specs=[out(first), out(second), out(first), out(second)]
         + [out(lambda s: (0, s))] * 2,
         scratch_shapes=[pltpu.VMEM((n * 256, 2048), BF)],
-        compiler_params=params(),
+        compiler_params=params(24),
         cost_estimate=cost(2 * n * 256 * 2048 * 2048, (9 << 20) + n * (3 << 20)),
         name="product",
     )(*flat, own, oth)
@@ -221,10 +221,52 @@
         + [jax.ShapeDtypeStruct((rows, 1024), BF)] * 2,
         in_specs=[SMEM] + [VMEM] * len(flat),
         out_specs=[VMEM] * 4,
-        compiler_params=params(),
+        compiler_params=params(20),
         cost_estimate=cost(0, rows * 1024 * 24),
         name="collect",
     )(low, *flat)
+
+
+def index_kernel(place, slots, mask, inverse, code, row_of, count):
+    x = place[0]
+    c = place[1]
+
+    def clear(s, carry):
+        count[s] = 0
+        return carry
+
+    lax.fori_loop(0, 128, clear, 0, unroll=8)
+
+    def row(r, carry):
+        i = lax.bitwise_and(lax.shift_right_logical(r, 4) - x + 4, 3)
+        other = lax.bitwise_xor(lax.bitwise_and(lax.shift_right_logical(r, 3), 1), c)
+        part = other * 4 + lax.bitwise_xor(i, lax.shift_right_logical(i, 1))
+        at = part * 8 + lax.bitwise_and(r, 7)
+        row_of[r] = at * 8
+        for k in range(8):
+            t = r * 8 + k
+            s = slots[t]
+            n = count[s]
+            count[s] = n + 1
+            q = s * 4 + n
+            inverse[t] = q
+            code[q] = at * 16 + k * 2 + mask[t]
+        return carry
+
+    lax.fori_loop(0, 64, row, 0)
+
+
+def index(place, slots, mask):
+    return pl.pallas_call(
+        index_kernel,
+        out_shape=[jax.ShapeDtypeStruct((n,), jnp.int32) for n in (512, 512, 64)],
+        in_specs=[SMEM] * 3,
+        out_specs=[SMEM] * 3,
+        scratch_shapes=[pltpu.SMEM((128,), jnp.int32)],
+        compiler_params=params(1),
+        cost_estimate=cost(0, 8 << 10),
+        name="index",
+    )(place, slots, mask)
 
 
 def outgoing_kernel(code, *refs):
@@ -260,7 +302,7 @@
         ],
         in_specs=[SMEM] + [VMEM] * 8,
         out_specs=[VMEM] * 2,
-        compiler_params=params(),
+        compiler_params=params(12),
         cost_estimate=cost(0, 6 << 20),
         name="outgoing",
     )(code, *parts)
@@ -288,7 +330,7 @@
         out_shape=[jax.ShapeDtypeStruct((512, 1024), F32)] * 2,
         in_specs=[SMEM] * 2 + [VMEM] * 4,
         out_specs=[VMEM] * 2,
-        compiler_params=params(),
+        compiler_params=params(14),
         cost_estimate=cost(0, 8 << 20),
         name="base",
     )(row_of, mask, full, amp, occ, vir)
@@ -316,7 +358,7 @@
         in_specs=[SMEM] + [VMEM] * 3,
         out_specs=VMEM,
         scratch_shapes=[pltpu.VMEM((4096, 128), F32)],
-        compiler_params=params(),
+        compiler_params=params(12),
         cost_estimate=cost(0, 7 << 20),
         name="update",
     )(inverse, incoming, base, scale)
@@ -375,17 +417,8 @@
         stay_b = send(stay_b, shift(dc=1))
         last += [stay_a, got_a, stay_b, got_b]
 
-    slots = partner_slot.reshape(-1)
     mask = tile_mask.reshape(-1)
-    order = jnp.argsort(slots, stable=True).astype(jnp.int32)
-    inverse = jnp.argsort(order, stable=True).astype(jnp.int32)
-    tile_row = jnp.arange(64, dtype=jnp.int32)
-    part = ((tile_row >> 4) - x) & 3
-    part = (((tile_row >> 3) & 1) ^ c) * 4 + (part ^ (part >> 1))
-    row_of = part * 64 + (tile_row & 7) * 8
-    tile = jnp.arange(512, dtype=jnp.int32)
-    code = ((jnp.repeat(row_of, 8) >> 3) << 4) + ((tile & 7) << 1) + mask
-    code = jnp.take(code, order)
+    inverse, code, row_of = index(jnp.stack([x, c]), partner_slot.reshape(-1), mask)
     full, out = outgoing(code, *last)
     incoming = lax.all_to_all(out, AXES, split_axis=0, concat_axis=0, tiled=True)
     base, scale = make_base(

time: 313 us -> 309 us (0.987)
  Pallas kernels: 71.5 us -> 49.8 us
  local copies, waits for them, and re-layouts: 13.2 us -> 34.1 us
  starting transfers between devices: 69.6 us -> 81.5 us
  waiting for transfers between devices: 148 us -> 138 us
  other arithmetic: 9.85 us -> 3.78 us
    unnamed x100 -> x98, local copies, waits for them, and re-layouts: 7.75 us -> 33.5 us
    ppermute x41, waiting for transfers between devices: 140 us -> 126 us  [send(): return lax.ppermute(value, AXES, pairs)]
    ppermute x41, starting transfers between devices: 65.8 us -> 74.5 us  [send(): return lax.ppermute(value, AXES, pairs)]
    sort x2 -> x0, other arithmetic: 7.55 us -> none  [the longest x1 3.78 us: compute(): inverse = jnp.argsort(order, stable=True).astype(jnp.int32)]
    pallas_call x4, Pallas kernels: 38.8 us -> 31.3 us  [product(): pl.pallas_call(functools.partial(product_kernel, counts), out_shape=[half...]
    pallas_call x0 -> x1, Pallas kernels: none -> 4.28 us  [index(): pl.pallas_call(index_kernel, out_shape=[jax.ShapeDtypeStruct((n,), jnp.in...]
    pallas_call x2, Pallas kernels: 8.08 us -> 4.06 us  [collect(): pl.pallas_call(functools.partial(settle_kernel, len(groups), members), ou...]
    all_to_all x1, waiting for transfers between devices: 7.43 us -> 11.2 us  [compute(): lax.all_to_all(out, AXES, split_axis=0, concat_axis=0, tiled=True)]
  transfers between devices with their start and end apart: 42 -> 42, of which waited for: 17 -> 16; matrix products, arithmetic and copies ran while one was open for 5% -> 1% of each run, Pallas kernels for 16% -> 14%
where the time goes in v2:
time: 309 us; the launch traced here: 307 us
  waiting for transfers between devices  138 us (45%)
  starting transfers between devices  81.5 us (26%)
  Pallas kernels  49.8 us (16%)
  local copies, waits for them, and re-layouts  34.1 us (11%)
  other arithmetic  3.78 us (1%)
    ppermute x41, waiting for transfers between devices, send(): return lax.ppermute(value, AXES, pairs)  126 us
    ppermute x41, starting transfers between devices, send(): return lax.ppermute(value, AXES, pairs)  74.5 us
    unnamed x98, local copies, waits for them, and re-layouts  33.5 us
    pallas_call x4, Pallas kernels, product(): pl.pallas_call(functools.partial(product_kernel, counts), out_shape=[half...  31.3 us
    all_to_all x1, waiting for transfers between devices, compute(): lax.all_to_all(out, AXES, split_axis=0, concat_axis=0, tiled=True)  11.2 us
    all_to_all x1, starting transfers between devices, compute(): lax.all_to_all(out, AXES, split_axis=0, concat_axis=0, tiled=True)  7.03 us
  transfers between devices with their start and end apart: 42, of which 16 were waited for; matrix products, arithmetic and copies ran while one was open for 1% of the time, Pallas kernels for 14%

profile of v2, /device:TPU:1, one launch (start us, length us, event | category | flops | bytes accessed | tf_op | source)
XLA Modules:
  0.0 307.3 jit_solution(2428076071799769801)
XLA Ops:
  3.8 5.3 %collective-permute-done.got = bf16[256,1024]{1,0:T(8,128)(2,1)S(1)} collective-permute-done((bf16[256,1024]{1,0:T(8,128)(2,1)S(1)}, bf16[256,1024]{1,0:T(8,128)(2,1)S(1)}, u32[]{:S(2)}, u32[]{:S(2)}) %collective-permute-start) | collective-permute-done | bytes 524320 | tf_op jit(solution)/shard_map/ppermute | solution.py:47
  9.9 8.2 %collective-permute-start.3 = (bf16[64,2048]{1,0:T(8,128)(2,1)S(1)}, bf16[64,2048]{1,0:T(8,128)(2,1)S(1)}, u32[]{:S(2)}, u32[]{:S(2)}) collective-permute-start(bf16[64,2048]{1,0:T(8,128)(2,1)S(1)} %get-tuple-element.55), channel_id=1, source_target_pairs={{0,2},{1,3},{2,26},{3,27},{4,0},{5,1},{6,24},{7,25},{8,6},{9,7},{1... | collective-permute-start | bytes 786440 | tf_op jit(solution)/shard_map/ppermute | solution.py:47
  20.0 5.7 %collective-permute-start.7 = (bf16[64,2048]{1,0:T(8,128)(2,1)S(1)}, bf16[64,2048]{1,0:T(8,128)(2,1)S(1)}, u32[]{:S(2)}, u32[]{:S(2)}) collective-permute-start(bf16[64,2048]{1,0:T(8,128)(2,1)S(1)} %get-tuple-element.57), channel_id=1, source_target_pairs={{0,6},{1,7},{2,30},{3,31},{4,4},{5,5},{6,28},{7,29},{8,2},{9,3},{1... | collective-permute-start | bytes 786440 | tf_op jit(solution)/shard_map/ppermute | solution.py:47
  28.6 18.0 %collective-permute-done.5 = bf16[64,2048]{1,0:T(8,128)(2,1)S(1)} collective-permute-done((bf16[64,2048]{1,0:T(8,128)(2,1)S(1)}, bf16[64,2048]{1,0:T(8,128)(2,1)S(1)}, u32[]{:S(2)}, u32[]{:S(2)}) %collective-permute-start.5) | collective-permute-done | bytes 262176 | tf_op jit(solution)/shard_map/ppermute | solution.py:47
  50.5 5.8 %collective-permute-done.6.refs_2_ = bf16[64,2048]{1,0:T(8,128)(2,1)S(1)} collective-permute-done((bf16[64,2048]{1,0:T(8,128)(2,1)S(1)}, bf16[64,2048]{1,0:T(8,128)(2,1)S(1)}, u32[]{:S(2)}, u32[]{:S(2)}) %collective-permute-start.6) | collective-permute-done | bytes 262176 | tf_op jit(solution)/shard_map/ppermute | solution.py:47
  61.8 19.5 %collective-permute-done.14.refs_0_ = bf16[256,2048]{1,0:T(8,128)(2,1)S(1)} collective-permute-done((bf16[256,2048]{1,0:T(8,128)(2,1)S(1)}, bf16[256,2048]{1,0:T(8,128)(2,1)S(1)}, u32[]{:S(2)}, u32[]{:S(2)}) %collective-permute-start.14) | collective-permute-done | bytes 1048608 | tf_op jit(solution)/shard_map/ppermute | solution.py:47
  84.8 20.9 %collective-permute-done.21.refs_0_ = bf16[256,2048]{1,0:T(8,128)(2,1)S(1)} collective-permute-done((bf16[256,2048]{1,0:T(8,128)(2,1)S(1)}, bf16[256,2048]{1,0:T(8,128)(2,1)S(1)}, u32[]{:S(2)}, u32[]{:S(2)}) %collective-permute-start.21) | collective-permute-done | bytes 1048608 | tf_op jit(solution)/shard_map/ppermute | solution.py:47
  107.5 7.6 %product.6 = (f32[128,1024]{1,0:T(8,128)S(1)}, f32[128,1024]{1,0:T(8,128)S(1)}, f32[128,1024]{1,0:T(8,128)S(1)}, f32[128,1024]{1,0:T(8,128)S(1)}, bf16[128,2048]...) custom-call(bf16[256,2048]{1,0:T(8,128)(2,1)S(1)} %collective-permute-done.21.refs_0_, ...), custom_call_target="tpu_custom_call" | custom-call | flops 4294967296 | bytes 15728640 | tf_op jit(solution)/shard_map/product/pallas_call | solution.py:170
  119.6 5.8 %product.4 = (f32[64,1024]{1,0:T(8,128)S(1)}, f32[64,1024]{1,0:T(8,128)S(1)}, f32[64,1024]{1,0:T(8,128)S(1)}, f32[64,1024]{1,0:T(8,128)S(1)}, bf16[64,2048]{1,0:...) custom-call(bf16[256,2048]{1,0:T(8,128)(2,1)S(1)} %join.1.refs_0_, bf16[2048,1024]{1,0:T(8,128)(2,1)S(1)} %copy-done.2, ...), custom_call_target="tpu_custom_call" | custom-call | flops 2147483648 | bytes 12582912 | tf_op jit(solution)/shard_map/product/pallas_call | solution.py:170
  126.7 9.6 %product.5 = (f32[192,1024]{1,0:T(8,128)S(1)}, f32[192,1024]{1,0:T(8,128)S(1)}, f32[192,1024]{1,0:T(8,128)S(1)}, f32[192,1024]{1,0:T(8,128)S(1)}, bf16[192,2048]...) custom-call(bf16[256,2048]{1,0:T(8,128)(2,1)S(1)} %collective-permute-done.14.refs_0_, ...), custom_call_target="tpu_custom_call" | custom-call | flops 6442450944 | bytes 18874368 | tf_op jit(solution)/shard_map/product/pallas_call | solution.py:170
  139.6 3.0 collective-permute-start.11
  142.6 8.3 %product.7 = (f32[128,1024]{1,0:T(8,128)S(1)}, f32[128,1024]{1,0:T(8,128)S(1)}, f32[128,1024]{1,0:T(8,128)S(1)}, f32[128,1024]{1,0:T(8,128)S(1)}, bf16[128,2048]{1,0:T(8,128)(2,1)}, /*index=5*/bf16[128,2048]{1,0:T(8,128)(2,1)}) custom-call(bf16[128,2048]{1,0:T(8,128)(2,1)S(1)} %collective-permute-done.30.refs_0_, ...), custom_call_target="tpu_custom_call" | custom-call | flops 4294967296 | bytes 15728640 | tf_op jit(solution)/shard_map/product/pallas_call | solution.py:170
  153.6 5.6 %collective-permute-done.11.refs_3_ = bf16[64,2048]{1,0:T(8,128)(2,1)S(1)} collective-permute-done((bf16[64,2048]{1,0:T(8,128)(2,1)S(1)}, bf16[64,2048]{1,0:T(8,128)(2,1)S(1)}, u32[]{:S(2)}, u32[]{:S(2)}) %collective-permute-start.11) | collective-permute-done | bytes 262176 | tf_op jit(solution)/shard_map/ppermute | solution.py:47
  165.1 6.3 %collective-permute-done.17.refs_8_ = bf16[192,2048]{1,0:T(8,128)(2,1)S(1)} collective-permute-done((bf16[192,2048]{1,0:T(8,128)(2,1)S(1)}, bf16[192,2048]{1,0:T(8,128)(2,1)S(1)}, u32[]{:S(2)}, u32[]{:S(2)}) %collective-permute-start.17) | collective-permute-done | bytes 786464 | tf_op jit(solution)/shard_map/ppermute | solution.py:47
  175.2 8.2 %collective-permute-done.12.refs_4_ = bf16[64,1024]{1,0:T(8,128)(2,1)S(1)} collective-permute-done((bf16[64,1024]{1,0:T(8,128)(2,1)S(1)}, bf16[64,1024]{1,0:T(8,128)(2,1)S(1)}, u32[]{:S(2)}, u32[]{:S(2)}) %collective-permute-start.12) | collective-permute-done | bytes 131104 | tf_op jit(solution)/shard_map/ppermute | solution.py:47
  187.8 21.0 %collective-permute-done.25.refs_16_ = bf16[128,1024]{1,0:T(8,128)(2,1)} collective-permute-done((bf16[128,1024]{1,0:T(8,128)(2,1)}, bf16[128,1024]{1,0:T(8,128)(2,1)}, u32[]{:S(2)}, u32[]{:S(2)}) %collective-permute-start.25) | collective-permute-done | bytes 262176 | tf_op jit(solution)/shard_map/ppermute | solution.py:47
  221.6 11.1 %collective-permute-start.28 = (f32[192,1024]{1,0:T(8,128)}, f32[192,1024]{1,0:T(8,128)S(1)}, u32[]{:S(2)}, u32[]{:S(2)}) collective-permute-start(f32[192,1024]{1,0:T(8,128)} %get-tuple-element.78), channel_id=1, source_target_pairs={{0,1},{1,0},{2,3},{3,2},{4,5},{5,4},{6,7},{7,6},{8,9},{9,8},{10,11... | collective-permute-start | bytes 2359304 | tf_op jit(solution)/shard_map/ppermute | solution.py:47
  237.7 3.1 %collective-permute-done.37.refs_5_ = bf16[128,1024]{1,0:T(8,128)(2,1)S(1)} collective-permute-done((bf16[128,1024]{1,0:T(8,128)(2,1)S(1)}, bf16[128,1024]{1,0:T(8,128)(2,1)S(1)}, u32[]{:S(2)}, u32[]{:S(2)}) %collective-permute-start.37) | collective-permute-done | bytes 262176 | tf_op jit(solution)/shard_map/ppermute | solution.py:47
  240.7 3.0 collective-permute-done.36.refs_4_
  248.4 8.6 %collective-permute-done.38.refs_5_ = bf16[64,1024]{1,0:T(8,128)(2,1)S(1)} collective-permute-done((bf16[64,1024]{1,0:T(8,128)(2,1)S(1)}, bf16[64,1024]{1,0:T(8,128)(2,1)S(1)}, u32[]{:S(2)}, u32[]{:S(2)}) %collective-permute-start.38) | collective-permute-done | bytes 131104 | tf_op jit(solution)/shard_map/ppermute | solution.py:47
  260.0 4.3 %index.1 = (s32[512]{0:T(512)S(1)}, s32[512]{0:T(512)S(1)}, s32[64]{0:T(128)S(1)}) custom-call(s32[2]{0:T(128)S(1)} %pad_add_fusion.place, s32[512]{0:T(512)S(1)} %reshape.9.slots, s32[512]{0:T(512)S(1)} %reshape.10.mask), custom_call_target="tpu_custom_call" | custom-call | bytes 8192 | tf_op jit(solution)/shard_map/index/pallas_call | solution.py:260
  275.2 7.0 %all-to-all-start = ((bf16[128,32,128]{2,1,0:T(8,128)(2,1)}), bf16[128,32,128]{2,1,0:T(8,128)(2,1)S(1)}, u32[]{:S(2)}, u32[]{:S(2)}) async-start(bf16[128,32,128]{2,1,0:T(8,128)(2,1)} %copy-done.9), calls=%async_computation | async-start | bytes 2097152 | tf_op jit(solution)/shard_map/all_to_all | solution.py:423
  284.0 3.3 %base.1 = (f32[512,1024]{1,0:T(8,128)S(1)}, f32[512,1024]{1,0:T(8,128)S(1)}) custom-call(s32[64]{0:T(128)S(1)} %get-tuple-element.91.row_of, s32[512]{0:T(512)S(1)} %reshape.10.mask, f32[512,1024]{1,0:T(8,128)S(1)} %copy-done.4, f32[512,1024]{1,0:T(8,128)S(1)} %copy-done.1, f32[512,1]{1,0:T(8,128)S(1)} %copy.9.occ, f32[1,1024]{1,0:T(1,128)S(1)} %bitcast.19), custom_call_target="tpu_custom_call" | custom-call | bytes 8388608 | tf_op jit(solution)/shard_map/base/pallas_call | solution.py:328
  290.0 11.2 %all-to-all-done = bf16[128,32,128]{2,1,0:T(8,128)(2,1)S(1)} async-done(((bf16[128,32,128]{2,1,0:T(8,128)(2,1)}), bf16[128,32,128]{2,1,0:T(8,128)(2,1)S(1)}, u32[]{:S(2)}, u32[]{:S(2)}) %all-to-all-start) | async-done | bytes 1048608 | tf_op jit(solution)/shard_map/all_to_all | solution.py:423
  (189 shorter events, 96.3 us)
Async XLA Ops:
  0.0 107.5 %collective-permute-start.9 = (bf16[2048,1024]{1,0:T(8,128)(2,1)}, bf16[2048,1024]{1,0:T(8,128)(2,1)}, u32[]{:S(2)}, u32[]{:S(2)}) collective-permute-start(bf16[2048,1024]{1,0:T(8,128)(2,1)} %refs_4_.1), channel_id=1, source_target_pairs={{0,1},{1,0},{2,3},{3,2},{4,5},{5,4},{6,7},{7,6},{8,9},{9,8},{10,11... | collective-permute-start | bytes 12582920 | tf_op jit(solution)/shard_map/ppermute | solution.py:47
  18.1 28.5 %collective-permute-start.5 = (bf16[64,2048]{1,0:T(8,128)(2,1)S(1)}, bf16[64,2048]{1,0:T(8,128)(2,1)S(1)}, u32[]{:S(2)}, u32[]{:S(2)}) collective-permute-start(bf16[64,2048]{1,0:T(8,128)(2,1)S(1)} %get-tuple-element.56), channel_id=1, source_target_pairs={{0,4},{1,5},{2,28},{3,29},{4,2},{5,3},{6,26},{7,27},{8,0},{9,1},{1... | collective-permute-start | bytes 786440 | tf_op jit(solution)/shard_map/ppermute | solution.py:47
  20.0 28.5 %collective-permute-start.7 = (bf16[64,2048]{1,0:T(8,128)(2,1)S(1)}, bf16[64,2048]{1,0:T(8,128)(2,1)S(1)}, u32[]{:S(2)}, u32[]{:S(2)}) collective-permute-start(bf16[64,2048]{1,0:T(8,128)(2,1)S(1)} %get-tuple-element.57), channel_id=1, source_target_pairs={{0,6},{1,7},{2,30},{3,31},{4,4},{5,5},{6,28},{7,29},{8,2},{9,3},{1... | collective-permute-start | bytes 786440 | tf_op jit(solution)/shard_map/ppermute | solution.py:47
  25.7 24.8 %collective-permute-start.2 = (bf16[64,2048]{1,0:T(8,128)(2,1)S(1)}, bf16[64,2048]{1,0:T(8,128)(2,1)S(1)}, u32[]{:S(2)}, u32[]{:S(2)}) collective-permute-start(bf16[64,2048]{1,0:T(8,128)(2,1)S(1)} %collective-permute-done.1), channel_id=1, source_target_pairs={{0,0},{1,1},{2,98},{3,99},{4,68},{5,69},{6,38},{7,39},{8,8},{9,9},... | collective-permute-start | bytes 786440 | tf_op jit(solution)/shard_map/ppermute | solution.py:47
  26.6 24.0 %collective-permute-start.4 = (bf16[64,2048]{1,0:T(8,128)(2,1)S(1)}, bf16[64,2048]{1,0:T(8,128)(2,1)S(1)}, u32[]{:S(2)}, u32[]{:S(2)}) collective-permute-start(bf16[64,2048]{1,0:T(8,128)(2,1)S(1)} %collective-permute-done.3), channel_id=1, source_target_pairs={{0,32},{1,33},{2,2},{3,3},{4,100},{5,101},{6,70},{7,71},{8,40},{9,... | collective-permute-start | bytes 786440 | tf_op jit(solution)/shard_map/ppermute | solution.py:47
  57.4 23.9 %collective-permute-start.14 = (bf16[256,2048]{1,0:T(8,128)(2,1)S(1)}, bf16[256,2048]{1,0:T(8,128)(2,1)S(1)}, u32[]{:S(2)}, u32[]{:S(2)}) collective-permute-start(bf16[256,2048]{1,0:T(8,128)(2,1)S(1)} %join.1.refs_0_), channel_id=1, source_target_pairs={{0,8},{1,9},{2,10},{3,11},{4,12},{5,13},{6,14},{7,15},{8,0},{9,1},... | collective-permute-start | bytes 3145736 | tf_op jit(solution)/shard_map/ppermute | solution.py:47
  60.3 22.8 %collective-permute-start.15 = (bf16[256,2048]{1,0:T(8,128)(2,1)S(1)}, bf16[256,2048]{1,0:T(8,128)(2,1)S(1)}, u32[]{:S(2)}, u32[]{:S(2)}) collective-permute-start(bf16[256,2048]{1,0:T(8,128)(2,1)S(1)} %join.1.refs_0_), channel_id=1, source_target_pairs={{0,6},{1,7},{2,0},{3,1},{4,2},{5,3},{6,4},{7,5},{8,14},{9,15},{10,... | collective-permute-start | bytes 3145736 | tf_op jit(solution)/shard_map/ppermute | solution.py:47
  60.3 24.4 %collective-permute-start.16 = (bf16[256,2048]{1,0:T(8,128)(2,1)S(1)}, bf16[256,2048]{1,0:T(8,128)(2,1)S(1)}, u32[]{:S(2)}, u32[]{:S(2)}) collective-permute-start(bf16[256,2048]{1,0:T(8,128)(2,1)S(1)} %join.1.refs_0_), channel_id=1, source_target_pairs={{0,2},{1,3},{2,4},{3,5},{4,6},{5,7},{6,0},{7,1},{8,10},{9,11},{10,... | collective-permute-start | bytes 3145736 | tf_op jit(solution)/shard_map/ppermute | solution.py:47
  81.3 24.5 %collective-permute-start.21 = (bf16[256,2048]{1,0:T(8,128)(2,1)S(1)}, bf16[256,2048]{1,0:T(8,128)(2,1)S(1)}, u32[]{:S(2)}, u32[]{:S(2)}) collective-permute-start(bf16[256,2048]{1,0:T(8,128)(2,1)S(1)} %collective-permute-done.14.refs_0_), channel_id=1, source_target_pairs={{0,6},{1,7},{2,0},{3,1},{4,2},{5,3},{6,4},{7,5},{8,14},{9,15},{10,... | collective-permute-start | bytes 3145736 | tf_op jit(solution)/shard_map/ppermute | solution.py:47
  81.3 26.1 %collective-permute-start.22 = (bf16[256,2048]{1,0:T(8,128)(2,1)S(1)}, bf16[256,2048]{1,0:T(8,128)(2,1)S(1)}, u32[]{:S(2)}, u32[]{:S(2)}) collective-permute-start(bf16[256,2048]{1,0:T(8,128)(2,1)S(1)} %collective-permute-done.14.refs_0_), channel_id=1, source_target_pairs={{0,2},{1,3},{2,4},{3,5},{4,6},{5,7},{6,0},{7,1},{8,10},{9,11},{10,... | collective-permute-start | bytes 3145736 | tf_op jit(solution)/shard_map/ppermute | solution.py:47
  83.1 55.0 %collective-permute-start.30 = (bf16[128,2048]{1,0:T(8,128)(2,1)S(1)}, bf16[128,2048]{1,0:T(8,128)(2,1)S(1)}, u32[]{:S(2)}, u32[]{:S(2)}) collective-permute-start(bf16[128,2048]{1,0:T(8,128)(2,1)S(1)} %slice.54), channel_id=1, source_target_pairs={{0,6},{1,7},{2,0},{3,1},{4,2},{5,3},{6,4},{7,5},{8,14},{9,15},{10,... | collective-permute-start | bytes 1572872 | tf_op jit(solution)/shard_map/ppermute | solution.py:47
  84.8 54.9 %collective-permute-start.31 = (bf16[128,2048]{1,0:T(8,128)(2,1)S(1)}, bf16[128,2048]{1,0:T(8,128)(2,1)S(1)}, u32[]{:S(2)}, u32[]{:S(2)}) collective-permute-start(bf16[128,2048]{1,0:T(8,128)(2,1)S(1)} %slice.55), channel_id=1, source_target_pairs={{0,2},{1,3},{2,4},{3,5},{4,6},{5,7},{6,0},{7,1},{8,10},{9,11},{10,... | collective-permute-start | bytes 1572872 | tf_op jit(solution)/shard_map/ppermute | solution.py:47
  105.8 36.8 %collective-permute-start.32 = (bf16[128,2048]{1,0:T(8,128)(2,1)S(1)}, bf16[128,2048]{1,0:T(8,128)(2,1)S(1)}, u32[]{:S(2)}, u32[]{:S(2)}) collective-permute-start(bf16[128,2048]{1,0:T(8,128)(2,1)S(1)} %slice.56), channel_id=1, source_target_pairs={{0,6},{1,7},{2,0},{3,1},{4,2},{5,3},{6,4},{7,5},{8,14},{9,15},{10,... | collective-permute-start | bytes 1572872 | tf_op jit(solution)/shard_map/ppermute | solution.py:47
  107.4 35.2 %collective-permute-start.33 = (bf16[128,2048]{1,0:T(8,128)(2,1)S(1)}, bf16[128,2048]{1,0:T(8,128)(2,1)S(1)}, u32[]{:S(2)}, u32[]{:S(2)}) collective-permute-start(bf16[128,2048]{1,0:T(8,128)(2,1)S(1)} %slice.57), channel_id=1, source_target_pairs={{0,2},{1,3},{2,4},{3,5},{4,6},{5,7},{6,0},{7,1},{8,10},{9,11},{10,... | collective-permute-start | bytes 1572872 | tf_op jit(solution)/shard_map/ppermute | solution.py:47
  116.7 45.8 %collective-permute-start.24 = (bf16[128,2048]{1,0:T(8,128)(2,1)S(1)}, bf16[128,2048]{1,0:T(8,128)(2,1)S(1)}, u32[]{:S(2)}, u32[]{:S(2)}) collective-permute-start(bf16[128,2048]{1,0:T(8,128)(2,1)S(1)} %get-tuple-element.73), channel_id=1, source_target_pairs={{0,96},{1,97},{2,98},{3,99},{4,100},{5,101},{6,102},{7,103},{8,104... | collective-permute-start | bytes 1572872 | tf_op jit(solution)/shard_map/ppermute | solution.py:47
  138.2 26.0 %collective-permute-start.18 = (bf16[192,2048]{1,0:T(8,128)(2,1)S(1)}, bf16[192,2048]{1,0:T(8,128)(2,1)S(1)}, u32[]{:S(2)}, u32[]{:S(2)}) collective-permute-start(bf16[192,2048]{1,0:T(8,128)(2,1)S(1)} %get-tuple-element.67), channel_id=1, source_target_pairs={{0,96},{1,97},{2,98},{3,99},{4,100},{5,101},{6,102},{7,103},{8,104... | collective-permute-start | bytes 2359304 | tf_op jit(solution)/shard_map/ppermute | solution.py:47
  150.9 81.8 %collective-permute-start.35 = (bf16[128,2048]{1,0:T(8,128)(2,1)}, bf16[128,2048]{1,0:T(8,128)(2,1)S(1)}, u32[]{:S(2)}, u32[]{:S(2)}) collective-permute-start(bf16[128,2048]{1,0:T(8,128)(2,1)} %get-tuple-element.83), channel_id=1, source_target_pairs={{0,96},{1,97},{2,98},{3,99},{4,100},{5,101},{6,102},{7,103},{8,104... | collective-permute-start | bytes 1572872 | tf_op jit(solution)/shard_map/ppermute | solution.py:47
  173.5 60.4 %collective-permute-start.34 = (bf16[128,2048]{1,0:T(8,128)(2,1)}, bf16[128,2048]{1,0:T(8,128)(2,1)}, u32[]{:S(2)}, u32[]{:S(2)}) collective-permute-start(bf16[128,2048]{1,0:T(8,128)(2,1)} %get-tuple-element.82), channel_id=1, source_target_pairs={{0,32},{1,33},{2,34},{3,35},{4,36},{5,37},{6,38},{7,39},{8,40},{9,... | collective-permute-start | bytes 1572872 | tf_op jit(solution)/shard_map/ppermute | solution.py:47
  183.4 25.4 %collective-permute-start.20 = (bf16[192,1024]{1,0:T(8,128)(2,1)}, bf16[192,1024]{1,0:T(8,128)(2,1)}, u32[]{:S(2)}, u32[]{:S(2)}) collective-permute-start(bf16[192,1024]{1,0:T(8,128)(2,1)} %add_convert_fusion), channel_id=1, source_target_pairs={{0,96},{1,97},{2,98},{3,99},{4,100},{5,101},{6,102},{7,103},{8,104... | collective-permute-start | bytes 1179656 | tf_op jit(solution)/shard_map/ppermute | solution.py:47
  183.9 24.9 %collective-permute-start.19 = (bf16[192,1024]{1,0:T(8,128)(2,1)}, bf16[192,1024]{1,0:T(8,128)(2,1)}, u32[]{:S(2)}, u32[]{:S(2)}) collective-permute-start(bf16[192,1024]{1,0:T(8,128)(2,1)} %add_convert_fusion.1), channel_id=1, source_target_pairs={{0,32},{1,33},{2,34},{3,35},{4,36},{5,37},{6,38},{7,39},{8,40},{9,... | collective-permute-start | bytes 1179656 | tf_op jit(solution)/shard_map/ppermute | solution.py:47
  221.6 43.5 %collective-permute-start.28 = (f32[192,1024]{1,0:T(8,128)}, f32[192,1024]{1,0:T(8,128)S(1)}, u32[]{:S(2)}, u32[]{:S(2)}) collective-permute-start(f32[192,1024]{1,0:T(8,128)} %get-tuple-element.78), channel_id=1, source_target_pairs={{0,1},{1,0},{2,3},{3,2},{4,5},{5,4},{6,7},{7,6},{8,9},{9,8},{10,11... | collective-permute-start | bytes 2359304 | tf_op jit(solution)/shard_map/ppermute | solution.py:47
  235.5 28.9 %collective-permute-start.27 = (bf16[192,1024]{1,0:T(8,128)(2,1)}, bf16[192,1024]{1,0:T(8,128)(2,1)S(1)}, u32[]{:S(2)}, u32[]{:S(2)}) collective-permute-start(bf16[192,1024]{1,0:T(8,128)(2,1)} %get-tuple-element.77), channel_id=1, source_target_pairs={{0,16},{1,17},{2,18},{3,19},{4,20},{5,21},{6,22},{7,23},{8,24},{9,... | collective-permute-start | bytes 1179656 | tf_op jit(solution)/shard_map/ppermute | solution.py:47
  236.7 27.6 %collective-permute-start.29 = (bf16[192,1024]{1,0:T(8,128)(2,1)}, bf16[192,1024]{1,0:T(8,128)(2,1)S(1)}, u32[]{:S(2)}, u32[]{:S(2)}) collective-permute-start(bf16[192,1024]{1,0:T(8,128)(2,1)} %get-tuple-element.79), channel_id=1, source_target_pairs={{0,17},{1,16},{2,19},{3,18},{4,21},{5,20},{6,23},{7,22},{8,25},{9,... | collective-permute-start | bytes 1179656 | tf_op jit(solution)/shard_map/ppermute | solution.py:47
  275.2 26.0 %all-to-all-start = ((bf16[128,32,128]{2,1,0:T(8,128)(2,1)}), bf16[128,32,128]{2,1,0:T(8,128)(2,1)S(1)}, u32[]{:S(2)}, u32[]{:S(2)}) async-start(bf16[128,32,128]{2,1,0:T(8,128)(2,1)} %copy-done.9), calls=%async_computation | async-start | bytes 2097152 | tf_op jit(solution)/shard_map/all_to_all | solution.py:423
  (66 other events, 598.6 us)

commit v3 on v2

--- a/solution.py
+++ b/solution.py
@@ -34,13 +34,9 @@
 def spread(a):
     def move(x, y, zl, zh, c):
         fy, fzl = 2 * zh + x // 2, x % 2
-        return (y - fy + a, y, fzl, zl ^ fzl, c)
+        return (y - fy + a, fy, fzl, zl, c)
 
     return permutation(move)
-
-
-def settle(a):
-    return permutation(lambda x, y, zl, zh, c: (x, y - x + a, zl, zh, c))
 
 
 def send(value, pairs):
@@ -49,6 +45,12 @@
 
 VMEM = pl.BlockSpec(memory_space=pltpu.VMEM)
 SMEM = pl.BlockSpec(memory_space=pltpu.SMEM)
+HBM = pl.BlockSpec(memory_space=pltpu.HBM)
+ANY = pl.BlockSpec(memory_space=pl.ANY)
+
+
+def off_chip(*arrays):
+    return [pltpu.with_memory_space_constraint(a, pltpu.HBM) for a in arrays]
 
 
 def params(megabytes):
@@ -122,106 +124,137 @@
     blocks = refs[:n_in]
     own, oth = refs[n_in : n_in + 2]
     zero_a, zero_b, one_a, three_b, up, down = refs[n_in + 2 : n_in + 8]
-    held = refs[n_in + 8]
-    step = pl.program_id(0)
-
-    @pl.when(step == 0)
-    def _():
-        at = 0
-        for ref in blocks:
-            rows = ref.shape[0]
-            held[at : at + rows, :] = ref[...]
-            at += rows
+    held, keep_a, keep_b, sems = refs[n_in + 8 :]
+    at = 0
+    for ref in blocks:
+        rows = ref.shape[0]
+        held[at : at + rows, :] = ref[...]
+        at += rows
 
     def rows_of(r, i, k):
         return r[i * 256 + k * 64 : i * 256 + k * 64 + 64]
 
-    @pl.when(step < 2)
-    def _():
-        r = jnp.dot(held[...], own[...], preferred_element_type=F32)
+    def first(j, carry):
+        cols = pl.ds(pl.multiple_of(j * 512, 512), 512)
+        r = jnp.dot(held[...], own[:, cols], preferred_element_type=F32)
         for i in range(n):
             at = slice(i * 64, i * 64 + 64)
-            zero_a[at, :] = rows_of(r, i, 0)
-            one_a[at, :] = rows_of(r, i, 1)
-            up[at, :] = rows_of(r, i, 2).astype(BF)
-            down[at, :] = rows_of(r, i, 3).astype(BF)
-
-    @pl.when(step >= 2)
-    def _():
-        r = jnp.dot(held[...], oth[...], preferred_element_type=F32)
+            keep_a[at, cols] = rows_of(r, i, 0)
+            one_a[at, cols] = rows_of(r, i, 1)
+            up[at, cols] = rows_of(r, i, 2).astype(BF)
+            down[at, cols] = rows_of(r, i, 3).astype(BF)
+        return carry
+
+    def second(j, carry):
+        cols = pl.ds(pl.multiple_of(j * 512, 512), 512)
+        wide = pl.ds(pl.multiple_of(j * 512 + 1024, 512), 512)
+        r = jnp.dot(held[...], oth[:, cols], preferred_element_type=F32)
         for i in range(n):
             at = slice(i * 64, i * 64 + 64)
-            zero_b[at, :] = rows_of(r, i, 0)
-            up[at, :] = rows_of(r, i, 1).astype(BF)
-            down[at, :] = rows_of(r, i, 2).astype(BF)
-            three_b[at, :] = rows_of(r, i, 3)
+            keep_b[at, cols] = rows_of(r, i, 0)
+            up[at, wide] = rows_of(r, i, 1).astype(BF)
+            down[at, wide] = rows_of(r, i, 2).astype(BF)
+            three_b[at, cols] = rows_of(r, i, 3)
+        return carry
+
+    lax.fori_loop(0, 2, first, 0)
+    copy_a = pltpu.make_async_copy(keep_a, zero_a, sems.at[0])
+    copy_a.start()
+    lax.fori_loop(0, 2, second, 0)
+    copy_b = pltpu.make_async_copy(keep_b, zero_b, sems.at[1])
+    copy_b.start()
+    copy_a.wait()
+    copy_b.wait()
 
 
 def product(groups, own, oth):
     flat = [a for g in groups for a in g]
     counts = tuple(len(g) for g in groups)
     n = len(groups)
-    whole = lambda a: pl.BlockSpec(a.shape, lambda s: (0, 0))
-    first = lambda s: (0, jnp.minimum(s, 1))
-    second = lambda s: (0, jnp.maximum(s - 2, 0))
     half = jax.ShapeDtypeStruct((n * 64, 1024), F32)
     full = jax.ShapeDtypeStruct((n * 64, 2048), BF)
-    out = lambda at: pl.BlockSpec((n * 64, 512), at)
     return pl.pallas_call(
         functools.partial(product_kernel, counts),
-        out_shape=[half] * 4 + [full] * 2,
-        grid=(4,),
-        in_specs=[whole(a) for a in flat]
-        + [pl.BlockSpec((2048, 512), first), pl.BlockSpec((2048, 512), second)],
-        out_specs=[out(first), out(second), out(first), out(second)]
-        + [out(lambda s: (0, s))] * 2,
-        scratch_shapes=[pltpu.VMEM((n * 256, 2048), BF)],
-        compiler_params=params(24),
+        out_shape=[pltpu.HBM(half.shape, F32)] * 2 + [half] * 2 + [full] * 2,
+        in_specs=[VMEM] * (len(flat) + 2),
+        out_specs=[HBM] * 2 + [VMEM] * 4,
+        scratch_shapes=[
+            pltpu.VMEM((n * 256, 2048), BF),
+            pltpu.VMEM((n * 64, 1024), F32),
+            pltpu.VMEM((n * 64, 1024), F32),
+            pltpu.SemaphoreType.DMA((2,)),
+        ],
+        compiler_params=params(28),
         cost_estimate=cost(2 * n * 256 * 2048 * 2048, (9 << 20) + n * (3 << 20)),
         name="product",
     )(*flat, own, oth)
 
 
-def settle_kernel(n_groups, members, low, *refs):
-    ins, outs = refs[: 6 * n_groups], refs[6 * n_groups :]
-    stay_a, stay_b, leave_a, leave_b = outs
-
-    def total(g, n):
+def collect_kernel(n_groups, members, low, *refs):
+    ins = refs[: 6 * n_groups]
+    stay_a, stay_b, leave_a, leave_b = refs[6 * n_groups : 6 * n_groups + 4]
+    wide, thin, sems = refs[6 * n_groups + 4 :]
+    chunks = [q for pair in members for q in pair]
+    copies = []
+    for k, (g, n) in enumerate(chunks):
         za, zb, up, down, nup, ndown = ins[6 * g : 6 * g + 6]
-        at = slice(n * 64, n * 64 + 64)
-        a = za[at, :] + down[at, :1024].astype(F32) + nup[at, :].astype(F32)
-        b = zb[at, :] + up[at, 1024:].astype(F32) + ndown[at, :].astype(F32)
+        at = pl.ds(n * 64, 64)
+        pairs = (
+            (za.at[at, :], wide.at[2 * k]),
+            (zb.at[at, :], wide.at[2 * k + 1]),
+            (down.at[at, pl.ds(0, 1024)], thin.at[4 * k]),
+            (nup.at[at, :], thin.at[4 * k + 1]),
+            (up.at[at, pl.ds(1024, 1024)], thin.at[4 * k + 2]),
+            (ndown.at[at, :], thin.at[4 * k + 3]),
+        )
+        copies += [pltpu.make_async_copy(a, b, sems.at[6 * k + j]) for j, (a, b) in enumerate(pairs)]
+    for copy in copies:
+        copy.start()
+    for copy in copies:
+        copy.wait()
+
+    def total(k):
+        a = wide[2 * k] + thin[4 * k].astype(F32) + thin[4 * k + 1].astype(F32)
+        b = wide[2 * k + 1] + thin[4 * k + 2].astype(F32) + thin[4 * k + 3].astype(F32)
         return a, b
 
     def write(swap):
-        for k, (c0, c1) in enumerate(members):
+        for k in range(len(members)):
             at = slice(k * 64, k * 64 + 64)
-            a, b = total(*(c1 if swap else c0))
+            a, b = total(2 * k + swap)
             stay_a[at, :] = a
             stay_b[at, :] = b
-            a, b = total(*(c0 if swap else c1))
+            a, b = total(2 * k + 1 - swap)
             leave_a[at, :] = a.astype(BF)
             leave_b[at, :] = b.astype(BF)
 
     @pl.when(low[0] == 1)
     def _():
-        write(False)
+        write(0)
 
     @pl.when(low[0] == 0)
     def _():
-        write(True)
+        write(1)
 
 
 def collect(low, groups, members):
     rows = 64 * len(members)
-    flat = [a for g in groups for a in g]
-    return pl.pallas_call(
-        functools.partial(settle_kernel, len(groups), members),
+    flat = []
+    for g in groups:
+        flat += off_chip(*g[:2]) + (off_chip(*g[2:]) if len(groups) > 1 else list(g[2:]))
+    n = 2 * len(members)
+    return pl.pallas_call(
+        functools.partial(collect_kernel, len(groups), members),
         out_shape=[jax.ShapeDtypeStruct((rows, 1024), F32)] * 2
         + [jax.ShapeDtypeStruct((rows, 1024), BF)] * 2,
-        in_specs=[SMEM] + [VMEM] * len(flat),
+        in_specs=[SMEM] + [ANY] * len(flat),
         out_specs=[VMEM] * 4,
-        compiler_params=params(20),
+        scratch_shapes=[
+            pltpu.VMEM((2 * n, 64, 1024), F32),
+            pltpu.VMEM((4 * n, 64, 1024), BF),
+            pltpu.SemaphoreType.DMA((6 * n,)),
+        ],
+        compiler_params=params(12),
         cost_estimate=cost(0, rows * 1024 * 24),
         name="collect",
     )(low, *flat)
@@ -270,14 +303,32 @@
 
 
 def outgoing_kernel(code, *refs):
-    full, out = refs[-2:]
+    ins = refs[:12]
+    full, out = refs[12:14]
+    full_v, out_v, wide, thin, sems = refs[14:]
+    copies = []
     at = 0
     for k in (0, 2):
         for g in range(2):
-            stay, got = refs[4 * g + k : 4 * g + k + 2]
+            stay, got = ins[4 * g + k : 4 * g + k + 2]
             rows = stay.shape[0]
-            full[at : at + rows, :] = stay[...] + got[...].astype(F32)
+            n = len(copies)
+            copies += [
+                pltpu.make_async_copy(stay, wide.at[pl.ds(at, rows), :], sems.at[n]),
+                pltpu.make_async_copy(got, thin.at[pl.ds(at, rows), :], sems.at[n + 1]),
+            ]
             at += rows
+    for copy in copies:
+        copy.start()
+    for k, to in ((0, 192), (2, 448)):
+        stay, got = ins[8 + k : 8 + k + 2]
+        full_v[to : to + 64, :] = stay[...] + got[...].astype(F32)
+    for copy in copies:
+        copy.wait()
+    for at, to in ((0, 0), (192, 256)):
+        full_v[to : to + 192, :] = wide[at : at + 192, :] + thin[at : at + 192, :].astype(F32)
+    save = pltpu.make_async_copy(full_v, full, sems.at[8])
+    save.start()
 
     def gather(s, carry):
         rows = []
@@ -286,22 +337,34 @@
             row = pl.multiple_of(lax.shift_right_logical(q, 4) * 8, 8)
             col = pl.multiple_of(lax.bitwise_and(lax.shift_right_logical(q, 1), 7) * 128, 128)
             w = lax.bitwise_and(q, 1).astype(F32)
-            rows.append(full[pl.ds(row, 8), pl.ds(col, 128)] * w)
-        out[s] = jnp.concatenate(rows, axis=0).astype(BF)
-        return carry
-
-    lax.fori_loop(0, 128, gather, 0, unroll=4)
+            rows.append(full_v[pl.ds(row, 8), pl.ds(col, 128)] * w)
+        out_v[s] = jnp.concatenate(rows, axis=0).astype(BF)
+        return carry
+
+    sends = []
+    for k in range(4):
+        part = pl.ds(32 * k, 32)
+        lax.fori_loop(32 * k, 32 * k + 32, gather, 0, unroll=4)
+        sends.append(pltpu.make_async_copy(out_v.at[part], out.at[part], sems.at[9 + k]))
+        sends[-1].start()
+    for copy in sends:
+        copy.wait()
+    save.wait()
 
 
 def outgoing(code, *parts):
     return pl.pallas_call(
         outgoing_kernel,
-        out_shape=[
-            jax.ShapeDtypeStruct((512, 1024), F32),
-            jax.ShapeDtypeStruct((128, 32, 128), BF),
+        out_shape=[pltpu.HBM((512, 1024), F32), pltpu.HBM((128, 32, 128), BF)],
+        in_specs=[SMEM] + [ANY] * 8 + [VMEM] * 4,
+        out_specs=[HBM] * 2,
+        scratch_shapes=[
+            pltpu.VMEM((512, 1024), F32),
+            pltpu.VMEM((128, 32, 128), BF),
+            pltpu.VMEM((384, 1024), F32),
+            pltpu.VMEM((384, 1024), BF),
+            pltpu.SemaphoreType.DMA((13,)),
         ],
-        in_specs=[SMEM] + [VMEM] * 8,
-        out_specs=[VMEM] * 2,
         compiler_params=params(12),
         cost_estimate=cost(0, 6 << 20),
         name="outgoing",
@@ -336,7 +399,19 @@
     )(row_of, mask, full, amp, occ, vir)
 
 
-def update_kernel(inverse, incoming, base, scale, out, wide):
+def update_kernel(inverse, incoming, base, scale, out, wide, base_v, scale_v, out_v, sems):
+    loads = []
+    for k in range(4):
+        part = pl.ds(128 * k, 128)
+        loads.append(
+            (
+                pltpu.make_async_copy(base.at[part, :], base_v.at[part, :], sems.at[3 * k]),
+                pltpu.make_async_copy(scale.at[part, :], scale_v.at[part, :], sems.at[3 * k + 1]),
+            )
+        )
+    for pair in loads:
+        for copy in pair:
+            copy.start()
     wide[...] = incoming[...].astype(F32)
 
     def row(r, carry):
@@ -345,28 +420,46 @@
             q = inverse[r * 8 + k]
             partner = wide[pl.ds(pl.multiple_of(q * 8, 8), 8), :]
             cols = slice(k * 128, k * 128 + 128)
-            out[pl.ds(at, 8), cols] = base[pl.ds(at, 8), cols] - partner * scale[pl.ds(at, 8), cols]
-        return carry
-
-    lax.fori_loop(0, 64, row, 0, unroll=4)
+            out_v[pl.ds(at, 8), cols] = (
+                base_v[pl.ds(at, 8), cols] - partner * scale_v[pl.ds(at, 8), cols]
+            )
+        return carry
+
+    stores = []
+    for k in range(4):
+        for copy in loads[k]:
+            copy.wait()
+        lax.fori_loop(16 * k, 16 * k + 16, row, 0, unroll=4)
+        part = pl.ds(128 * k, 128)
+        stores.append(pltpu.make_async_copy(out_v.at[part, :], out.at[part, :], sems.at[3 * k + 2]))
+        stores[-1].start()
+    for copy in stores:
+        copy.wait()
 
 
 def update(inverse, incoming, base, scale):
     return pl.pallas_call(
         update_kernel,
         out_shape=jax.ShapeDtypeStruct((512, 1024), F32),
-        in_specs=[SMEM] + [VMEM] * 3,
-        out_specs=VMEM,
-        scratch_shapes=[pltpu.VMEM((4096, 128), F32)],
-        compiler_params=params(12),
+        in_specs=[SMEM, VMEM, HBM, HBM],
+        out_specs=HBM,
+        scratch_shapes=[
+            pltpu.VMEM((4096, 128), F32),
+            pltpu.VMEM((512, 1024), F32),
+            pltpu.VMEM((512, 1024), F32),
+            pltpu.VMEM((512, 1024), F32),
+            pltpu.SemaphoreType.DMA((12,)),
+        ],
+        compiler_params=params(14),
         cost_estimate=cost(0, 7 << 20),
         name="update",
-    )(inverse, incoming, base, scale)
+    )(inverse, incoming, *off_chip(base, scale))
 
 
 GROUPS = (((0, 0),), ((0, 1), (1, 0), (3, 0)), ((1, 1), (3, 1)), ((2, 0), (2, 1)))
 LAST = (
-    ((0, 1, 2), (((0, 0), (1, 0)), ((1, 1), (2, 0)), ((1, 2), (2, 1)))),
+    ((0, 1), (((0, 0), (1, 0)),)),
+    ((1, 2), (((0, 1), (1, 0)), ((0, 2), (1, 1)))),
     ((3,), (((0, 0), (0, 1)),)),
 )
 
@@ -382,7 +475,6 @@
     got = send(give, shift(dc=1))
     pieces = weave(c[None], keep, got)
     moved = [send(pieces[a], spread(a)) for a in range(4)]
-    moved = [send(moved[a], settle(a)) for a in range(4)]
     own = integrals
     oth = send(integrals, shift(dc=1))
     block = {}
@@ -408,7 +500,7 @@
         ndown = send(ndown, shift(dy=-1))
         sums.append((za, zb, up, down, nup, ndown))
 
-    low = (zh == 0).astype(jnp.int32)[None]
+    low = (zh == ((device >> 4) & 1)).astype(jnp.int32)[None]
     last = []
     for groups, members in LAST:
         stay_a, stay_b, leave_a, leave_b = collect(low, [sums[k] for k in groups], members)

time: 309 us -> 281 us (0.909)
  waiting for transfers between devices: 138 us -> 110 us
  local copies, waits for them, and re-layouts: 34.1 us -> 20.4 us
  Pallas kernels: 49.8 us -> 57 us
  starting transfers between devices: 81.5 us -> 87.2 us
    ppermute x41 -> x40, waiting for transfers between devices: 126 us -> 99.3 us  [send(): return lax.ppermute(value, AXES, pairs)]
    unnamed x98 -> x72, local copies, waits for them, and re-layouts: 33.5 us -> 19.9 us
    ppermute x41 -> x40, starting transfers between devices: 74.5 us -> 81.4 us  [send(): return lax.ppermute(value, AXES, pairs)]
    pallas_call x7 -> x8, Pallas kernels: 38 us -> 44.3 us  [the longest x4 33.3 us: product(): pl.pallas_call(functools.partial(product_kernel, counts), out_shape=[pltp...]
  transfers between devices with their start and end apart: 42 -> 41, of which waited for: 16 -> 18; matrix products, arithmetic and copies ran while one was open for 1% -> 2% of each run, Pallas kernels for 14% -> 15%
where the time goes in v3:
time: 281 us; the launch traced here: 280 us
  waiting for transfers between devices  110 us (39%)
  starting transfers between devices  87.2 us (31%)
  Pallas kernels  57 us (20%)
  local copies, waits for them, and re-layouts  20.4 us (7%)
  other arithmetic  4.6 us (2%)
    ppermute x40, waiting for transfers between devices, send(): return lax.ppermute(value, AXES, pairs)  99.3 us
    ppermute x40, starting transfers between devices, send(): return lax.ppermute(value, AXES, pairs)  81.4 us
    pallas_call x4, Pallas kernels, product(): pl.pallas_call(functools.partial(product_kernel, counts), out_shape=[pltp...  33.3 us
    unnamed x72, local copies, waits for them, and re-layouts  19.9 us
    all_to_all x1, waiting for transfers between devices, compute(): lax.all_to_all(out, AXES, split_axis=0, concat_axis=0, tiled=True)  11.2 us
    pallas_call x3, Pallas kernels, collect(): pl.pallas_call(functools.partial(collect_kernel, len(groups), members), o...  7 us
    all_to_all x1, starting transfers between devices, compute(): lax.all_to_all(out, AXES, split_axis=0, concat_axis=0, tiled=True)  5.77 us
  transfers between devices with their start and end apart: 41, of which 18 were waited for; matrix products, arithmetic and copies ran while one was open for 2% of the time, Pallas kernels for 15%

profile of v3, /device:TPU:1, one launch (start us, length us, event | category | flops | bytes accessed | tf_op | source)
XLA Modules:
  0.0 280.4 jit_solution(8040782569894905123)
XLA Ops:
  3.8 5.3 %collective-permute-done.got = bf16[256,1024]{1,0:T(8,128)(2,1)S(1)} collective-permute-done((bf16[256,1024]{1,0:T(8,128)(2,1)S(1)}, bf16[256,1024]{1,0:T(8,128)(2,1)S(1)}, u32[]{:S(2)}, u32[]{:S(2)}) %collective-permute-start) | collective-permute-done | bytes 524320 | tf_op jit(solution)/shard_map/ppermute | solution.py:43
  9.9 6.1 %collective-permute-start.2 = (bf16[64,2048]{1,0:T(8,128)(2,1)S(1)}, bf16[64,2048]{1,0:T(8,128)(2,1)S(1)}, u32[]{:S(2)}, u32[]{:S(2)}) collective-permute-start(bf16[64,2048]{1,0:T(8,128)(2,1)S(1)} %get-tuple-element.59), channel_id=1, source_target_pairs={{0,2},{1,3},{2,18},{3,19},{4,32},{5,33},{6,48},{7,49},{8,70},{9,71... | collective-permute-start | bytes 786440 | tf_op jit(solution)/shard_map/ppermute | solution.py:43
  16.0 4.2 %collective-permute-start.3 = (bf16[64,2048]{1,0:T(8,128)(2,1)S(1)}, bf16[64,2048]{1,0:T(8,128)(2,1)S(1)}, u32[]{:S(2)}, u32[]{:S(2)}) collective-permute-start(bf16[64,2048]{1,0:T(8,128)(2,1)S(1)} %get-tuple-element.60), channel_id=1, source_target_pairs={{0,4},{1,5},{2,20},{3,21},{4,34},{5,35},{6,50},{7,51},{8,64},{9,65... | collective-permute-start | bytes 786440 | tf_op jit(solution)/shard_map/ppermute | solution.py:43
  20.1 8.9 %collective-permute-start.4 = (bf16[64,2048]{1,0:T(8,128)(2,1)S(1)}, bf16[64,2048]{1,0:T(8,128)(2,1)S(1)}, u32[]{:S(2)}, u32[]{:S(2)}) collective-permute-start(bf16[64,2048]{1,0:T(8,128)(2,1)S(1)} %get-tuple-element.61), channel_id=1, source_target_pairs={{0,6},{1,7},{2,22},{3,23},{4,36},{5,37},{6,52},{7,53},{8,66},{9,67... | collective-permute-start | bytes 786440 | tf_op jit(solution)/shard_map/ppermute | solution.py:43
  32.7 6.3 %collective-permute-done.4.refs_3_ = bf16[64,2048]{1,0:T(8,128)(2,1)S(1)} collective-permute-done((bf16[64,2048]{1,0:T(8,128)(2,1)S(1)}, bf16[64,2048]{1,0:T(8,128)(2,1)S(1)}, u32[]{:S(2)}, u32[]{:S(2)}) %collective-permute-start.4) | collective-permute-done | bytes 262176 | tf_op jit(solution)/shard_map/ppermute | solution.py:43
  39.6 8.4 %collective-permute-start.10 = (bf16[256,2048]{1,0:T(8,128)(2,1)S(1)}, bf16[256,2048]{1,0:T(8,128)(2,1)S(1)}, u32[]{:S(2)}, u32[]{:S(2)}) collective-permute-start(bf16[256,2048]{1,0:T(8,128)(2,1)S(1)} %join.1.refs_0_), channel_id=1, source_target_pairs={{0,8},{1,9},{2,10},{3,11},{4,12},{5,13},{6,14},{7,15},{8,0},{9,1},... | collective-permute-start | bytes 3145736 | tf_op jit(solution)/shard_map/ppermute | solution.py:43
  48.1 6.3 %collective-permute-start.11 = (bf16[256,2048]{1,0:T(8,128)(2,1)S(1)}, bf16[256,2048]{1,0:T(8,128)(2,1)S(1)}, u32[]{:S(2)}, u32[]{:S(2)}) collective-permute-start(bf16[256,2048]{1,0:T(8,128)(2,1)S(1)} %join.1.refs_0_), channel_id=1, source_target_pairs={{0,6},{1,7},{2,0},{3,1},{4,2},{5,3},{6,4},{7,5},{8,14},{9,15},{10,... | collective-permute-start | bytes 3145736 | tf_op jit(solution)/shard_map/ppermute | solution.py:43
  54.4 15.6 %collective-permute-done.10.refs_0_ = bf16[256,2048]{1,0:T(8,128)(2,1)S(1)} collective-permute-done((bf16[256,2048]{1,0:T(8,128)(2,1)S(1)}, bf16[256,2048]{1,0:T(8,128)(2,1)S(1)}, u32[]{:S(2)}, u32[]{:S(2)}) %collective-permute-start.10) | collective-permute-done | bytes 1048608 | tf_op jit(solution)/shard_map/ppermute | solution.py:43
  70.0 7.0 %collective-permute-start.20 = (bf16[256,2048]{1,0:T(8,128)(2,1)S(1)}, bf16[256,2048]{1,0:T(8,128)(2,1)S(1)}, u32[]{:S(2)}, u32[]{:S(2)}) collective-permute-start(bf16[256,2048]{1,0:T(8,128)(2,1)S(1)} %collective-permute-done.10.refs_0_), channel_id=1, source_target_pairs={{0,6},{1,7},{2,0},{3,1},{4,2},{5,3},{6,4},{7,5},{8,14},{9,15},{10,... | collective-permute-start | bytes 3145736 | tf_op jit(solution)/shard_map/ppermute | solution.py:43
  80.0 18.1 %collective-permute-done.20.refs_0_ = bf16[256,2048]{1,0:T(8,128)(2,1)S(1)} collective-permute-done((bf16[256,2048]{1,0:T(8,128)(2,1)S(1)}, bf16[256,2048]{1,0:T(8,128)(2,1)S(1)}, u32[]{:S(2)}, u32[]{:S(2)}) %collective-permute-start.20) | collective-permute-done | bytes 1048608 | tf_op jit(solution)/shard_map/ppermute | solution.py:43
  101.7 7.6 %collective-permute-done.29.refs_0_ = bf16[128,2048]{1,0:T(8,128)(2,1)S(1)} collective-permute-done((bf16[128,2048]{1,0:T(8,128)(2,1)S(1)}, bf16[128,2048]{1,0:T(8,128)(2,1)S(1)}, u32[]{:S(2)}, u32[]{:S(2)}) %collective-permute-start.29) | collective-permute-done | bytes 524320 | tf_op jit(solution)/shard_map/ppermute | solution.py:43
  112.4 8.1 %collective-permute-done.31.refs_2_ = bf16[128,2048]{1,0:T(8,128)(2,1)S(1)} collective-permute-done((bf16[128,2048]{1,0:T(8,128)(2,1)S(1)}, bf16[128,2048]{1,0:T(8,128)(2,1)S(1)}, u32[]{:S(2)}, u32[]{:S(2)}) %collective-permute-start.31) | collective-permute-done | bytes 524320 | tf_op jit(solution)/shard_map/ppermute | solution.py:43
  123.7 8.2 %product.7 = (f32[128,1024]{1,0:T(8,128)}, f32[128,1024]{1,0:T(8,128)}, f32[128,1024]{1,0:T(8,128)S(1)}, f32[128,1024]{1,0:T(8,128)S(1)}, bf16[128,2048]{1,0:T(8,128)(2,1)S(1)}, /*index=5*/bf16[128,2048]{1,0:T(8,128)(2,1)S(1)}) custom-call(bf16[128,2048]{1,0:T(8,128)(2,1)S(1)} %collective-permute-done.29.refs_0_, ...), custom_call_target="tpu_custom_call" | custom-call | flops 4294967296 | bytes 15728640 | tf_op jit(solution)/shard_map/product/pallas_call | solution.py:176
  133.4 8.1 %product.6 = (f32[128,1024]{1,0:T(8,128)}, f32[128,1024]{1,0:T(8,128)}, f32[128,1024]{1,0:T(8,128)S(1)}, f32[128,1024]{1,0:T(8,128)S(1)}, bf16[128,2048]{1,0:T(8,128)(2,1)S(1)}, /*index=5*/bf16[128,2048]{1,0:T(8,128)(2,1)S(1)}) custom-call(bf16[256,2048]{1,0:T(8,128)(2,1)S(1)} %collective-permute-done.20.refs_0_, ...), custom_call_target="tpu_custom_call" | custom-call | flops 4294967296 | bytes 15728640 | tf_op jit(solution)/shard_map/product/pallas_call | solution.py:176
  143.1 10.4 %product.5 = (f32[192,1024]{1,0:T(8,128)}, f32[192,1024]{1,0:T(8,128)}, f32[192,1024]{1,0:T(8,128)S(1)}, f32[192,1024]{1,0:T(8,128)S(1)}, bf16[192,2048]{1,0:T(8,128)(2,1)S(1)}, /*index=5*/bf16[192,2048]{1,0:T(8,128)(2,1)S(1)}) custom-call(bf16[256,2048]{1,0:T(8,128)(2,1)S(1)} %collective-permute-done.10.refs_0_, ...), custom_call_target="tpu_custom_call" | custom-call | flops 6442450944 | bytes 18874368 | tf_op jit(solution)/shard_map/product/pallas_call | solution.py:176
  156.3 6.5 %product.4 = (f32[64,1024]{1,0:T(8,128)}, f32[64,1024]{1,0:T(8,128)}, f32[64,1024]{1,0:T(8,128)S(1)}, f32[64,1024]{1,0:T(8,128)S(1)}, bf16[64,2048]{1,0:T(8,128)(2,1)}, /*index=5*/bf16[64,2048]{1,0:T(8,128)(2,1)S(1)}) custom-call(bf16[256,2048]{1,0:T(8,128)(2,1)S(1)} %join.1.refs_0_, bf16[2048,1024]{1,0:T(8,128)(2,1)S(1)} %copy-done.2, ...), custom_call_target="tpu_custom_call" | custom-call | flops 2147483648 | bytes 12582912 | tf_op jit(solution)/shard_map/product/pallas_call | solution.py:176
  171.5 8.0 %collective-permute-done.13.refs_8_.refs_2_ = bf16[192,2048]{1,0:T(8,128)(2,1)S(1)} collective-permute-done((bf16[192,2048]{1,0:T(8,128)(2,1)S(1)}, bf16[192,2048]{1,0:T(8,128)(2,1)S(1)}, u32[]{:S(2)}, u32[]{:S(2)}) %collective-permute-start.13) | collective-permute-done | bytes 786464 | tf_op jit(solution)/shard_map/ppermute | solution.py:43
  186.9 7.8 %collective-permute-done.25.refs_11_ = bf16[128,1024]{1,0:T(8,128)(2,1)} collective-permute-done((bf16[128,1024]{1,0:T(8,128)(2,1)}, bf16[128,1024]{1,0:T(8,128)(2,1)}, u32[]{:S(2)}, u32[]{:S(2)}) %collective-permute-start.25) | collective-permute-done | bytes 262176 | tf_op jit(solution)/shard_map/ppermute | solution.py:43
  198.8 7.9 %collective-permute-start.38 = (f32[64,1024]{1,0:T(8,128)S(1)}, f32[64,1024]{1,0:T(8,128)S(1)}, u32[]{:S(2)}, u32[]{:S(2)}) collective-permute-start(f32[64,1024]{1,0:T(8,128)S(1)} %get-tuple-element.96), channel_id=1, source_target_pairs={{0,1},{1,0},{2,3},{3,2},{4,5},{5,4},{6,7},{7,6},{8,9},{9,8},{10,11... | collective-permute-start | bytes 786440 | tf_op jit(solution)/shard_map/ppermute | solution.py:43
  231.5 4.3 %index.1 = (s32[512]{0:T(512)S(1)}, s32[512]{0:T(512)S(1)}, s32[64]{0:T(128)S(1)}) custom-call(s32[2]{0:T(128)S(1)} %pad_add_fusion.place, s32[512]{0:T(512)S(1)} %reshape.9.slots, s32[512]{0:T(512)S(1)} %reshape.10.mask), custom_call_target="tpu_custom_call" | custom-call | bytes 8192 | tf_op jit(solution)/shard_map/index/pallas_call | solution.py:293
  247.7 4.0 %outgoing.1 = (f32[512,1024]{1,0:T(8,128)}, bf16[128,32,128]{2,1,0:T(8,128)(2,1)}) custom-call(s32[512]{0:T(512)S(1)} %get-tuple-element.55.code, f32[64,1024]{1,0:T(8,128)S(1)} %copy-done.11, bf16[64,1024]{1,0:T(8,128)(2,1)S(1)} %copy-done.19, f32[64,1024]{1,0:T(8,128)S(1)} %copy-done.15, bf16[64,1024]{1,0:T(8,128)(2,1)S(1)} %copy-done.21, ...), custom_call_target="tpu_custom_call" | custom-call | bytes 6291456 | tf_op jit(solution)/shard_map/outgoing/pallas_call | solution.py:356
  251.7 5.8 %all-to-all-start = ((bf16[128,32,128]{2,1,0:T(8,128)(2,1)}), bf16[128,32,128]{2,1,0:T(8,128)(2,1)S(1)}, u32[]{:S(2)}, u32[]{:S(2)}) async-start(bf16[128,32,128]{2,1,0:T(8,128)(2,1)} %get-tuple-element.98), calls=%async_computation | async-start | bytes 2097152 | tf_op jit(solution)/shard_map/all_to_all | solution.py:515
  265.3 11.2 %all-to-all-done = bf16[128,32,128]{2,1,0:T(8,128)(2,1)S(1)} async-done(((bf16[128,32,128]{2,1,0:T(8,128)(2,1)}), bf16[128,32,128]{2,1,0:T(8,128)(2,1)S(1)}, u32[]{:S(2)}, u32[]{:S(2)}) %all-to-all-start) | async-done | bytes 1048608 | tf_op jit(solution)/shard_map/all_to_all | solution.py:515
  276.4 3.8 %update.1 = f32[512,1024]{1,0:T(8,128)} custom-call(s32[512]{0:T(512)S(1)} %get-tuple-element.54.inverse, bf16[4096,128]{1,0:T(8,128)(2,1)S(1)} %bitcast.18, f32[512,1024]{1,0:T(8,128)} %copy-done.4, f32[512,1024]{1,0:T(8,128)} %copy-done.5), custom_call_target="tpu_custom_call" | custom-call | bytes 7340032 | tf_op jit(solution)/shard_map/update/pallas_call | solution.py:441
  (162 shorter events, 91.8 us)
Async XLA Ops:
  0.0 123.7 %collective-permute-start.5 = (bf16[2048,1024]{1,0:T(8,128)(2,1)}, bf16[2048,1024]{1,0:T(8,128)(2,1)}, u32[]{:S(2)}, u32[]{:S(2)}) collective-permute-start(bf16[2048,1024]{1,0:T(8,128)(2,1)} %refs_4_.1), channel_id=1, source_target_pairs={{0,1},{1,0},{2,3},{3,2},{4,5},{5,4},{6,7},{7,6},{8,9},{9,8},{10,11... | collective-permute-start | bytes 12582920 | tf_op jit(solution)/shard_map/ppermute | solution.py:43
  9.2 19.9 %collective-permute-start.1 = (bf16[64,2048]{1,0:T(8,128)(2,1)S(1)}, bf16[64,2048]{1,0:T(8,128)(2,1)S(1)}, u32[]{:S(2)}, u32[]{:S(2)}) collective-permute-start(bf16[64,2048]{1,0:T(8,128)(2,1)S(1)} %get-tuple-element.58), channel_id=1, source_target_pairs={{0,0},{1,1},{2,16},{3,17},{4,38},{5,39},{6,54},{7,55},{8,68},{9,69... | collective-permute-start | bytes 786440 | tf_op jit(solution)/shard_map/ppermute | solution.py:43
  9.9 19.2 %collective-permute-start.2 = (bf16[64,2048]{1,0:T(8,128)(2,1)S(1)}, bf16[64,2048]{1,0:T(8,128)(2,1)S(1)}, u32[]{:S(2)}, u32[]{:S(2)}) collective-permute-start(bf16[64,2048]{1,0:T(8,128)(2,1)S(1)} %get-tuple-element.59), channel_id=1, source_target_pairs={{0,2},{1,3},{2,18},{3,19},{4,32},{5,33},{6,48},{7,49},{8,70},{9,71... | collective-permute-start | bytes 786440 | tf_op jit(solution)/shard_map/ppermute | solution.py:43
  39.6 30.4 %collective-permute-start.10 = (bf16[256,2048]{1,0:T(8,128)(2,1)S(1)}, bf16[256,2048]{1,0:T(8,128)(2,1)S(1)}, u32[]{:S(2)}, u32[]{:S(2)}) collective-permute-start(bf16[256,2048]{1,0:T(8,128)(2,1)S(1)} %join.1.refs_0_), channel_id=1, source_target_pairs={{0,8},{1,9},{2,10},{3,11},{4,12},{5,13},{6,14},{7,15},{8,0},{9,1},... | collective-permute-start | bytes 3145736 | tf_op jit(solution)/shard_map/ppermute | solution.py:43
  48.1 29.0 %collective-permute-start.11 = (bf16[256,2048]{1,0:T(8,128)(2,1)S(1)}, bf16[256,2048]{1,0:T(8,128)(2,1)S(1)}, u32[]{:S(2)}, u32[]{:S(2)}) collective-permute-start(bf16[256,2048]{1,0:T(8,128)(2,1)S(1)} %join.1.refs_0_), channel_id=1, source_target_pairs={{0,6},{1,7},{2,0},{3,1},{4,2},{5,3},{6,4},{7,5},{8,14},{9,15},{10,... | collective-permute-start | bytes 3145736 | tf_op jit(solution)/shard_map/ppermute | solution.py:43
  54.4 25.5 %collective-permute-start.12 = (bf16[256,2048]{1,0:T(8,128)(2,1)S(1)}, bf16[256,2048]{1,0:T(8,128)(2,1)S(1)}, u32[]{:S(2)}, u32[]{:S(2)}) collective-permute-start(bf16[256,2048]{1,0:T(8,128)(2,1)S(1)} %join.1.refs_0_), channel_id=1, source_target_pairs={{0,2},{1,3},{2,4},{3,5},{4,6},{5,7},{6,0},{7,1},{8,10},{9,11},{10,... | collective-permute-start | bytes 3145736 | tf_op jit(solution)/shard_map/ppermute | solution.py:43
  70.0 28.1 %collective-permute-start.20 = (bf16[256,2048]{1,0:T(8,128)(2,1)S(1)}, bf16[256,2048]{1,0:T(8,128)(2,1)S(1)}, u32[]{:S(2)}, u32[]{:S(2)}) collective-permute-start(bf16[256,2048]{1,0:T(8,128)(2,1)S(1)} %collective-permute-done.10.refs_0_), channel_id=1, source_target_pairs={{0,6},{1,7},{2,0},{3,1},{4,2},{5,3},{6,4},{7,5},{8,14},{9,15},{10,... | collective-permute-start | bytes 3145736 | tf_op jit(solution)/shard_map/ppermute | solution.py:43
  77.0 24.6 %collective-permute-start.21 = (bf16[256,2048]{1,0:T(8,128)(2,1)S(1)}, bf16[256,2048]{1,0:T(8,128)(2,1)S(1)}, u32[]{:S(2)}, u32[]{:S(2)}) collective-permute-start(bf16[256,2048]{1,0:T(8,128)(2,1)S(1)} %collective-permute-done.10.refs_0_), channel_id=1, source_target_pairs={{0,2},{1,3},{2,4},{3,5},{4,6},{5,7},{6,0},{7,1},{8,10},{9,11},{10,... | collective-permute-start | bytes 3145736 | tf_op jit(solution)/shard_map/ppermute | solution.py:43
  77.1 32.2 %collective-permute-start.29 = (bf16[128,2048]{1,0:T(8,128)(2,1)S(1)}, bf16[128,2048]{1,0:T(8,128)(2,1)S(1)}, u32[]{:S(2)}, u32[]{:S(2)}) collective-permute-start(bf16[128,2048]{1,0:T(8,128)(2,1)S(1)} %slice.54), channel_id=1, source_target_pairs={{0,6},{1,7},{2,0},{3,1},{4,2},{5,3},{6,4},{7,5},{8,14},{9,15},{10,... | collective-permute-start | bytes 1572872 | tf_op jit(solution)/shard_map/ppermute | solution.py:43
  79.9 32.6 %collective-permute-start.30 = (bf16[128,2048]{1,0:T(8,128)(2,1)S(1)}, bf16[128,2048]{1,0:T(8,128)(2,1)S(1)}, u32[]{:S(2)}, u32[]{:S(2)}) collective-permute-start(bf16[128,2048]{1,0:T(8,128)(2,1)S(1)} %slice.55), channel_id=1, source_target_pairs={{0,2},{1,3},{2,4},{3,5},{4,6},{5,7},{6,0},{7,1},{8,10},{9,11},{10,... | collective-permute-start | bytes 1572872 | tf_op jit(solution)/shard_map/ppermute | solution.py:43
  98.1 22.4 %collective-permute-start.31 = (bf16[128,2048]{1,0:T(8,128)(2,1)S(1)}, bf16[128,2048]{1,0:T(8,128)(2,1)S(1)}, u32[]{:S(2)}, u32[]{:S(2)}) collective-permute-start(bf16[128,2048]{1,0:T(8,128)(2,1)S(1)} %slice.56), channel_id=1, source_target_pairs={{0,6},{1,7},{2,0},{3,1},{4,2},{5,3},{6,4},{7,5},{8,14},{9,15},{10,... | collective-permute-start | bytes 1572872 | tf_op jit(solution)/shard_map/ppermute | solution.py:43
  101.7 22.0 %collective-permute-start.32 = (bf16[128,2048]{1,0:T(8,128)(2,1)S(1)}, bf16[128,2048]{1,0:T(8,128)(2,1)S(1)}, u32[]{:S(2)}, u32[]{:S(2)}) collective-permute-start(bf16[128,2048]{1,0:T(8,128)(2,1)S(1)} %slice.57), channel_id=1, source_target_pairs={{0,2},{1,3},{2,4},{3,5},{4,6},{5,7},{6,0},{7,1},{8,10},{9,11},{10,... | collective-permute-start | bytes 1572872 | tf_op jit(solution)/shard_map/ppermute | solution.py:43
  131.9 30.9 %collective-permute-start.34 = (bf16[128,2048]{1,0:T(8,128)(2,1)S(1)}, bf16[128,2048]{1,0:T(8,128)(2,1)S(1)}, u32[]{:S(2)}, u32[]{:S(2)}) collective-permute-start(bf16[128,2048]{1,0:T(8,128)(2,1)S(1)} %get-tuple-element.91), channel_id=1, source_target_pairs={{0,96},{1,97},{2,98},{3,99},{4,100},{5,101},{6,102},{7,103},{8,104... | collective-permute-start | bytes 1572872 | tf_op jit(solution)/shard_map/ppermute | solution.py:43
  132.0 31.0 %collective-permute-start.33 = (bf16[128,2048]{1,0:T(8,128)(2,1)S(1)}, bf16[128,2048]{1,0:T(8,128)(2,1)S(1)}, u32[]{:S(2)}, u32[]{:S(2)}) collective-permute-start(bf16[128,2048]{1,0:T(8,128)(2,1)S(1)} %get-tuple-element.90), channel_id=1, source_target_pairs={{0,32},{1,33},{2,34},{3,35},{4,36},{5,37},{6,38},{7,39},{8,40},{9,... | collective-permute-start | bytes 1572872 | tf_op jit(solution)/shard_map/ppermute | solution.py:43
  141.5 24.2 %collective-permute-start.23 = (bf16[128,2048]{1,0:T(8,128)(2,1)S(1)}, bf16[128,2048]{1,0:T(8,128)(2,1)S(1)}, u32[]{:S(2)}, u32[]{:S(2)}) collective-permute-start(bf16[128,2048]{1,0:T(8,128)(2,1)S(1)} %get-tuple-element.81), channel_id=1, source_target_pairs={{0,96},{1,97},{2,98},{3,99},{4,100},{5,101},{6,102},{7,103},{8,104... | collective-permute-start | bytes 1572872 | tf_op jit(solution)/shard_map/ppermute | solution.py:43
  142.9 37.5 %collective-permute-start.22 = (bf16[128,2048]{1,0:T(8,128)(2,1)S(1)}, bf16[128,2048]{1,0:T(8,128)(2,1)S(1)}, u32[]{:S(2)}, u32[]{:S(2)}) collective-permute-start(bf16[128,2048]{1,0:T(8,128)(2,1)S(1)} %get-tuple-element.80), channel_id=1, source_target_pairs={{0,32},{1,33},{2,34},{3,35},{4,36},{5,37},{6,38},{7,39},{8,40},{9,... | collective-permute-start | bytes 1572872 | tf_op jit(solution)/shard_map/ppermute | solution.py:43
  163.0 19.7 %collective-permute-start.7 = (bf16[64,2048]{1,0:T(8,128)(2,1)S(1)}, bf16[64,2048]{1,0:T(8,128)(2,1)S(1)}, u32[]{:S(2)}, u32[]{:S(2)}) collective-permute-start(bf16[64,2048]{1,0:T(8,128)(2,1)S(1)} %get-tuple-element.65), channel_id=1, source_target_pairs={{0,96},{1,97},{2,98},{3,99},{4,100},{5,101},{6,102},{7,103},{8,104... | collective-permute-start | bytes 786440 | tf_op jit(solution)/shard_map/ppermute | solution.py:43
  179.5 27.1 %collective-permute-start.16 = (bf16[192,1024]{1,0:T(8,128)(2,1)}, bf16[192,1024]{1,0:T(8,128)(2,1)S(1)}, u32[]{:S(2)}, u32[]{:S(2)}) collective-permute-start(bf16[192,1024]{1,0:T(8,128)(2,1)} %add_convert_fusion), channel_id=1, source_target_pairs={{0,96},{1,97},{2,98},{3,99},{4,100},{5,101},{6,102},{7,103},{8,104... | collective-permute-start | bytes 1179656 | tf_op jit(solution)/shard_map/ppermute | solution.py:43
  180.5 26.2 %collective-permute-start.15 = (bf16[192,1024]{1,0:T(8,128)(2,1)}, bf16[192,1024]{1,0:T(8,128)(2,1)S(1)}, u32[]{:S(2)}, u32[]{:S(2)}) collective-permute-start(bf16[192,1024]{1,0:T(8,128)(2,1)} %add_convert_fusion.1), channel_id=1, source_target_pairs={{0,32},{1,33},{2,34},{3,35},{4,36},{5,37},{6,38},{7,39},{8,40},{9,... | collective-permute-start | bytes 1179656 | tf_op jit(solution)/shard_map/ppermute | solution.py:43
  185.1 26.0 %collective-permute-start.6 = (bf16[64,2048]{1,0:T(8,128)(2,1)}, bf16[64,2048]{1,0:T(8,128)(2,1)}, u32[]{:S(2)}, u32[]{:S(2)}) collective-permute-start(bf16[64,2048]{1,0:T(8,128)(2,1)} %get-tuple-element.64), channel_id=1, source_target_pairs={{0,32},{1,33},{2,34},{3,35},{4,36},{5,37},{6,38},{7,39},{8,40},{9,... | collective-permute-start | bytes 786440 | tf_op jit(solution)/shard_map/ppermute | solution.py:43
  198.8 26.0 %collective-permute-start.38 = (f32[64,1024]{1,0:T(8,128)S(1)}, f32[64,1024]{1,0:T(8,128)S(1)}, u32[]{:S(2)}, u32[]{:S(2)}) collective-permute-start(f32[64,1024]{1,0:T(8,128)S(1)} %get-tuple-element.96), channel_id=1, source_target_pairs={{0,1},{1,0},{2,3},{3,2},{4,5},{5,4},{6,7},{7,6},{8,9},{9,8},{10,11... | collective-permute-start | bytes 786440 | tf_op jit(solution)/shard_map/ppermute | solution.py:43
  211.0 29.1 %collective-permute-start.27 = (f32[128,1024]{1,0:T(8,128)}, f32[128,1024]{1,0:T(8,128)S(1)}, u32[]{:S(2)}, u32[]{:S(2)}) collective-permute-start(f32[128,1024]{1,0:T(8,128)} %get-tuple-element.86), channel_id=1, source_target_pairs={{0,1},{1,0},{2,3},{3,2},{4,5},{5,4},{6,7},{7,6},{8,9},{9,8},{10,11... | collective-permute-start | bytes 1572872 | tf_op jit(solution)/shard_map/ppermute | solution.py:43
  217.9 20.1 %collective-permute-start.26 = (bf16[128,1024]{1,0:T(8,128)(2,1)}, bf16[128,1024]{1,0:T(8,128)(2,1)S(1)}, u32[]{:S(2)}, u32[]{:S(2)}) collective-permute-start(bf16[128,1024]{1,0:T(8,128)(2,1)} %get-tuple-element.85), channel_id=1, source_target_pairs={{0,16},{1,17},{2,18},{3,19},{4,20},{5,21},{6,22},{7,23},{8,24},{9,... | collective-permute-start | bytes 786440 | tf_op jit(solution)/shard_map/ppermute | solution.py:43
  251.7 24.7 %all-to-all-start = ((bf16[128,32,128]{2,1,0:T(8,128)(2,1)}), bf16[128,32,128]{2,1,0:T(8,128)(2,1)S(1)}, u32[]{:S(2)}, u32[]{:S(2)}) async-start(bf16[128,32,128]{2,1,0:T(8,128)(2,1)} %get-tuple-element.98), calls=%async_computation | async-start | bytes 2097152 | tf_op jit(solution)/shard_map/all_to_all | solution.py:515
  (52 other events, 437.0 us)

commit v4 on v3

--- a/solution.py
+++ b/solution.py
@@ -116,6 +116,25 @@
         cost_estimate=cost(0, 2 << 20),
         name="join",
     )(where, *pieces)
+
+
+def hold_kernel(source, target, sem):
+    copy = pltpu.make_async_copy(source, target, sem)
+    copy.start()
+    copy.wait()
+
+
+def hold(source):
+    return pl.pallas_call(
+        hold_kernel,
+        out_shape=jax.ShapeDtypeStruct(source.shape, source.dtype),
+        in_specs=[ANY],
+        out_specs=VMEM,
+        scratch_shapes=[pltpu.SemaphoreType.DMA],
+        compiler_params=params(6),
+        cost_estimate=cost(0, 8 << 20),
+        name="hold",
+    )(*off_chip(source))
 
 
 def product_kernel(counts, *refs):
@@ -475,7 +494,7 @@
     got = send(give, shift(dc=1))
     pieces = weave(c[None], keep, got)
     moved = [send(pieces[a], spread(a)) for a in range(4)]
-    own = integrals
+    own = hold(integrals)
     oth = send(integrals, shift(dc=1))
     block = {}
     block[0, 0] = join(jnp.stack([(x - a) & 3 for a in range(4)]), moved)

time: 281 us -> 281 us (level)
    unnamed x72 -> x70, local copies, waits for them, and re-layouts: 19.9 us -> 19.8 us
where the time goes in v4:
time: 281 us; the launch traced here: 280 us
  waiting for transfers between devices  108 us (38%)
  starting transfers between devices  87.2 us (31%)
  Pallas kernels  59.2 us (21%)
  local copies, waits for them, and re-layouts  20.4 us (7%)
  other arithmetic  4.59 us (2%)
    ppermute x40, waiting for transfers between devices, send(): return lax.ppermute(value, AXES, pairs)  97.1 us
    ppermute x40, starting transfers between devices, send(): return lax.ppermute(value, AXES, pairs)  81.4 us
    pallas_call x4, Pallas kernels, product(): pl.pallas_call(functools.partial(product_kernel, counts), out_shape=[pltp...  33.2 us
    unnamed x70, local copies, waits for them, and re-layouts  19.8 us
    all_to_all x1, waiting for transfers between devices, compute(): lax.all_to_all(out, AXES, split_axis=0, concat_axis=0, tiled=True)  11.2 us
    pallas_call x3, Pallas kernels, collect(): pl.pallas_call(functools.partial(collect_kernel, len(groups), members), o...  6.99 us
    all_to_all x1, starting transfers between devices, compute(): lax.all_to_all(out, AXES, split_axis=0, concat_axis=0, tiled=True)  5.78 us
  transfers between devices with their start and end apart: 41, of which 18 were waited for; matrix products, arithmetic and copies ran while one was open for 2% of the time, Pallas kernels for 15%

profile of v4, /device:TPU:1, one launch (start us, length us, event | category | flops | bytes accessed | tf_op | source)
XLA Modules:
  0.0 280.3 jit_solution(13649827722053026527)
XLA Ops:
  3.8 5.3 %collective-permute-done.got = bf16[256,1024]{1,0:T(8,128)(2,1)S(1)} collective-permute-done((bf16[256,1024]{1,0:T(8,128)(2,1)S(1)}, bf16[256,1024]{1,0:T(8,128)(2,1)S(1)}, u32[]{:S(2)}, u32[]{:S(2)}) %collective-permute-start) | collective-permute-done | bytes 524320 | tf_op jit(solution)/shard_map/ppermute | solution.py:43
  9.9 6.1 %collective-permute-start.2 = (bf16[64,2048]{1,0:T(8,128)(2,1)S(1)}, bf16[64,2048]{1,0:T(8,128)(2,1)S(1)}, u32[]{:S(2)}, u32[]{:S(2)}) collective-permute-start(bf16[64,2048]{1,0:T(8,128)(2,1)S(1)} %get-tuple-element.59), channel_id=1, source_target_pairs={{0,2},{1,3},{2,18},{3,19},{4,32},{5,33},{6,48},{7,49},{8,70},{9,71... | collective-permute-start | bytes 786440 | tf_op jit(solution)/shard_map/ppermute | solution.py:43
  16.0 4.2 %collective-permute-start.3 = (bf16[64,2048]{1,0:T(8,128)(2,1)S(1)}, bf16[64,2048]{1,0:T(8,128)(2,1)S(1)}, u32[]{:S(2)}, u32[]{:S(2)}) collective-permute-start(bf16[64,2048]{1,0:T(8,128)(2,1)S(1)} %get-tuple-element.60), channel_id=1, source_target_pairs={{0,4},{1,5},{2,20},{3,21},{4,34},{5,35},{6,50},{7,51},{8,64},{9,65... | collective-permute-start | bytes 786440 | tf_op jit(solution)/shard_map/ppermute | solution.py:43
  20.1 8.9 %collective-permute-start.4 = (bf16[64,2048]{1,0:T(8,128)(2,1)S(1)}, bf16[64,2048]{1,0:T(8,128)(2,1)S(1)}, u32[]{:S(2)}, u32[]{:S(2)}) collective-permute-start(bf16[64,2048]{1,0:T(8,128)(2,1)S(1)} %get-tuple-element.61), channel_id=1, source_target_pairs={{0,6},{1,7},{2,22},{3,23},{4,36},{5,37},{6,52},{7,53},{8,66},{9,67... | collective-permute-start | bytes 786440 | tf_op jit(solution)/shard_map/ppermute | solution.py:43
  32.7 6.3 %collective-permute-done.4.refs_3_ = bf16[64,2048]{1,0:T(8,128)(2,1)S(1)} collective-permute-done((bf16[64,2048]{1,0:T(8,128)(2,1)S(1)}, bf16[64,2048]{1,0:T(8,128)(2,1)S(1)}, u32[]{:S(2)}, u32[]{:S(2)}) %collective-permute-start.4) | collective-permute-done | bytes 262176 | tf_op jit(solution)/shard_map/ppermute | solution.py:43
  39.6 8.4 %collective-permute-start.10 = (bf16[256,2048]{1,0:T(8,128)(2,1)S(1)}, bf16[256,2048]{1,0:T(8,128)(2,1)S(1)}, u32[]{:S(2)}, u32[]{:S(2)}) collective-permute-start(bf16[256,2048]{1,0:T(8,128)(2,1)S(1)} %join.1.refs_0_), channel_id=1, source_target_pairs={{0,8},{1,9},{2,10},{3,11},{4,12},{5,13},{6,14},{7,15},{8,0},{9,1},... | collective-permute-start | bytes 3145736 | tf_op jit(solution)/shard_map/ppermute | solution.py:43
  48.1 6.3 %collective-permute-start.11 = (bf16[256,2048]{1,0:T(8,128)(2,1)S(1)}, bf16[256,2048]{1,0:T(8,128)(2,1)S(1)}, u32[]{:S(2)}, u32[]{:S(2)}) collective-permute-start(bf16[256,2048]{1,0:T(8,128)(2,1)S(1)} %join.1.refs_0_), channel_id=1, source_target_pairs={{0,6},{1,7},{2,0},{3,1},{4,2},{5,3},{6,4},{7,5},{8,14},{9,15},{10,... | collective-permute-start | bytes 3145736 | tf_op jit(solution)/shard_map/ppermute | solution.py:43
  54.4 15.6 %collective-permute-done.10.refs_0_ = bf16[256,2048]{1,0:T(8,128)(2,1)S(1)} collective-permute-done((bf16[256,2048]{1,0:T(8,128)(2,1)S(1)}, bf16[256,2048]{1,0:T(8,128)(2,1)S(1)}, u32[]{:S(2)}, u32[]{:S(2)}) %collective-permute-start.10) | collective-permute-done | bytes 1048608 | tf_op jit(solution)/shard_map/ppermute | solution.py:43
  70.0 7.0 %collective-permute-start.20 = (bf16[256,2048]{1,0:T(8,128)(2,1)S(1)}, bf16[256,2048]{1,0:T(8,128)(2,1)S(1)}, u32[]{:S(2)}, u32[]{:S(2)}) collective-permute-start(bf16[256,2048]{1,0:T(8,128)(2,1)S(1)} %collective-permute-done.10.refs_0_), channel_id=1, source_target_pairs={{0,6},{1,7},{2,0},{3,1},{4,2},{5,3},{6,4},{7,5},{8,14},{9,15},{10,... | collective-permute-start | bytes 3145736 | tf_op jit(solution)/shard_map/ppermute | solution.py:43
  80.0 18.1 %collective-permute-done.20.refs_0_ = bf16[256,2048]{1,0:T(8,128)(2,1)S(1)} collective-permute-done((bf16[256,2048]{1,0:T(8,128)(2,1)S(1)}, bf16[256,2048]{1,0:T(8,128)(2,1)S(1)}, u32[]{:S(2)}, u32[]{:S(2)}) %collective-permute-start.20) | collective-permute-done | bytes 1048608 | tf_op jit(solution)/shard_map/ppermute | solution.py:43
  103.9 5.4 %collective-permute-done.29.refs_0_ = bf16[128,2048]{1,0:T(8,128)(2,1)S(1)} collective-permute-done((bf16[128,2048]{1,0:T(8,128)(2,1)S(1)}, bf16[128,2048]{1,0:T(8,128)(2,1)S(1)}, u32[]{:S(2)}, u32[]{:S(2)}) %collective-permute-start.29) | collective-permute-done | bytes 524320 | tf_op jit(solution)/shard_map/ppermute | solution.py:43
  112.4 8.1 %collective-permute-done.31.refs_2_ = bf16[128,2048]{1,0:T(8,128)(2,1)S(1)} collective-permute-done((bf16[128,2048]{1,0:T(8,128)(2,1)S(1)}, bf16[128,2048]{1,0:T(8,128)(2,1)S(1)}, u32[]{:S(2)}, u32[]{:S(2)}) %collective-permute-start.31) | collective-permute-done | bytes 524320 | tf_op jit(solution)/shard_map/ppermute | solution.py:43
  123.7 8.2 %product.7 = (f32[128,1024]{1,0:T(8,128)}, f32[128,1024]{1,0:T(8,128)}, f32[128,1024]{1,0:T(8,128)S(1)}, f32[128,1024]{1,0:T(8,128)S(1)}, bf16[128,2048]{1,0:T(8,128)(2,1)S(1)}, /*index=5*/bf16[128,2048]{1,0:T(8,128)(2,1)S(1)}) custom-call(bf16[128,2048]{1,0:T(8,128)(2,1)S(1)} %collective-permute-done.29.refs_0_, ...), custom_call_target="tpu_custom_call" | custom-call | flops 4294967296 | bytes 15728640 | tf_op jit(solution)/shard_map/product/pallas_call | solution.py:195
  133.4 8.1 %product.6 = (f32[128,1024]{1,0:T(8,128)}, f32[128,1024]{1,0:T(8,128)}, f32[128,1024]{1,0:T(8,128)S(1)}, f32[128,1024]{1,0:T(8,128)S(1)}, bf16[128,2048]{1,0:T(8,128)(2,1)S(1)}, /*index=5*/bf16[128,2048]{1,0:T(8,128)(2,1)S(1)}) custom-call(bf16[256,2048]{1,0:T(8,128)(2,1)S(1)} %collective-permute-done.20.refs_0_, ...), custom_call_target="tpu_custom_call" | custom-call | flops 4294967296 | bytes 15728640 | tf_op jit(solution)/shard_map/product/pallas_call | solution.py:195
  143.0 10.4 %product.5 = (f32[192,1024]{1,0:T(8,128)}, f32[192,1024]{1,0:T(8,128)}, f32[192,1024]{1,0:T(8,128)S(1)}, f32[192,1024]{1,0:T(8,128)S(1)}, bf16[192,2048]{1,0:T(8,128)(2,1)S(1)}, /*index=5*/bf16[192,2048]{1,0:T(8,128)(2,1)S(1)}) custom-call(bf16[256,2048]{1,0:T(8,128)(2,1)S(1)} %collective-permute-done.10.refs_0_, ...), custom_call_target="tpu_custom_call" | custom-call | flops 6442450944 | bytes 18874368 | tf_op jit(solution)/shard_map/product/pallas_call | solution.py:195
  156.2 6.5 %product.4 = (f32[64,1024]{1,0:T(8,128)}, f32[64,1024]{1,0:T(8,128)}, f32[64,1024]{1,0:T(8,128)S(1)}, f32[64,1024]{1,0:T(8,128)S(1)}, bf16[64,2048]{1,0:T(8,128)(2,1)}, /*index=5*/bf16[64,2048]{1,0:T(8,128)(2,1)S(1)}) custom-call(bf16[256,2048]{1,0:T(8,128)(2,1)S(1)} %join.1.refs_0_, bf16[2048,1024]{1,0:T(8,128)(2,1)S(1)} %hold.1.refs_1_.refs_3_.refs_2_.refs_4_, ...), custom_call_target="tpu_custom_call" | custom-call | flops 2147483648 | bytes 12582912 | tf_op jit(solution)/shard_map/product/pallas_call | solution.py:195
  171.5 7.9 %collective-permute-done.13.refs_8_.refs_2_ = bf16[192,2048]{1,0:T(8,128)(2,1)S(1)} collective-permute-done((bf16[192,2048]{1,0:T(8,128)(2,1)S(1)}, bf16[192,2048]{1,0:T(8,128)(2,1)S(1)}, u32[]{:S(2)}, u32[]{:S(2)}) %collective-permute-start.13) | collective-permute-done | bytes 786464 | tf_op jit(solution)/shard_map/ppermute | solution.py:43
  186.8 7.9 %collective-permute-done.25.refs_11_ = bf16[128,1024]{1,0:T(8,128)(2,1)} collective-permute-done((bf16[128,1024]{1,0:T(8,128)(2,1)}, bf16[128,1024]{1,0:T(8,128)(2,1)}, u32[]{:S(2)}, u32[]{:S(2)}) %collective-permute-start.25) | collective-permute-done | bytes 262176 | tf_op jit(solution)/shard_map/ppermute | solution.py:43
  198.7 7.9 %collective-permute-start.38 = (f32[64,1024]{1,0:T(8,128)S(1)}, f32[64,1024]{1,0:T(8,128)S(1)}, u32[]{:S(2)}, u32[]{:S(2)}) collective-permute-start(f32[64,1024]{1,0:T(8,128)S(1)} %get-tuple-element.96), channel_id=1, source_target_pairs={{0,1},{1,0},{2,3},{3,2},{4,5},{5,4},{6,7},{7,6},{8,9},{9,8},{10,11... | collective-permute-start | bytes 786440 | tf_op jit(solution)/shard_map/ppermute | solution.py:43
  231.5 4.3 %index.1 = (s32[512]{0:T(512)S(1)}, s32[512]{0:T(512)S(1)}, s32[64]{0:T(128)S(1)}) custom-call(s32[2]{0:T(128)S(1)} %pad_add_fusion.place, s32[512]{0:T(512)S(1)} %reshape.9.slots, s32[512]{0:T(512)S(1)} %reshape.10.mask), custom_call_target="tpu_custom_call" | custom-call | bytes 8192 | tf_op jit(solution)/shard_map/index/pallas_call | solution.py:312
  247.6 4.0 %outgoing.1 = (f32[512,1024]{1,0:T(8,128)}, bf16[128,32,128]{2,1,0:T(8,128)(2,1)}) custom-call(s32[512]{0:T(512)S(1)} %get-tuple-element.55.code, f32[64,1024]{1,0:T(8,128)S(1)} %copy-done.10, bf16[64,1024]{1,0:T(8,128)(2,1)S(1)} %copy-done.18, f32[64,1024]{1,0:T(8,128)S(1)} %copy-done.14, bf16[64,1024]{1,0:T(8,128)(2,1)S(1)} %copy-done.20, ...), custom_call_target="tpu_custom_call" | custom-call | bytes 6291456 | tf_op jit(solution)/shard_map/outgoing/pallas_call | solution.py:375
  251.6 5.8 %all-to-all-start = ((bf16[128,32,128]{2,1,0:T(8,128)(2,1)}), bf16[128,32,128]{2,1,0:T(8,128)(2,1)S(1)}, u32[]{:S(2)}, u32[]{:S(2)}) async-start(bf16[128,32,128]{2,1,0:T(8,128)(2,1)} %get-tuple-element.98), calls=%async_computation | async-start | bytes 2097152 | tf_op jit(solution)/shard_map/all_to_all | solution.py:534
  265.1 11.2 %all-to-all-done = bf16[128,32,128]{2,1,0:T(8,128)(2,1)S(1)} async-done(((bf16[128,32,128]{2,1,0:T(8,128)(2,1)}), bf16[128,32,128]{2,1,0:T(8,128)(2,1)S(1)}, u32[]{:S(2)}, u32[]{:S(2)}) %all-to-all-start) | async-done | bytes 1048608 | tf_op jit(solution)/shard_map/all_to_all | solution.py:534
  276.3 3.8 %update.1 = f32[512,1024]{1,0:T(8,128)} custom-call(s32[512]{0:T(512)S(1)} %get-tuple-element.54.inverse, bf16[4096,128]{1,0:T(8,128)(2,1)S(1)} %bitcast.18, f32[512,1024]{1,0:T(8,128)} %copy-done.3, f32[512,1024]{1,0:T(8,128)} %copy-done.4), custom_call_target="tpu_custom_call" | custom-call | bytes 7340032 | tf_op jit(solution)/shard_map/update/pallas_call | solution.py:460
  (161 shorter events, 93.9 us)
Async XLA Ops:
  0.0 123.7 %collective-permute-start.5 = (bf16[2048,1024]{1,0:T(8,128)(2,1)}, bf16[2048,1024]{1,0:T(8,128)(2,1)}, u32[]{:S(2)}, u32[]{:S(2)}) collective-permute-start(bf16[2048,1024]{1,0:T(8,128)(2,1)} %source.1), channel_id=1, source_target_pairs={{0,1},{1,0},{2,3},{3,2},{4,5},{5,4},{6,7},{7,6},{8,9},{9,8},{10,11... | collective-permute-start | bytes 12582920 | tf_op jit(solution)/shard_map/ppermute | solution.py:43
  9.2 19.9 %collective-permute-start.1 = (bf16[64,2048]{1,0:T(8,128)(2,1)S(1)}, bf16[64,2048]{1,0:T(8,128)(2,1)S(1)}, u32[]{:S(2)}, u32[]{:S(2)}) collective-permute-start(bf16[64,2048]{1,0:T(8,128)(2,1)S(1)} %get-tuple-element.58), channel_id=1, source_target_pairs={{0,0},{1,1},{2,16},{3,17},{4,38},{5,39},{6,54},{7,55},{8,68},{9,69... | collective-permute-start | bytes 786440 | tf_op jit(solution)/shard_map/ppermute | solution.py:43
  9.9 19.2 %collective-permute-start.2 = (bf16[64,2048]{1,0:T(8,128)(2,1)S(1)}, bf16[64,2048]{1,0:T(8,128)(2,1)S(1)}, u32[]{:S(2)}, u32[]{:S(2)}) collective-permute-start(bf16[64,2048]{1,0:T(8,128)(2,1)S(1)} %get-tuple-element.59), channel_id=1, source_target_pairs={{0,2},{1,3},{2,18},{3,19},{4,32},{5,33},{6,48},{7,49},{8,70},{9,71... | collective-permute-start | bytes 786440 | tf_op jit(solution)/shard_map/ppermute | solution.py:43
  39.6 30.4 %collective-permute-start.10 = (bf16[256,2048]{1,0:T(8,128)(2,1)S(1)}, bf16[256,2048]{1,0:T(8,128)(2,1)S(1)}, u32[]{:S(2)}, u32[]{:S(2)}) collective-permute-start(bf16[256,2048]{1,0:T(8,128)(2,1)S(1)} %join.1.refs_0_), channel_id=1, source_target_pairs={{0,8},{1,9},{2,10},{3,11},{4,12},{5,13},{6,14},{7,15},{8,0},{9,1},... | collective-permute-start | bytes 3145736 | tf_op jit(solution)/shard_map/ppermute | solution.py:43
  48.1 29.0 %collective-permute-start.11 = (bf16[256,2048]{1,0:T(8,128)(2,1)S(1)}, bf16[256,2048]{1,0:T(8,128)(2,1)S(1)}, u32[]{:S(2)}, u32[]{:S(2)}) collective-permute-start(bf16[256,2048]{1,0:T(8,128)(2,1)S(1)} %join.1.refs_0_), channel_id=1, source_target_pairs={{0,6},{1,7},{2,0},{3,1},{4,2},{5,3},{6,4},{7,5},{8,14},{9,15},{10,... | collective-permute-start | bytes 3145736 | tf_op jit(solution)/shard_map/ppermute | solution.py:43
  54.4 25.5 %collective-permute-start.12 = (bf16[256,2048]{1,0:T(8,128)(2,1)S(1)}, bf16[256,2048]{1,0:T(8,128)(2,1)S(1)}, u32[]{:S(2)}, u32[]{:S(2)}) collective-permute-start(bf16[256,2048]{1,0:T(8,128)(2,1)S(1)} %join.1.refs_0_), channel_id=1, source_target_pairs={{0,2},{1,3},{2,4},{3,5},{4,6},{5,7},{6,0},{7,1},{8,10},{9,11},{10,... | collective-permute-start | bytes 3145736 | tf_op jit(solution)/shard_map/ppermute | solution.py:43
  70.0 28.1 %collective-permute-start.20 = (bf16[256,2048]{1,0:T(8,128)(2,1)S(1)}, bf16[256,2048]{1,0:T(8,128)(2,1)S(1)}, u32[]{:S(2)}, u32[]{:S(2)}) collective-permute-start(bf16[256,2048]{1,0:T(8,128)(2,1)S(1)} %collective-permute-done.10.refs_0_), channel_id=1, source_target_pairs={{0,6},{1,7},{2,0},{3,1},{4,2},{5,3},{6,4},{7,5},{8,14},{9,15},{10,... | collective-permute-start | bytes 3145736 | tf_op jit(solution)/shard_map/ppermute | solution.py:43
  77.0 24.6 %collective-permute-start.21 = (bf16[256,2048]{1,0:T(8,128)(2,1)S(1)}, bf16[256,2048]{1,0:T(8,128)(2,1)S(1)}, u32[]{:S(2)}, u32[]{:S(2)}) collective-permute-start(bf16[256,2048]{1,0:T(8,128)(2,1)S(1)} %collective-permute-done.10.refs_0_), channel_id=1, source_target_pairs={{0,2},{1,3},{2,4},{3,5},{4,6},{5,7},{6,0},{7,1},{8,10},{9,11},{10,... | collective-permute-start | bytes 3145736 | tf_op jit(solution)/shard_map/ppermute | solution.py:43
  77.1 32.2 %collective-permute-start.29 = (bf16[128,2048]{1,0:T(8,128)(2,1)S(1)}, bf16[128,2048]{1,0:T(8,128)(2,1)S(1)}, u32[]{:S(2)}, u32[]{:S(2)}) collective-permute-start(bf16[128,2048]{1,0:T(8,128)(2,1)S(1)} %slice.54), channel_id=1, source_target_pairs={{0,6},{1,7},{2,0},{3,1},{4,2},{5,3},{6,4},{7,5},{8,14},{9,15},{10,... | collective-permute-start | bytes 1572872 | tf_op jit(solution)/shard_map/ppermute | solution.py:43
  79.9 32.6 %collective-permute-start.30 = (bf16[128,2048]{1,0:T(8,128)(2,1)S(1)}, bf16[128,2048]{1,0:T(8,128)(2,1)S(1)}, u32[]{:S(2)}, u32[]{:S(2)}) collective-permute-start(bf16[128,2048]{1,0:T(8,128)(2,1)S(1)} %slice.55), channel_id=1, source_target_pairs={{0,2},{1,3},{2,4},{3,5},{4,6},{5,7},{6,0},{7,1},{8,10},{9,11},{10,... | collective-permute-start | bytes 1572872 | tf_op jit(solution)/shard_map/ppermute | solution.py:43
  98.1 22.4 %collective-permute-start.31 = (bf16[128,2048]{1,0:T(8,128)(2,1)S(1)}, bf16[128,2048]{1,0:T(8,128)(2,1)S(1)}, u32[]{:S(2)}, u32[]{:S(2)}) collective-permute-start(bf16[128,2048]{1,0:T(8,128)(2,1)S(1)} %slice.56), channel_id=1, source_target_pairs={{0,6},{1,7},{2,0},{3,1},{4,2},{5,3},{6,4},{7,5},{8,14},{9,15},{10,... | collective-permute-start | bytes 1572872 | tf_op jit(solution)/shard_map/ppermute | solution.py:43
  101.7 22.0 %collective-permute-start.32 = (bf16[128,2048]{1,0:T(8,128)(2,1)S(1)}, bf16[128,2048]{1,0:T(8,128)(2,1)S(1)}, u32[]{:S(2)}, u32[]{:S(2)}) collective-permute-start(bf16[128,2048]{1,0:T(8,128)(2,1)S(1)} %slice.57), channel_id=1, source_target_pairs={{0,2},{1,3},{2,4},{3,5},{4,6},{5,7},{6,0},{7,1},{8,10},{9,11},{10,... | collective-permute-start | bytes 1572872 | tf_op jit(solution)/shard_map/ppermute | solution.py:43
  131.8 30.9 %collective-permute-start.34 = (bf16[128,2048]{1,0:T(8,128)(2,1)S(1)}, bf16[128,2048]{1,0:T(8,128)(2,1)S(1)}, u32[]{:S(2)}, u32[]{:S(2)}) collective-permute-start(bf16[128,2048]{1,0:T(8,128)(2,1)S(1)} %get-tuple-element.91), channel_id=1, source_target_pairs={{0,96},{1,97},{2,98},{3,99},{4,100},{5,101},{6,102},{7,103},{8,104... | collective-permute-start | bytes 1572872 | tf_op jit(solution)/shard_map/ppermute | solution.py:43
  131.9 31.0 %collective-permute-start.33 = (bf16[128,2048]{1,0:T(8,128)(2,1)S(1)}, bf16[128,2048]{1,0:T(8,128)(2,1)S(1)}, u32[]{:S(2)}, u32[]{:S(2)}) collective-permute-start(bf16[128,2048]{1,0:T(8,128)(2,1)S(1)} %get-tuple-element.90), channel_id=1, source_target_pairs={{0,32},{1,33},{2,34},{3,35},{4,36},{5,37},{6,38},{7,39},{8,40},{9,... | collective-permute-start | bytes 1572872 | tf_op jit(solution)/shard_map/ppermute | solution.py:43
  141.5 24.2 %collective-permute-start.23 = (bf16[128,2048]{1,0:T(8,128)(2,1)S(1)}, bf16[128,2048]{1,0:T(8,128)(2,1)S(1)}, u32[]{:S(2)}, u32[]{:S(2)}) collective-permute-start(bf16[128,2048]{1,0:T(8,128)(2,1)S(1)} %get-tuple-element.81), channel_id=1, source_target_pairs={{0,96},{1,97},{2,98},{3,99},{4,100},{5,101},{6,102},{7,103},{8,104... | collective-permute-start | bytes 1572872 | tf_op jit(solution)/shard_map/ppermute | solution.py:43
  142.9 37.5 %collective-permute-start.22 = (bf16[128,2048]{1,0:T(8,128)(2,1)S(1)}, bf16[128,2048]{1,0:T(8,128)(2,1)S(1)}, u32[]{:S(2)}, u32[]{:S(2)}) collective-permute-start(bf16[128,2048]{1,0:T(8,128)(2,1)S(1)} %get-tuple-element.80), channel_id=1, source_target_pairs={{0,32},{1,33},{2,34},{3,35},{4,36},{5,37},{6,38},{7,39},{8,40},{9,... | collective-permute-start | bytes 1572872 | tf_op jit(solution)/shard_map/ppermute | solution.py:43
  162.9 19.7 %collective-permute-start.7 = (bf16[64,2048]{1,0:T(8,128)(2,1)S(1)}, bf16[64,2048]{1,0:T(8,128)(2,1)S(1)}, u32[]{:S(2)}, u32[]{:S(2)}) collective-permute-start(bf16[64,2048]{1,0:T(8,128)(2,1)S(1)} %get-tuple-element.65), channel_id=1, source_target_pairs={{0,96},{1,97},{2,98},{3,99},{4,100},{5,101},{6,102},{7,103},{8,104... | collective-permute-start | bytes 786440 | tf_op jit(solution)/shard_map/ppermute | solution.py:43
  179.4 27.2 %collective-permute-start.16 = (bf16[192,1024]{1,0:T(8,128)(2,1)}, bf16[192,1024]{1,0:T(8,128)(2,1)S(1)}, u32[]{:S(2)}, u32[]{:S(2)}) collective-permute-start(bf16[192,1024]{1,0:T(8,128)(2,1)} %add_convert_fusion), channel_id=1, source_target_pairs={{0,96},{1,97},{2,98},{3,99},{4,100},{5,101},{6,102},{7,103},{8,104... | collective-permute-start | bytes 1179656 | tf_op jit(solution)/shard_map/ppermute | solution.py:43
  180.4 26.2 %collective-permute-start.15 = (bf16[192,1024]{1,0:T(8,128)(2,1)}, bf16[192,1024]{1,0:T(8,128)(2,1)S(1)}, u32[]{:S(2)}, u32[]{:S(2)}) collective-permute-start(bf16[192,1024]{1,0:T(8,128)(2,1)} %add_convert_fusion.1), channel_id=1, source_target_pairs={{0,32},{1,33},{2,34},{3,35},{4,36},{5,37},{6,38},{7,39},{8,40},{9,... | collective-permute-start | bytes 1179656 | tf_op jit(solution)/shard_map/ppermute | solution.py:43
  185.1 26.0 %collective-permute-start.6 = (bf16[64,2048]{1,0:T(8,128)(2,1)}, bf16[64,2048]{1,0:T(8,128)(2,1)}, u32[]{:S(2)}, u32[]{:S(2)}) collective-permute-start(bf16[64,2048]{1,0:T(8,128)(2,1)} %get-tuple-element.64), channel_id=1, source_target_pairs={{0,32},{1,33},{2,34},{3,35},{4,36},{5,37},{6,38},{7,39},{8,40},{9,... | collective-permute-start | bytes 786440 | tf_op jit(solution)/shard_map/ppermute | solution.py:43
  198.7 25.9 %collective-permute-start.38 = (f32[64,1024]{1,0:T(8,128)S(1)}, f32[64,1024]{1,0:T(8,128)S(1)}, u32[]{:S(2)}, u32[]{:S(2)}) collective-permute-start(f32[64,1024]{1,0:T(8,128)S(1)} %get-tuple-element.96), channel_id=1, source_target_pairs={{0,1},{1,0},{2,3},{3,2},{4,5},{5,4},{6,7},{7,6},{8,9},{9,8},{10,11... | collective-permute-start | bytes 786440 | tf_op jit(solution)/shard_map/ppermute | solution.py:43
  211.0 29.1 %collective-permute-start.27 = (f32[128,1024]{1,0:T(8,128)}, f32[128,1024]{1,0:T(8,128)S(1)}, u32[]{:S(2)}, u32[]{:S(2)}) collective-permute-start(f32[128,1024]{1,0:T(8,128)} %get-tuple-element.86), channel_id=1, source_target_pairs={{0,1},{1,0},{2,3},{3,2},{4,5},{5,4},{6,7},{7,6},{8,9},{9,8},{10,11... | collective-permute-start | bytes 1572872 | tf_op jit(solution)/shard_map/ppermute | solution.py:43
  217.9 20.1 %collective-permute-start.26 = (bf16[128,1024]{1,0:T(8,128)(2,1)}, bf16[128,1024]{1,0:T(8,128)(2,1)S(1)}, u32[]{:S(2)}, u32[]{:S(2)}) collective-permute-start(bf16[128,1024]{1,0:T(8,128)(2,1)} %get-tuple-element.85), channel_id=1, source_target_pairs={{0,16},{1,17},{2,18},{3,19},{4,20},{5,21},{6,22},{7,23},{8,24},{9,... | collective-permute-start | bytes 786440 | tf_op jit(solution)/shard_map/ppermute | solution.py:43
  251.6 24.8 %all-to-all-start = ((bf16[128,32,128]{2,1,0:T(8,128)(2,1)}), bf16[128,32,128]{2,1,0:T(8,128)(2,1)S(1)}, u32[]{:S(2)}, u32[]{:S(2)}) async-start(bf16[128,32,128]{2,1,0:T(8,128)(2,1)} %get-tuple-element.98), calls=%async_computation | async-start | bytes 2097152 | tf_op jit(solution)/shard_map/all_to_all | solution.py:534
  (51 other events, 352.1 us)

commit v5 on v3

--- a/solution.py
+++ b/solution.py
@@ -102,41 +102,51 @@
 
 def join_kernel(where, *refs):
     out = refs[-1]
-    for a in range(4):
-        out[pl.ds(pl.multiple_of(where[a] * 64, 64), 64), :] = refs[a][...]
+    for k in range(2):
+        out[pl.ds(pl.multiple_of(where[k] * 64, 64), 64), :] = refs[k][...]
 
 
 def join(where, pieces):
     return pl.pallas_call(
         join_kernel,
-        out_shape=jax.ShapeDtypeStruct((256, 2048), BF),
-        in_specs=[SMEM] + [VMEM] * 4,
+        out_shape=jax.ShapeDtypeStruct((128, 2048), BF),
+        in_specs=[SMEM] + [VMEM] * 2,
         out_specs=VMEM,
-        compiler_params=params(6),
-        cost_estimate=cost(0, 2 << 20),
+        compiler_params=params(3),
+        cost_estimate=cost(0, 1 << 20),
         name="join",
     )(where, *pieces)
 
 
-def product_kernel(counts, *refs):
-    n_in = sum(counts)
-    n = len(counts)
+def product_kernel(steps, odd, *refs):
+    n = len(steps)
+    n_in = 2 * n
     blocks = refs[:n_in]
     own, oth = refs[n_in : n_in + 2]
     zero_a, zero_b, one_a, three_b, up, down = refs[n_in + 2 : n_in + 8]
-    held, keep_a, keep_b, sems = refs[n_in + 8 :]
-    at = 0
-    for ref in blocks:
-        rows = ref.shape[0]
-        held[at : at + rows, :] = ref[...]
-        at += rows
+    held, keep_a, keep_b, panel, sems = refs[n_in + 8 :]
+
+    def load(source, k, j):
+        cols = pl.ds(pl.multiple_of(j * 512, 512), 512)
+        return pltpu.make_async_copy(source.at[:, cols], panel.at[2 * k + j], sems.at[2 * k + j])
+
+    for k in range(2):
+        for j in range(2):
+            load((own, oth)[k], k, j).start()
+    for i in range(n):
+        for h in range(2):
+            offset = lax.bitwise_and(odd[0] + steps[i] + h, 1)
+            for k in range(2):
+                at = pl.multiple_of(i * 256 + k * 128 + offset * 64, 64)
+                held[pl.ds(at, 64), :] = blocks[2 * i + h][k * 64 : k * 64 + 64, :]
 
     def rows_of(r, i, k):
         return r[i * 256 + k * 64 : i * 256 + k * 64 + 64]
 
     def first(j, carry):
         cols = pl.ds(pl.multiple_of(j * 512, 512), 512)
-        r = jnp.dot(held[...], own[:, cols], preferred_element_type=F32)
+        load(own, 0, j).wait()
+        r = jnp.dot(held[...], panel[j], preferred_element_type=F32)
         for i in range(n):
             at = slice(i * 64, i * 64 + 64)
             keep_a[at, cols] = rows_of(r, i, 0)
@@ -148,7 +158,8 @@
     def second(j, carry):
         cols = pl.ds(pl.multiple_of(j * 512, 512), 512)
         wide = pl.ds(pl.multiple_of(j * 512 + 1024, 512), 512)
-        r = jnp.dot(held[...], oth[:, cols], preferred_element_type=F32)
+        load(oth, 1, j).wait()
+        r = jnp.dot(held[...], panel[2 + j], preferred_element_type=F32)
         for i in range(n):
             at = slice(i * 64, i * 64 + 64)
             keep_b[at, cols] = rows_of(r, i, 0)
@@ -158,36 +169,35 @@
         return carry
 
     lax.fori_loop(0, 2, first, 0)
-    copy_a = pltpu.make_async_copy(keep_a, zero_a, sems.at[0])
+    copy_a = pltpu.make_async_copy(keep_a, zero_a, sems.at[4])
     copy_a.start()
     lax.fori_loop(0, 2, second, 0)
-    copy_b = pltpu.make_async_copy(keep_b, zero_b, sems.at[1])
+    copy_b = pltpu.make_async_copy(keep_b, zero_b, sems.at[5])
     copy_b.start()
     copy_a.wait()
     copy_b.wait()
 
 
-def product(groups, own, oth):
-    flat = [a for g in groups for a in g]
-    counts = tuple(len(g) for g in groups)
-    n = len(groups)
+def product(odd, steps, halves, own, oth):
+    n = len(steps)
     half = jax.ShapeDtypeStruct((n * 64, 1024), F32)
     full = jax.ShapeDtypeStruct((n * 64, 2048), BF)
     return pl.pallas_call(
-        functools.partial(product_kernel, counts),
+        functools.partial(product_kernel, steps),
         out_shape=[pltpu.HBM(half.shape, F32)] * 2 + [half] * 2 + [full] * 2,
-        in_specs=[VMEM] * (len(flat) + 2),
+        in_specs=[SMEM] + [VMEM] * (2 * n) + [ANY] * 2,
         out_specs=[HBM] * 2 + [VMEM] * 4,
         scratch_shapes=[
             pltpu.VMEM((n * 256, 2048), BF),
             pltpu.VMEM((n * 64, 1024), F32),
             pltpu.VMEM((n * 64, 1024), F32),
-            pltpu.SemaphoreType.DMA((2,)),
+            pltpu.VMEM((4, 2048, 512), BF),
+            pltpu.SemaphoreType.DMA((6,)),
         ],
         compiler_params=params(28),
         cost_estimate=cost(2 * n * 256 * 2048 * 2048, (9 << 20) + n * (3 << 20)),
         name="product",
-    )(*flat, own, oth)
+    )(odd, *halves, *off_chip(own, oth))
 
 
 def collect_kernel(n_groups, members, low, *refs):
@@ -477,21 +487,28 @@
     moved = [send(pieces[a], spread(a)) for a in range(4)]
     own = integrals
     oth = send(integrals, shift(dc=1))
-    block = {}
-    block[0, 0] = join(jnp.stack([(x - a) & 3 for a in range(4)]), moved)
-
-    block[1, 0] = send(block[0, 0], shift(dx=-1))
-    block[3, 0] = send(block[0, 0], shift(dx=1))
-    block[0, 1] = send(block[0, 0], shift(dzh=1))
-    block[1, 1] = send(block[0, 1], shift(dx=-1))
-    block[3, 1] = send(block[0, 1], shift(dx=1))
-    parts = {k: (b,) for k, b in block.items()}
+    half = {}
+    for h in range(2):
+        where = jnp.stack([((x - a) & 3) >> 1 for a in (h, h + 2)])
+        half[0, 0, h] = join(where, [moved[h], moved[h + 2]])
+
+    for h in range(2):
+        half[1, 0, h] = send(half[0, 0, h], shift(dx=-1))
+        half[3, 0, h] = send(half[0, 0, h], shift(dx=1))
+        half[0, 1, h] = send(half[0, 0, h], shift(dzh=1))
+        half[1, 1, h] = send(half[0, 1, h], shift(dx=-1))
+        half[3, 1, h] = send(half[0, 1, h], shift(dx=1))
     for j in range(2):
-        parts[2, j] = (send(block[1, j][:128], shift(dx=-1)), send(block[3, j][128:], shift(dx=1)))
-
+        half[2, j, 0] = send(half[1, j, 0], shift(dx=-1))
+        half[2, j, 1] = send(half[3, j, 1], shift(dx=1))
+
+    odd = (x & 1)[None]
     sums = []
     for group in GROUPS:
-        za, zb, one_a, three_b, up, down = product([parts[k] for k in group], own, oth)
+        halves = [half[i, j, h] for i, j in group for h in range(2)]
+        za, zb, one_a, three_b, up, down = product(
+            odd, tuple(i for i, j in group), halves, own, oth
+        )
         up = send(up, shift(dy=1))
         down = send(down, shift(dy=-1))
         nup = (one_a + up[:, :1024].astype(F32)).astype(BF)

time: 281 us -> 293 us (1.043)
  waiting for transfers between devices: 110 us -> 118 us
  local copies, waits for them, and re-layouts: 20.4 us -> 24.5 us
    ppermute x40 -> x45, waiting for transfers between devices: 99.3 us -> 107 us  [send(): return lax.ppermute(value, AXES, pairs)]
    unnamed x72 -> x86, local copies, waits for them, and re-layouts: 19.9 us -> 24.1 us
    ppermute x40 -> x45, starting transfers between devices: 81.4 us -> 80 us  [send(): return lax.ppermute(value, AXES, pairs)]
    pallas_call x5 -> x6, Pallas kernels: 33.9 us -> 34.2 us  [the longest x4 33 us: product(): pl.pallas_call(functools.partial(product_kernel, steps), out_shape=[pltpu...]
  transfers between devices with their start and end apart: 41 -> 46, of which waited for: 18 -> 19; matrix products, arithmetic and copies ran while one was open for 2% -> 2% of each run, Pallas kernels for 15% -> 17%
where the time goes in v5:
time: 293 us
  waiting for transfers between devices  118 us (40%)
  starting transfers between devices  87.4 us (30%)
  Pallas kernels  57.3 us (20%)
  local copies, waits for them, and re-layouts  24.5 us (8%)
  other arithmetic  4.74 us (2%)
    ppermute x45, waiting for transfers between devices, send(): return lax.ppermute(value, AXES, pairs)  107 us
    ppermute x45, starting transfers between devices, send(): return lax.ppermute(value, AXES, pairs)  80 us
    pallas_call x4, Pallas kernels, product(): pl.pallas_call(functools.partial(product_kernel, steps), out_shape=[pltpu...  33 us
    unnamed x86, local copies, waits for them, and re-layouts  24.1 us
    all_to_all x1, waiting for transfers between devices, compute(): lax.all_to_all(out, AXES, split_axis=0, concat_axis=0, tiled=True)  11.2 us
    all_to_all x1, starting transfers between devices, compute(): lax.all_to_all(out, AXES, split_axis=0, concat_axis=0, tiled=True)  7.43 us
    pallas_call x3, Pallas kernels, collect(): pl.pallas_call(functools.partial(collect_kernel, len(groups), members), o...  6.9 us
  transfers between devices with their start and end apart: 46, of which 19 were waited for; matrix products, arithmetic and copies ran while one was open for 2% of the time, Pallas kernels for 17%

profile of v5, /device:TPU:1, one launch (start us, length us, event | category | flops | bytes accessed | tf_op | source)
XLA Modules:
  0.0 292.7 jit_solution(2919219131920124836)
XLA Ops:
  3.8 5.3 %collective-permute-done.got = bf16[256,1024]{1,0:T(8,128)(2,1)S(1)} collective-permute-done((bf16[256,1024]{1,0:T(8,128)(2,1)S(1)}, bf16[256,1024]{1,0:T(8,128)(2,1)S(1)}, u32[]{:S(2)}, u32[]{:S(2)}) %collective-permute-start) | collective-permute-done | bytes 524320 | tf_op jit(solution)/shard_map/ppermute | solution.py:43
  9.9 7.9 %collective-permute-start.2 = (bf16[64,2048]{1,0:T(8,128)(2,1)S(1)}, bf16[64,2048]{1,0:T(8,128)(2,1)S(1)}, u32[]{:S(2)}, u32[]{:S(2)}) collective-permute-start(bf16[64,2048]{1,0:T(8,128)(2,1)S(1)} %get-tuple-element.59), channel_id=1, source_target_pairs={{0,4},{1,5},{2,20},{3,21},{4,34},{5,35},{6,50},{7,51},{8,64},{9,65... | collective-permute-start | bytes 786440 | tf_op jit(solution)/shard_map/ppermute | solution.py:43
  17.9 12.3 %collective-permute-done.2.refs_1_ = bf16[64,2048]{1,0:T(8,128)(2,1)S(1)} collective-permute-done((bf16[64,2048]{1,0:T(8,128)(2,1)S(1)}, bf16[64,2048]{1,0:T(8,128)(2,1)S(1)}, u32[]{:S(2)}, u32[]{:S(2)}) %collective-permute-start.2) | collective-permute-done | bytes 262176 | tf_op jit(solution)/shard_map/ppermute | solution.py:43
  30.8 6.3 %collective-permute-start.10 = (bf16[128,2048]{1,0:T(8,128)(2,1)S(1)}, bf16[128,2048]{1,0:T(8,128)(2,1)S(1)}, u32[]{:S(2)}, u32[]{:S(2)}) collective-permute-start(bf16[128,2048]{1,0:T(8,128)(2,1)S(1)} %join.2.refs_0_), channel_id=1, source_target_pairs={{0,8},{1,9},{2,10},{3,11},{4,12},{5,13},{6,14},{7,15},{8,0},{9,1},... | collective-permute-start | bytes 1572872 | tf_op jit(solution)/shard_map/ppermute | solution.py:43
  39.0 8.0 %collective-permute-start.4 = (bf16[64,2048]{1,0:T(8,128)(2,1)S(1)}, bf16[64,2048]{1,0:T(8,128)(2,1)S(1)}, u32[]{:S(2)}, u32[]{:S(2)}) collective-permute-start(bf16[64,2048]{1,0:T(8,128)(2,1)S(1)} %get-tuple-element.61), channel_id=1, source_target_pairs={{0,6},{1,7},{2,22},{3,23},{4,36},{5,37},{6,52},{7,53},{8,66},{9,67... | collective-permute-start | bytes 786440 | tf_op jit(solution)/shard_map/ppermute | solution.py:43
  47.1 5.9 %collective-permute-done.3.refs_0_ = bf16[64,2048]{1,0:T(8,128)(2,1)S(1)} collective-permute-done((bf16[64,2048]{1,0:T(8,128)(2,1)S(1)}, bf16[64,2048]{1,0:T(8,128)(2,1)S(1)}, u32[]{:S(2)}, u32[]{:S(2)}) %collective-permute-start.3) | collective-permute-done | bytes 262176 | tf_op jit(solution)/shard_map/ppermute | solution.py:43
  53.0 5.6 %collective-permute-done.4.refs_1_ = bf16[64,2048]{1,0:T(8,128)(2,1)S(1)} collective-permute-done((bf16[64,2048]{1,0:T(8,128)(2,1)S(1)}, bf16[64,2048]{1,0:T(8,128)(2,1)S(1)}, u32[]{:S(2)}, u32[]{:S(2)}) %collective-permute-start.4) | collective-permute-done | bytes 262176 | tf_op jit(solution)/shard_map/ppermute | solution.py:43
  59.2 8.6 %collective-permute-start.11 = (bf16[128,2048]{1,0:T(8,128)(2,1)S(1)}, bf16[128,2048]{1,0:T(8,128)(2,1)S(1)}, u32[]{:S(2)}, u32[]{:S(2)}) collective-permute-start(bf16[128,2048]{1,0:T(8,128)(2,1)S(1)} %join.3.refs_1_), channel_id=1, source_target_pairs={{0,8},{1,9},{2,10},{3,11},{4,12},{5,13},{6,14},{7,15},{8,0},{9,1},... | collective-permute-start | bytes 1572872 | tf_op jit(solution)/shard_map/ppermute | solution.py:43
  70.5 8.7 %collective-permute-done.11.refs_1_ = bf16[128,2048]{1,0:T(8,128)(2,1)S(1)} collective-permute-done((bf16[128,2048]{1,0:T(8,128)(2,1)S(1)}, bf16[128,2048]{1,0:T(8,128)(2,1)S(1)}, u32[]{:S(2)}, u32[]{:S(2)}) %collective-permute-start.11) | collective-permute-done | bytes 524320 | tf_op jit(solution)/shard_map/ppermute | solution.py:43
  81.4 10.0 %collective-permute-done.23.refs_0_ = bf16[128,2048]{1,0:T(8,128)(2,1)} collective-permute-done((bf16[128,2048]{1,0:T(8,128)(2,1)S(1)}, bf16[128,2048]{1,0:T(8,128)(2,1)}, u32[]{:S(2)}, u32[]{:S(2)}) %collective-permute-start.23) | collective-permute-done | bytes 524320 | tf_op jit(solution)/shard_map/ppermute | solution.py:43
  92.9 9.7 %collective-permute-done.24.refs_1_ = bf16[128,2048]{1,0:T(8,128)(2,1)S(1)} collective-permute-done((bf16[128,2048]{1,0:T(8,128)(2,1)S(1)}, bf16[128,2048]{1,0:T(8,128)(2,1)S(1)}, u32[]{:S(2)}, u32[]{:S(2)}) %collective-permute-start.24) | collective-permute-done | bytes 524320 | tf_op jit(solution)/shard_map/ppermute | solution.py:43
  107.0 6.9 %collective-permute-done.34.refs_0_ = bf16[128,2048]{1,0:T(8,128)(2,1)} collective-permute-done((bf16[128,2048]{1,0:T(8,128)(2,1)S(1)}, bf16[128,2048]{1,0:T(8,128)(2,1)}, u32[]{:S(2)}, u32[]{:S(2)}) %collective-permute-start.34) | collective-permute-done | bytes 524320 | tf_op jit(solution)/shard_map/ppermute | solution.py:43
  117.5 8.6 %product.6 = (f32[128,1024]{1,0:T(8,128)}, f32[128,1024]{1,0:T(8,128)}, f32[128,1024]{1,0:T(8,128)S(1)}, f32[128,1024]{1,0:T(8,128)S(1)}, bf16[128,2048]{1,0:T(8,128)(2,1)S(1)}, /*index=5*/bf16[128,2048]{1,0:T(8,128)(2,1)S(1)}) custom-call(s32[1]{0:T(128)} %bitcast.3.odd, bf16[128,2048]{1,0:T(8,128)(2,1)} %collective-permute-done.23.refs_0_, ...), custom_call_target="tpu_custom_call" | custom-call | flops 4294967296 | bytes 15728640 | tf_op jit(solution)/shard_map/product/pallas_call | solution.py:185
  126.2 9.0 %product.7 = (f32[128,1024]{1,0:T(8,128)}, f32[128,1024]{1,0:T(8,128)}, f32[128,1024]{1,0:T(8,128)S(1)}, f32[128,1024]{1,0:T(8,128)S(1)}, bf16[128,2048]{1,0:T(8,128)(2,1)S(1)}, /*index=5*/bf16[128,2048]{1,0:T(8,128)(2,1)S(1)}) custom-call(s32[1]{0:T(128)} %bitcast.3.odd, bf16[128,2048]{1,0:T(8,128)(2,1)} %collective-permute-done.34.refs_0_, ...), custom_call_target="tpu_custom_call" | custom-call | flops 4294967296 | bytes 15728640 | tf_op jit(solution)/shard_map/product/pallas_call | solution.py:185
  137.0 9.6 %product.5 = (f32[192,1024]{1,0:T(8,128)}, f32[192,1024]{1,0:T(8,128)}, f32[192,1024]{1,0:T(8,128)S(1)}, f32[192,1024]{1,0:T(8,128)S(1)}, bf16[192,2048]{1,0:T(8,128)(2,1)S(1)}, /*index=5*/bf16[192,2048]{1,0:T(8,128)(2,1)S(1)}) custom-call(s32[1]{0:T(128)} %bitcast.3.odd, bf16[128,2048]{1,0:T(8,128)(2,1)S(1)} %collective-permute-done.10.refs_0_, ...), custom_call_target="tpu_custom_call" | custom-call | flops 6442450944 | bytes 18874368 | tf_op jit(solution)/shard_map/product/pallas_call | solution.py:185
  149.4 5.9 %product.4 = (f32[64,1024]{1,0:T(8,128)}, f32[64,1024]{1,0:T(8,128)}, f32[64,1024]{1,0:T(8,128)S(1)}, f32[64,1024]{1,0:T(8,128)S(1)}, bf16[64,2048]{1,0:T(8,128)(2,1)S(1)}, /*index=5*/bf16[64,2048]{1,0:T(8,128)(2,1)}) custom-call(s32[1]{0:T(128)} %bitcast.3.odd, bf16[128,2048]{1,0:T(8,128)(2,1)S(1)} %join.2.refs_0_, bf16[128,2048]{1,0:T(8,128)(2,1)S(1)} %join.3.refs_1_, ...), custom_call_target="tpu_custom_call" | custom-call | flops 2147483648 | bytes 12582912 | tf_op jit(solution)/shard_map/product/pallas_call | solution.py:185
  160.5 5.8 %collective-permute-done.16.refs_8_.refs_2_ = bf16[192,2048]{1,0:T(8,128)(2,1)S(1)} collective-permute-done((bf16[192,2048]{1,0:T(8,128)(2,1)S(1)}, bf16[192,2048]{1,0:T(8,128)(2,1)S(1)}, u32[]{:S(2)}, u32[]{:S(2)}) %collective-permute-start.16) | collective-permute-done | bytes 786464 | tf_op jit(solution)/shard_map/ppermute | solution.py:43
  167.3 8.1 %collective-permute-done.17.refs_9_.refs_3_ = bf16[192,2048]{1,0:T(8,128)(2,1)S(1)} collective-permute-done((bf16[192,2048]{1,0:T(8,128)(2,1)S(1)}, bf16[192,2048]{1,0:T(8,128)(2,1)S(1)}, u32[]{:S(2)}, u32[]{:S(2)}) %collective-permute-start.17) | collective-permute-done | bytes 786464 | tf_op jit(solution)/shard_map/ppermute | solution.py:43
  176.4 10.2 %collective-permute-done.28.refs_9_ = bf16[128,2048]{1,0:T(8,128)(2,1)S(1)} collective-permute-done((bf16[128,2048]{1,0:T(8,128)(2,1)S(1)}, bf16[128,2048]{1,0:T(8,128)(2,1)S(1)}, u32[]{:S(2)}, u32[]{:S(2)}) %collective-permute-start.28) | collective-permute-done | bytes 524320 | tf_op jit(solution)/shard_map/ppermute | solution.py:43
  198.3 8.1 %collective-permute-done.30.refs_11_ = bf16[128,1024]{1,0:T(8,128)(2,1)} collective-permute-done((bf16[128,1024]{1,0:T(8,128)(2,1)}, bf16[128,1024]{1,0:T(8,128)(2,1)}, u32[]{:S(2)}, u32[]{:S(2)}) %collective-permute-start.30) | collective-permute-done | bytes 262176 | tf_op jit(solution)/shard_map/ppermute | solution.py:43
  206.4 7.9 %collective-permute-start.43 = (f32[64,1024]{1,0:T(8,128)S(1)}, f32[64,1024]{1,0:T(8,128)S(1)}, u32[]{:S(2)}, u32[]{:S(2)}) collective-permute-start(f32[64,1024]{1,0:T(8,128)S(1)} %get-tuple-element.96), channel_id=1, source_target_pairs={{0,1},{1,0},{2,3},{3,2},{4,5},{5,4},{6,7},{7,6},{8,9},{9,8},{10,11... | collective-permute-start | bytes 786440 | tf_op jit(solution)/shard_map/ppermute | solution.py:43
  241.3 6.7 %collective-permute-done.22.refs_3_ = bf16[64,1024]{1,0:T(8,128)(2,1)S(1)} collective-permute-done((bf16[64,1024]{1,0:T(8,128)(2,1)}, bf16[64,1024]{1,0:T(8,128)(2,1)S(1)}, u32[]{:S(2)}, u32[]{:S(2)}) %collective-permute-start.22) | collective-permute-done | bytes 131104 | tf_op jit(solution)/shard_map/ppermute | solution.py:43
  262.3 7.4 %all-to-all-start = ((bf16[128,32,128]{2,1,0:T(8,128)(2,1)}), bf16[128,32,128]{2,1,0:T(8,128)(2,1)S(1)}, u32[]{:S(2)}, u32[]{:S(2)}) async-start(bf16[128,32,128]{2,1,0:T(8,128)(2,1)} %get-tuple-element.98), calls=%async_computation | async-start | bytes 2097152 | tf_op jit(solution)/shard_map/all_to_all | solution.py:532
  277.5 11.2 %all-to-all-done = bf16[128,32,128]{2,1,0:T(8,128)(2,1)S(1)} async-done(((bf16[128,32,128]{2,1,0:T(8,128)(2,1)}), bf16[128,32,128]{2,1,0:T(8,128)(2,1)S(1)}, u32[]{:S(2)}, u32[]{:S(2)}) %all-to-all-start) | async-done | bytes 1048608 | tf_op jit(solution)/shard_map/all_to_all | solution.py:532
  (184 shorter events, 98.0 us)
Async XLA Ops:
  0.0 115.4 %collective-permute-start.5 = (bf16[2048,1024]{1,0:T(8,128)(2,1)}, bf16[2048,1024]{1,0:T(8,128)(2,1)}, u32[]{:S(2)}, u32[]{:S(2)}) collective-permute-start(bf16[2048,1024]{1,0:T(8,128)(2,1)} %refs_4_.3), channel_id=1, source_target_pairs={{0,1},{1,0},{2,3},{3,2},{4,5},{5,4},{6,7},{7,6},{8,9},{9,8},{10,11... | collective-permute-start | bytes 12582920 | tf_op jit(solution)/shard_map/ppermute | solution.py:43
  30.8 38.5 %collective-permute-start.10 = (bf16[128,2048]{1,0:T(8,128)(2,1)S(1)}, bf16[128,2048]{1,0:T(8,128)(2,1)S(1)}, u32[]{:S(2)}, u32[]{:S(2)}) collective-permute-start(bf16[128,2048]{1,0:T(8,128)(2,1)S(1)} %join.2.refs_0_), channel_id=1, source_target_pairs={{0,8},{1,9},{2,10},{3,11},{4,12},{5,13},{6,14},{7,15},{8,0},{9,1},... | collective-permute-start | bytes 1572872 | tf_op jit(solution)/shard_map/ppermute | solution.py:43
  69.3 22.2 %collective-permute-start.23 = (bf16[128,2048]{1,0:T(8,128)(2,1)S(1)}, bf16[128,2048]{1,0:T(8,128)(2,1)}, u32[]{:S(2)}, u32[]{:S(2)}) collective-permute-start(bf16[128,2048]{1,0:T(8,128)(2,1)S(1)} %collective-permute-done.10.refs_0_), channel_id=1, source_target_pairs={{0,6},{1,7},{2,0},{3,1},{4,2},{5,3},{6,4},{7,5},{8,14},{9,15},{10,... | collective-permute-start | bytes 1572872 | tf_op jit(solution)/shard_map/ppermute | solution.py:43
  79.2 23.5 %collective-permute-start.24 = (bf16[128,2048]{1,0:T(8,128)(2,1)S(1)}, bf16[128,2048]{1,0:T(8,128)(2,1)S(1)}, u32[]{:S(2)}, u32[]{:S(2)}) collective-permute-start(bf16[128,2048]{1,0:T(8,128)(2,1)S(1)} %collective-permute-done.11.refs_1_), channel_id=1, source_target_pairs={{0,6},{1,7},{2,0},{3,1},{4,2},{5,3},{6,4},{7,5},{8,14},{9,15},{10,... | collective-permute-start | bytes 1572872 | tf_op jit(solution)/shard_map/ppermute | solution.py:43
  80.1 23.4 %collective-permute-start.25 = (bf16[128,2048]{1,0:T(8,128)(2,1)S(1)}, bf16[128,2048]{1,0:T(8,128)(2,1)S(1)}, u32[]{:S(2)}, u32[]{:S(2)}) collective-permute-start(bf16[128,2048]{1,0:T(8,128)(2,1)S(1)} %collective-permute-done.10.refs_0_), channel_id=1, source_target_pairs={{0,2},{1,3},{2,4},{3,5},{4,6},{5,7},{6,0},{7,1},{8,10},{9,11},{10,... | collective-permute-start | bytes 1572872 | tf_op jit(solution)/shard_map/ppermute | solution.py:43
  81.3 25.7 %collective-permute-start.26 = (bf16[128,2048]{1,0:T(8,128)(2,1)S(1)}, bf16[128,2048]{1,0:T(8,128)(2,1)}, u32[]{:S(2)}, u32[]{:S(2)}) collective-permute-start(bf16[128,2048]{1,0:T(8,128)(2,1)S(1)} %collective-permute-done.11.refs_1_), channel_id=1, source_target_pairs={{0,2},{1,3},{2,4},{3,5},{4,6},{5,7},{6,0},{7,1},{8,10},{9,11},{10,... | collective-permute-start | bytes 1572872 | tf_op jit(solution)/shard_map/ppermute | solution.py:43
  91.4 22.5 %collective-permute-start.34 = (bf16[128,2048]{1,0:T(8,128)(2,1)S(1)}, bf16[128,2048]{1,0:T(8,128)(2,1)}, u32[]{:S(2)}, u32[]{:S(2)}) collective-permute-start(bf16[128,2048]{1,0:T(8,128)(2,1)S(1)} %collective-permute-done.12.refs_2_), channel_id=1, source_target_pairs={{0,6},{1,7},{2,0},{3,1},{4,2},{5,3},{6,4},{7,5},{8,14},{9,15},{10,... | collective-permute-start | bytes 1572872 | tf_op jit(solution)/shard_map/ppermute | solution.py:43
  103.5 22.6 %collective-permute-start.35 = (bf16[128,2048]{1,0:T(8,128)(2,1)S(1)}, bf16[128,2048]{1,0:T(8,128)(2,1)}, u32[]{:S(2)}, u32[]{:S(2)}) collective-permute-start(bf16[128,2048]{1,0:T(8,128)(2,1)S(1)} %collective-permute-done.15.refs_5_), channel_id=1, source_target_pairs={{0,2},{1,3},{2,4},{3,5},{4,6},{5,7},{6,0},{7,1},{8,10},{9,11},{10,... | collective-permute-start | bytes 1572872 | tf_op jit(solution)/shard_map/ppermute | solution.py:43
  104.3 21.9 %collective-permute-start.36 = (bf16[128,2048]{1,0:T(8,128)(2,1)}, bf16[128,2048]{1,0:T(8,128)(2,1)}, u32[]{:S(2)}, u32[]{:S(2)}) collective-permute-start(bf16[128,2048]{1,0:T(8,128)(2,1)} %collective-permute-done.23.refs_0_), channel_id=1, source_target_pairs={{0,6},{1,7},{2,0},{3,1},{4,2},{5,3},{6,4},{7,5},{8,14},{9,15},{10,... | collective-permute-start | bytes 1572872 | tf_op jit(solution)/shard_map/ppermute | solution.py:43
  113.9 22.4 %collective-permute-start.13 = (bf16[128,2048]{1,0:T(8,128)(2,1)S(1)}, bf16[128,2048]{1,0:T(8,128)(2,1)S(1)}, u32[]{:S(2)}, u32[]{:S(2)}) collective-permute-start(bf16[128,2048]{1,0:T(8,128)(2,1)S(1)} %join.3.refs_1_), channel_id=1, source_target_pairs={{0,6},{1,7},{2,0},{3,1},{4,2},{5,3},{6,4},{7,5},{8,14},{9,15},{10,... | collective-permute-start | bytes 1572872 | tf_op jit(solution)/shard_map/ppermute | solution.py:43
  115.4 21.6 %collective-permute-start.14 = (bf16[128,2048]{1,0:T(8,128)(2,1)S(1)}, bf16[128,2048]{1,0:T(8,128)(2,1)S(1)}, u32[]{:S(2)}, u32[]{:S(2)}) collective-permute-start(bf16[128,2048]{1,0:T(8,128)(2,1)S(1)} %join.2.refs_0_), channel_id=1, source_target_pairs={{0,2},{1,3},{2,4},{3,5},{4,6},{5,7},{6,0},{7,1},{8,10},{9,11},{10,... | collective-permute-start | bytes 1572872 | tf_op jit(solution)/shard_map/ppermute | solution.py:43
  126.1 29.3 %collective-permute-start.27 = (bf16[128,2048]{1,0:T(8,128)(2,1)S(1)}, bf16[128,2048]{1,0:T(8,128)(2,1)S(1)}, u32[]{:S(2)}, u32[]{:S(2)}) collective-permute-start(bf16[128,2048]{1,0:T(8,128)(2,1)S(1)} %get-tuple-element.80), channel_id=1, source_target_pairs={{0,32},{1,33},{2,34},{3,35},{4,36},{5,37},{6,38},{7,39},{8,40},{9,... | collective-permute-start | bytes 1572872 | tf_op jit(solution)/shard_map/ppermute | solution.py:43
  135.2 23.6 %collective-permute-start.38 = (bf16[128,2048]{1,0:T(8,128)(2,1)S(1)}, bf16[128,2048]{1,0:T(8,128)(2,1)S(1)}, u32[]{:S(2)}, u32[]{:S(2)}) collective-permute-start(bf16[128,2048]{1,0:T(8,128)(2,1)S(1)} %get-tuple-element.90), channel_id=1, source_target_pairs={{0,32},{1,33},{2,34},{3,35},{4,36},{5,37},{6,38},{7,39},{8,40},{9,... | collective-permute-start | bytes 1572872 | tf_op jit(solution)/shard_map/ppermute | solution.py:43
  155.3 35.5 %collective-permute-start.6 = (bf16[64,2048]{1,0:T(8,128)(2,1)S(1)}, bf16[64,2048]{1,0:T(8,128)(2,1)S(1)}, u32[]{:S(2)}, u32[]{:S(2)}) collective-permute-start(bf16[64,2048]{1,0:T(8,128)(2,1)S(1)} %get-tuple-element.64), channel_id=1, source_target_pairs={{0,32},{1,33},{2,34},{3,35},{4,36},{5,37},{6,38},{7,39},{8,40},{9,... | collective-permute-start | bytes 786440 | tf_op jit(solution)/shard_map/ppermute | solution.py:43
  158.8 27.8 %collective-permute-start.28 = (bf16[128,2048]{1,0:T(8,128)(2,1)S(1)}, bf16[128,2048]{1,0:T(8,128)(2,1)S(1)}, u32[]{:S(2)}, u32[]{:S(2)}) collective-permute-start(bf16[128,2048]{1,0:T(8,128)(2,1)S(1)} %get-tuple-element.81), channel_id=1, source_target_pairs={{0,96},{1,97},{2,98},{3,99},{4,100},{5,101},{6,102},{7,103},{8,104... | collective-permute-start | bytes 1572872 | tf_op jit(solution)/shard_map/ppermute | solution.py:43
  159.0 31.9 %collective-permute-start.40 = (bf16[128,1024]{1,0:T(8,128)(2,1)S(1)}, bf16[128,1024]{1,0:T(8,128)(2,1)S(1)}, u32[]{:S(2)}, u32[]{:S(2)}) collective-permute-start(bf16[128,1024]{1,0:T(8,128)(2,1)S(1)} %add_convert_fusion.3), channel_id=1, source_target_pairs={{0,32},{1,33},{2,34},{3,35},{4,36},{5,37},{6,38},{7,39},{8,40},{9,... | collective-permute-start | bytes 786440 | tf_op jit(solution)/shard_map/ppermute | solution.py:43
  166.3 27.2 %collective-permute-start.41 = (bf16[128,1024]{1,0:T(8,128)(2,1)S(1)}, bf16[128,1024]{1,0:T(8,128)(2,1)S(1)}, u32[]{:S(2)}, u32[]{:S(2)}) collective-permute-start(bf16[128,1024]{1,0:T(8,128)(2,1)S(1)} %add_convert_fusion.2), channel_id=1, source_target_pairs={{0,96},{1,97},{2,98},{3,99},{4,100},{5,101},{6,102},{7,103},{8,104... | collective-permute-start | bytes 786440 | tf_op jit(solution)/shard_map/ppermute | solution.py:43
  175.4 38.9 %collective-permute-start.18 = (bf16[192,1024]{1,0:T(8,128)(2,1)}, bf16[192,1024]{1,0:T(8,128)(2,1)S(1)}, u32[]{:S(2)}, u32[]{:S(2)}) collective-permute-start(bf16[192,1024]{1,0:T(8,128)(2,1)} %add_convert_fusion.1), channel_id=1, source_target_pairs={{0,32},{1,33},{2,34},{3,35},{4,36},{5,37},{6,38},{7,39},{8,40},{9,... | collective-permute-start | bytes 1179656 | tf_op jit(solution)/shard_map/ppermute | solution.py:43
  186.6 27.7 %collective-permute-start.19 = (bf16[192,1024]{1,0:T(8,128)(2,1)}, bf16[192,1024]{1,0:T(8,128)(2,1)}, u32[]{:S(2)}, u32[]{:S(2)}) collective-permute-start(bf16[192,1024]{1,0:T(8,128)(2,1)} %add_convert_fusion), channel_id=1, source_target_pairs={{0,96},{1,97},{2,98},{3,99},{4,100},{5,101},{6,102},{7,103},{8,104... | collective-permute-start | bytes 1179656 | tf_op jit(solution)/shard_map/ppermute | solution.py:43
  193.6 24.3 %collective-permute-start.7 = (bf16[64,2048]{1,0:T(8,128)(2,1)}, bf16[64,2048]{1,0:T(8,128)(2,1)}, u32[]{:S(2)}, u32[]{:S(2)}) collective-permute-start(bf16[64,2048]{1,0:T(8,128)(2,1)} %get-tuple-element.65), channel_id=1, source_target_pairs={{0,96},{1,97},{2,98},{3,99},{4,100},{5,101},{6,102},{7,103},{8,104... | collective-permute-start | bytes 786440 | tf_op jit(solution)/shard_map/ppermute | solution.py:43
  197.5 25.4 %collective-permute-start.8 = (bf16[64,1024]{1,0:T(8,128)(2,1)S(1)}, bf16[64,1024]{1,0:T(8,128)(2,1)S(1)}, u32[]{:S(2)}, u32[]{:S(2)}) collective-permute-start(bf16[64,1024]{1,0:T(8,128)(2,1)S(1)} %add_convert_fusion.7), channel_id=1, source_target_pairs={{0,32},{1,33},{2,34},{3,35},{4,36},{5,37},{6,38},{7,39},{8,40},{9,... | collective-permute-start | bytes 393224 | tf_op jit(solution)/shard_map/ppermute | solution.py:43
  206.4 25.6 %collective-permute-start.43 = (f32[64,1024]{1,0:T(8,128)S(1)}, f32[64,1024]{1,0:T(8,128)S(1)}, u32[]{:S(2)}, u32[]{:S(2)}) collective-permute-start(f32[64,1024]{1,0:T(8,128)S(1)} %get-tuple-element.96), channel_id=1, source_target_pairs={{0,1},{1,0},{2,3},{3,2},{4,5},{5,4},{6,7},{7,6},{8,9},{9,8},{10,11... | collective-permute-start | bytes 786440 | tf_op jit(solution)/shard_map/ppermute | solution.py:43
  217.8 33.0 %collective-permute-start.32 = (f32[128,1024]{1,0:T(8,128)S(1)}, f32[128,1024]{1,0:T(8,128)S(1)}, u32[]{:S(2)}, u32[]{:S(2)}) collective-permute-start(f32[128,1024]{1,0:T(8,128)S(1)} %get-tuple-element.86), channel_id=1, source_target_pairs={{0,1},{1,0},{2,3},{3,2},{4,5},{5,4},{6,7},{7,6},{8,9},{9,8},{10,11... | collective-permute-start | bytes 1572872 | tf_op jit(solution)/shard_map/ppermute | solution.py:43
  262.3 26.4 %all-to-all-start = ((bf16[128,32,128]{2,1,0:T(8,128)(2,1)}), bf16[128,32,128]{2,1,0:T(8,128)(2,1)S(1)}, u32[]{:S(2)}, u32[]{:S(2)}) async-start(bf16[128,32,128]{2,1,0:T(8,128)(2,1)} %get-tuple-element.98), calls=%async_computation | async-start | bytes 2097152 | tf_op jit(solution)/shard_map/all_to_all | solution.py:532
  (64 other events, 567.2 us)

commit v6 on v5

--- a/solution.py
+++ b/solution.py
@@ -312,10 +312,8 @@
     )(place, slots, mask)
 
 
-def outgoing_kernel(code, *refs):
-    ins = refs[:12]
-    full, out = refs[12:14]
-    full_v, out_v, wide, thin, sems = refs[14:]
+def prefill_kernel(*refs):
+    ins, out, wide, thin, sems = refs[:8], refs[8], refs[9], refs[10], refs[11]
     copies = []
     at = 0
     for k in (0, 2):
@@ -330,14 +328,37 @@
             at += rows
     for copy in copies:
         copy.start()
-    for k, to in ((0, 192), (2, 448)):
-        stay, got = ins[8 + k : 8 + k + 2]
-        full_v[to : to + 64, :] = stay[...] + got[...].astype(F32)
     for copy in copies:
         copy.wait()
-    for at, to in ((0, 0), (192, 256)):
-        full_v[to : to + 192, :] = wide[at : at + 192, :] + thin[at : at + 192, :].astype(F32)
-    save = pltpu.make_async_copy(full_v, full, sems.at[8])
+    out[...] = wide[...] + thin[...].astype(F32)
+
+
+def prefill(*parts):
+    return pl.pallas_call(
+        prefill_kernel,
+        out_shape=jax.ShapeDtypeStruct((384, 1024), F32),
+        in_specs=[ANY] * 8,
+        out_specs=VMEM,
+        scratch_shapes=[
+            pltpu.VMEM((384, 1024), F32),
+            pltpu.VMEM((384, 1024), BF),
+            pltpu.SemaphoreType.DMA((8,)),
+        ],
+        compiler_params=params(8),
+        cost_estimate=cost(0, 4 << 20),
+        name="prefill",
+    )(*parts)
+
+
+def outgoing_kernel(code, ready, *refs):
+    ins = refs[:4]
+    full, out = refs[4:6]
+    full_v, out_v, sems = refs[6:]
+    for k, at, to in ((0, 0, 0), (2, 192, 256)):
+        full_v[to : to + 192, :] = ready[at : at + 192, :]
+        stay, got = ins[k : k + 2]
+        full_v[to + 192 : to + 256, :] = stay[...] + got[...].astype(F32)
+    save = pltpu.make_async_copy(full_v, full, sems.at[0])
     save.start()
 
     def gather(s, carry):
@@ -355,30 +376,28 @@
     for k in range(4):
         part = pl.ds(32 * k, 32)
         lax.fori_loop(32 * k, 32 * k + 32, gather, 0, unroll=4)
-        sends.append(pltpu.make_async_copy(out_v.at[part], out.at[part], sems.at[9 + k]))
+        sends.append(pltpu.make_async_copy(out_v.at[part], out.at[part], sems.at[1 + k]))
         sends[-1].start()
     for copy in sends:
         copy.wait()
     save.wait()
 
 
-def outgoing(code, *parts):
+def outgoing(code, ready, *parts):
     return pl.pallas_call(
         outgoing_kernel,
         out_shape=[pltpu.HBM((512, 1024), F32), pltpu.HBM((128, 32, 128), BF)],
-        in_specs=[SMEM] + [ANY] * 8 + [VMEM] * 4,
+        in_specs=[SMEM] + [VMEM] * 5,
         out_specs=[HBM] * 2,
         scratch_shapes=[
             pltpu.VMEM((512, 1024), F32),
             pltpu.VMEM((128, 32, 128), BF),
-            pltpu.VMEM((384, 1024), F32),
-            pltpu.VMEM((384, 1024), BF),
-            pltpu.SemaphoreType.DMA((13,)),
+            pltpu.SemaphoreType.DMA((5,)),
         ],
         compiler_params=params(12),
         cost_estimate=cost(0, 6 << 20),
         name="outgoing",
-    )(code, *parts)
+    )(code, ready, *parts)
 
 
 def base_kernel(row_of, mask, full, amp, occ, vir, base, scale):
@@ -528,7 +547,8 @@
 
     mask = tile_mask.reshape(-1)
     inverse, code, row_of = index(jnp.stack([x, c]), partner_slot.reshape(-1), mask)
-    full, out = outgoing(code, *last)
+    ready = prefill(*last[:8])
+    full, out = outgoing(code, ready, *last[8:])
     incoming = lax.all_to_all(out, AXES, split_axis=0, concat_axis=0, tiled=True)
     base, scale = make_base(
         row_of, mask, full, amplitudes, occ_energy[:, None], vir_energy[None, :]

time: 293 us -> 264 us (0.901)
  waiting for transfers between devices: 118 us -> 95.2 us
  local copies, waits for them, and re-layouts: 24.5 us -> 8.69 us
  starting transfers between devices: 87.4 us -> 102 us
  other arithmetic: 4.74 us -> 0.69 us
    ppermute x45, waiting for transfers between devices: 107 us -> 84 us  [send(): return lax.ppermute(value, AXES, pairs)]
    unnamed x86 -> x48, local copies, waits for them, and re-layouts: 24.1 us -> 8.28 us
    ppermute x45, starting transfers between devices: 80 us -> 94.7 us  [send(): return lax.ppermute(value, AXES, pairs)]
  transfers between devices with their start and end apart: 46 -> 46, of which waited for: 19 -> 19; matrix products, arithmetic and copies ran while one was open for 2% -> 0% of each run, Pallas kernels for 17% -> 19%
where the time goes in v6:
time: 264 us; the launch traced here: 263 us
  starting transfers between devices  102 us (39%)
  waiting for transfers between devices  95.2 us (36%)
  Pallas kernels  56.1 us (21%)
  local copies, waits for them, and re-layouts  8.69 us (3%)
    ppermute x45, starting transfers between devices, send(): return lax.ppermute(value, AXES, pairs)  94.7 us
    ppermute x45, waiting for transfers between devices, send(): return lax.ppermute(value, AXES, pairs)  84 us
    pallas_call x4, Pallas kernels, product(): pl.pallas_call(functools.partial(product_kernel, steps), out_shape=[pltpu...  31 us
    all_to_all x1, waiting for transfers between devices, compute(): lax.all_to_all(out, AXES, split_axis=0, concat_axis=0, tiled=True)  11.2 us
    unnamed x48, local copies, waits for them, and re-layouts  8.28 us
    pallas_call x3, Pallas kernels, collect(): pl.pallas_call(functools.partial(collect_kernel, len(groups), members), o...  7.71 us
    all_to_all x1, starting transfers between devices, compute(): lax.all_to_all(out, AXES, split_axis=0, concat_axis=0, tiled=True)  6.97 us
  transfers between devices with their start and end apart: 46, of which 19 were waited for; matrix products, arithmetic and copies ran while one was open for 0% of the time, Pallas kernels for 19%

profile of v6, /device:TPU:1, one launch (start us, length us, event | category | flops | bytes accessed | tf_op | source)
XLA Modules:
  0.0 263.1 jit_solution(12153687886184156711)
XLA Ops:
  3.8 5.3 %collective-permute-done.got = bf16[256,1024]{1,0:T(8,128)(2,1)S(1)} collective-permute-done((bf16[256,1024]{1,0:T(8,128)(2,1)S(1)}, bf16[256,1024]{1,0:T(8,128)(2,1)S(1)}, u32[]{:S(2)}, u32[]{:S(2)}) %collective-permute-start) | collective-permute-done | bytes 524320 | tf_op jit(solution)/shard_map/ppermute | solution.py:43
  9.9 7.9 %collective-permute-start.2 = (bf16[64,2048]{1,0:T(8,128)(2,1)S(1)}, bf16[64,2048]{1,0:T(8,128)(2,1)S(1)}, u32[]{:S(2)}, u32[]{:S(2)}) collective-permute-start(bf16[64,2048]{1,0:T(8,128)(2,1)S(1)} %get-tuple-element.59), channel_id=1, source_target_pairs={{0,4},{1,5},{2,20},{3,21},{4,34},{5,35},{6,50},{7,51},{8,64},{9,65... | collective-permute-start | bytes 786440 | tf_op jit(solution)/shard_map/ppermute | solution.py:43
  17.8 4.3 %collective-permute-start.3 = (bf16[64,2048]{1,0:T(8,128)(2,1)S(1)}, bf16[64,2048]{1,0:T(8,128)(2,1)S(1)}, u32[]{:S(2)}, u32[]{:S(2)}) collective-permute-start(bf16[64,2048]{1,0:T(8,128)(2,1)S(1)} %get-tuple-element.60), channel_id=1, source_target_pairs={{0,2},{1,3},{2,18},{3,19},{4,32},{5,33},{6,48},{7,49},{8,70},{9,71... | collective-permute-start | bytes 786440 | tf_op jit(solution)/shard_map/ppermute | solution.py:43
  22.1 6.7 %collective-permute-start.4 = (bf16[64,2048]{1,0:T(8,128)(2,1)S(1)}, bf16[64,2048]{1,0:T(8,128)(2,1)S(1)}, u32[]{:S(2)}, u32[]{:S(2)}) collective-permute-start(bf16[64,2048]{1,0:T(8,128)(2,1)S(1)} %get-tuple-element.61), channel_id=1, source_target_pairs={{0,6},{1,7},{2,22},{3,23},{4,36},{5,37},{6,52},{7,53},{8,66},{9,67... | collective-permute-start | bytes 786440 | tf_op jit(solution)/shard_map/ppermute | solution.py:43
  33.7 8.4 %collective-permute-start.10 = (bf16[128,2048]{1,0:T(8,128)(2,1)S(1)}, bf16[128,2048]{1,0:T(8,128)(2,1)S(1)}, u32[]{:S(2)}, u32[]{:S(2)}) collective-permute-start(bf16[128,2048]{1,0:T(8,128)(2,1)S(1)} %join.2.refs_0_), channel_id=1, source_target_pairs={{0,8},{1,9},{2,10},{3,11},{4,12},{5,13},{6,14},{7,15},{8,0},{9,1},... | collective-permute-start | bytes 1572872 | tf_op jit(solution)/shard_map/ppermute | solution.py:43
  42.8 8.0 %collective-permute-start.11 = (bf16[128,2048]{1,0:T(8,128)(2,1)S(1)}, bf16[128,2048]{1,0:T(8,128)(2,1)S(1)}, u32[]{:S(2)}, u32[]{:S(2)}) collective-permute-start(bf16[128,2048]{1,0:T(8,128)(2,1)S(1)} %join.3.refs_1_), channel_id=1, source_target_pairs={{0,8},{1,9},{2,10},{3,11},{4,12},{5,13},{6,14},{7,15},{8,0},{9,1},... | collective-permute-start | bytes 1572872 | tf_op jit(solution)/shard_map/ppermute | solution.py:43
  54.4 5.4 %collective-permute-start.23 = (bf16[128,2048]{1,0:T(8,128)(2,1)S(1)}, bf16[128,2048]{1,0:T(8,128)(2,1)S(1)}, u32[]{:S(2)}, u32[]{:S(2)}) collective-permute-start(bf16[128,2048]{1,0:T(8,128)(2,1)S(1)} %collective-permute-done.10.refs_0_), channel_id=1, source_target_pairs={{0,6},{1,7},{2,0},{3,1},{4,2},{5,3},{6,4},{7,5},{8,14},{9,15},{10,... | collective-permute-start | bytes 1572872 | tf_op jit(solution)/shard_map/ppermute | solution.py:43
  59.8 5.8 %collective-permute-done.11.refs_1_ = bf16[128,2048]{1,0:T(8,128)(2,1)S(1)} collective-permute-done((bf16[128,2048]{1,0:T(8,128)(2,1)S(1)}, bf16[128,2048]{1,0:T(8,128)(2,1)S(1)}, u32[]{:S(2)}, u32[]{:S(2)}) %collective-permute-start.11) | collective-permute-done | bytes 524320 | tf_op jit(solution)/shard_map/ppermute | solution.py:43
  65.6 5.4 %collective-permute-start.24 = (bf16[128,2048]{1,0:T(8,128)(2,1)S(1)}, bf16[128,2048]{1,0:T(8,128)(2,1)}, u32[]{:S(2)}, u32[]{:S(2)}) collective-permute-start(bf16[128,2048]{1,0:T(8,128)(2,1)S(1)} %collective-permute-done.11.refs_1_), channel_id=1, source_target_pairs={{0,6},{1,7},{2,0},{3,1},{4,2},{5,3},{6,4},{7,5},{8,14},{9,15},{10,... | collective-permute-start | bytes 1572872 | tf_op jit(solution)/shard_map/ppermute | solution.py:43
  75.8 5.2 %product.4 = (f32[64,1024]{1,0:T(8,128)}, f32[64,1024]{1,0:T(8,128)}, f32[64,1024]{1,0:T(8,128)S(1)}, f32[64,1024]{1,0:T(8,128)S(1)}, bf16[64,2048]{1,0:T(8,128)(2,1)S(1)}, /*index=5*/bf16[64,2048]{1,0:T(8,128)(2,1)S(1)}) custom-call(s32[1]{0:T(128)} %bitcast.3.odd, bf16[128,2048]{1,0:T(8,128)(2,1)S(1)} %join.2.refs_0_, bf16[128,2048]{1,0:T(8,128)(2,1)S(1)} %join.3.refs_1_, ...), custom_call_target="tpu_custom_call" | custom-call | flops 2147483648 | bytes 12582912 | tf_op jit(solution)/shard_map/product/pallas_call | solution.py:185
  81.0 4.7 %collective-permute-done.24.refs_1_ = bf16[128,2048]{1,0:T(8,128)(2,1)} collective-permute-done((bf16[128,2048]{1,0:T(8,128)(2,1)S(1)}, bf16[128,2048]{1,0:T(8,128)(2,1)}, u32[]{:S(2)}, u32[]{:S(2)}) %collective-permute-start.24) | collective-permute-done | bytes 524320 | tf_op jit(solution)/shard_map/ppermute | solution.py:43
  87.2 8.6 %collective-permute-done.26.refs_3_ = bf16[128,2048]{1,0:T(8,128)(2,1)} collective-permute-done((bf16[128,2048]{1,0:T(8,128)(2,1)S(1)}, bf16[128,2048]{1,0:T(8,128)(2,1)}, u32[]{:S(2)}, u32[]{:S(2)}) %collective-permute-start.26) | collective-permute-done | bytes 524320 | tf_op jit(solution)/shard_map/ppermute | solution.py:43
  95.7 8.8 %product.6 = (f32[128,1024]{1,0:T(8,128)}, f32[128,1024]{1,0:T(8,128)}, f32[128,1024]{1,0:T(8,128)S(1)}, f32[128,1024]{1,0:T(8,128)S(1)}, bf16[128,2048]{1,0:T(8,128)(2,1)S(1)}, /*index=5*/bf16[128,2048]{1,0:T(8,128)(2,1)S(1)}) custom-call(s32[1]{0:T(128)} %bitcast.3.odd, bf16[128,2048]{1,0:T(8,128)(2,1)S(1)} %collective-permute-done.23.refs_0_, ...), custom_call_target="tpu_custom_call" | custom-call | flops 4294967296 | bytes 15728640 | tf_op jit(solution)/shard_map/product/pallas_call | solution.py:185
  106.9 9.7 %product.5 = (f32[192,1024]{1,0:T(8,128)}, f32[192,1024]{1,0:T(8,128)}, f32[192,1024]{1,0:T(8,128)S(1)}, f32[192,1024]{1,0:T(8,128)S(1)}, bf16[192,2048]{1,0:T(8,128)(2,1)S(1)}, /*index=5*/bf16[192,2048]{1,0:T(8,128)(2,1)S(1)}) custom-call(s32[1]{0:T(128)} %bitcast.3.odd, bf16[128,2048]{1,0:T(8,128)(2,1)S(1)} %collective-permute-done.10.refs_0_, ...), custom_call_target="tpu_custom_call" | custom-call | flops 6442450944 | bytes 18874368 | tf_op jit(solution)/shard_map/product/pallas_call | solution.py:185
  119.6 9.8 %collective-permute-done.37.refs_3_ = bf16[128,2048]{1,0:T(8,128)(2,1)S(1)} collective-permute-done((bf16[128,2048]{1,0:T(8,128)(2,1)}, bf16[128,2048]{1,0:T(8,128)(2,1)S(1)}, u32[]{:S(2)}, u32[]{:S(2)}) %collective-permute-start.37) | collective-permute-done | bytes 524320 | tf_op jit(solution)/shard_map/ppermute | solution.py:43
  129.3 7.4 %product.7 = (f32[128,1024]{1,0:T(8,128)}, f32[128,1024]{1,0:T(8,128)}, f32[128,1024]{1,0:T(8,128)S(1)}, f32[128,1024]{1,0:T(8,128)S(1)}, bf16[128,2048]{1,0:T(8,128)(2,1)S(1)}, /*index=5*/bf16[128,2048]{1,0:T(8,128)(2,1)S(1)}) custom-call(s32[1]{0:T(128)} %bitcast.3.odd, bf16[128,2048]{1,0:T(8,128)(2,1)S(1)} %collective-permute-done.34.refs_0_, ...), custom_call_target="tpu_custom_call" | custom-call | flops 4294967296 | bytes 15728640 | tf_op jit(solution)/shard_map/product/pallas_call | solution.py:185
  138.3 7.9 %collective-permute-done.27.refs_8_ = bf16[128,2048]{1,0:T(8,128)(2,1)S(1)} collective-permute-done((bf16[128,2048]{1,0:T(8,128)(2,1)S(1)}, bf16[128,2048]{1,0:T(8,128)(2,1)S(1)}, u32[]{:S(2)}, u32[]{:S(2)}) %collective-permute-start.27) | collective-permute-done | bytes 524320 | tf_op jit(solution)/shard_map/ppermute | solution.py:43
  146.5 11.0 %collective-permute-done.38.refs_2_ = bf16[128,2048]{1,0:T(8,128)(2,1)S(1)} collective-permute-done((bf16[128,2048]{1,0:T(8,128)(2,1)S(1)}, bf16[128,2048]{1,0:T(8,128)(2,1)S(1)}, u32[]{:S(2)}, u32[]{:S(2)}) %collective-permute-start.38) | collective-permute-done | bytes 524320 | tf_op jit(solution)/shard_map/ppermute | solution.py:43
  160.6 5.4 %collective-permute-done.39.refs_3_ = bf16[128,2048]{1,0:T(8,128)(2,1)S(1)} collective-permute-done((bf16[128,2048]{1,0:T(8,128)(2,1)S(1)}, bf16[128,2048]{1,0:T(8,128)(2,1)S(1)}, u32[]{:S(2)}, u32[]{:S(2)}) %collective-permute-start.39) | collective-permute-done | bytes 524320 | tf_op jit(solution)/shard_map/ppermute | solution.py:43
  174.3 5.7 %collective-permute-done.19.refs_11_.refs_5_ = bf16[192,1024]{1,0:T(8,128)(2,1)S(1)} collective-permute-done((bf16[192,1024]{1,0:T(8,128)(2,1)S(1)}, bf16[192,1024]{1,0:T(8,128)(2,1)S(1)}, u32[]{:S(2)}, u32[]{:S(2)}) %collective-permute-start.19) | collective-permute-done | bytes 393248 | tf_op jit(solution)/shard_map/ppermute | solution.py:43
  184.4 16.5 %collective-permute-start.32 = (f32[128,1024]{1,0:T(8,128)}, f32[128,1024]{1,0:T(8,128)S(1)}, u32[]{:S(2)}, u32[]{:S(2)}) collective-permute-start(f32[128,1024]{1,0:T(8,128)} %get-tuple-element.86), channel_id=1, source_target_pairs={{0,1},{1,0},{2,3},{3,2},{4,5},{5,4},{6,7},{7,6},{8,9},{9,8},{10,11... | collective-permute-start | bytes 1572872 | tf_op jit(solution)/shard_map/ppermute | solution.py:43
  221.6 4.3 %index.1 = (s32[512]{0:T(512)S(1)}, s32[512]{0:T(512)S(1)}, s32[64]{0:T(128)S(1)}) custom-call(s32[2]{0:T(128)S(1)} %pad_add_fusion.place, s32[512]{0:T(512)S(1)} %reshape.9.slots, s32[512]{0:T(512)S(1)} %reshape.10.mask), custom_call_target="tpu_custom_call" | custom-call | bytes 8192 | tf_op jit(solution)/shard_map/index/pallas_call | solution.py:303
  233.2 7.0 %all-to-all-start = ((bf16[128,32,128]{2,1,0:T(8,128)(2,1)}), bf16[128,32,128]{2,1,0:T(8,128)(2,1)S(1)}, u32[]{:S(2)}, u32[]{:S(2)}) async-start(bf16[128,32,128]{2,1,0:T(8,128)(2,1)} %get-tuple-element.98), calls=%async_computation | async-start | bytes 2097152 | tf_op jit(solution)/shard_map/all_to_all | solution.py:552
  248.0 11.2 %all-to-all-done = bf16[128,32,128]{2,1,0:T(8,128)(2,1)S(1)} async-done(((bf16[128,32,128]{2,1,0:T(8,128)(2,1)}), bf16[128,32,128]{2,1,0:T(8,128)(2,1)S(1)}, u32[]{:S(2)}, u32[]{:S(2)}) %all-to-all-start) | async-done | bytes 1048608 | tf_op jit(solution)/shard_map/all_to_all | solution.py:552
  (147 shorter events, 82.1 us)
Async XLA Ops:
  0.0 75.6 %collective-permute-start.5 = (bf16[2048,1024]{1,0:T(8,128)(2,1)}, bf16[2048,1024]{1,0:T(8,128)(2,1)}, u32[]{:S(2)}, u32[]{:S(2)}) collective-permute-start(bf16[2048,1024]{1,0:T(8,128)(2,1)} %refs_4_.3), channel_id=1, source_target_pairs={{0,1},{1,0},{2,3},{3,2},{4,5},{5,4},{6,7},{7,6},{8,9},{9,8},{10,11... | collective-permute-start | bytes 12582920 | tf_op jit(solution)/shard_map/ppermute | solution.py:43
  9.9 23.3 %collective-permute-start.2 = (bf16[64,2048]{1,0:T(8,128)(2,1)S(1)}, bf16[64,2048]{1,0:T(8,128)(2,1)S(1)}, u32[]{:S(2)}, u32[]{:S(2)}) collective-permute-start(bf16[64,2048]{1,0:T(8,128)(2,1)S(1)} %get-tuple-element.59), channel_id=1, source_target_pairs={{0,4},{1,5},{2,20},{3,21},{4,34},{5,35},{6,50},{7,51},{8,64},{9,65... | collective-permute-start | bytes 786440 | tf_op jit(solution)/shard_map/ppermute | solution.py:43
  17.8 24.4 %collective-permute-start.3 = (bf16[64,2048]{1,0:T(8,128)(2,1)S(1)}, bf16[64,2048]{1,0:T(8,128)(2,1)S(1)}, u32[]{:S(2)}, u32[]{:S(2)}) collective-permute-start(bf16[64,2048]{1,0:T(8,128)(2,1)S(1)} %get-tuple-element.60), channel_id=1, source_target_pairs={{0,2},{1,3},{2,18},{3,19},{4,32},{5,33},{6,48},{7,49},{8,70},{9,71... | collective-permute-start | bytes 786440 | tf_op jit(solution)/shard_map/ppermute | solution.py:43
  33.7 20.7 %collective-permute-start.10 = (bf16[128,2048]{1,0:T(8,128)(2,1)S(1)}, bf16[128,2048]{1,0:T(8,128)(2,1)S(1)}, u32[]{:S(2)}, u32[]{:S(2)}) collective-permute-start(bf16[128,2048]{1,0:T(8,128)(2,1)S(1)} %join.2.refs_0_), channel_id=1, source_target_pairs={{0,8},{1,9},{2,10},{3,11},{4,12},{5,13},{6,14},{7,15},{8,0},{9,1},... | collective-permute-start | bytes 1572872 | tf_op jit(solution)/shard_map/ppermute | solution.py:43
  42.8 22.9 %collective-permute-start.11 = (bf16[128,2048]{1,0:T(8,128)(2,1)S(1)}, bf16[128,2048]{1,0:T(8,128)(2,1)S(1)}, u32[]{:S(2)}, u32[]{:S(2)}) collective-permute-start(bf16[128,2048]{1,0:T(8,128)(2,1)S(1)} %join.3.refs_1_), channel_id=1, source_target_pairs={{0,8},{1,9},{2,10},{3,11},{4,12},{5,13},{6,14},{7,15},{8,0},{9,1},... | collective-permute-start | bytes 1572872 | tf_op jit(solution)/shard_map/ppermute | solution.py:43
  50.8 20.3 %collective-permute-start.15 = (bf16[128,2048]{1,0:T(8,128)(2,1)S(1)}, bf16[128,2048]{1,0:T(8,128)(2,1)S(1)}, u32[]{:S(2)}, u32[]{:S(2)}) collective-permute-start(bf16[128,2048]{1,0:T(8,128)(2,1)S(1)} %join.3.refs_1_), channel_id=1, source_target_pairs={{0,2},{1,3},{2,4},{3,5},{4,6},{5,7},{6,0},{7,1},{8,10},{9,11},{10,... | collective-permute-start | bytes 1572872 | tf_op jit(solution)/shard_map/ppermute | solution.py:43
  71.9 23.9 %collective-permute-start.26 = (bf16[128,2048]{1,0:T(8,128)(2,1)S(1)}, bf16[128,2048]{1,0:T(8,128)(2,1)}, u32[]{:S(2)}, u32[]{:S(2)}) collective-permute-start(bf16[128,2048]{1,0:T(8,128)(2,1)S(1)} %collective-permute-done.11.refs_1_), channel_id=1, source_target_pairs={{0,2},{1,3},{2,4},{3,5},{4,6},{5,7},{6,0},{7,1},{8,10},{9,11},{10,... | collective-permute-start | bytes 1572872 | tf_op jit(solution)/shard_map/ppermute | solution.py:43
  74.3 30.2 %collective-permute-start.13 = (bf16[128,2048]{1,0:T(8,128)(2,1)S(1)}, bf16[128,2048]{1,0:T(8,128)(2,1)S(1)}, u32[]{:S(2)}, u32[]{:S(2)}) collective-permute-start(bf16[128,2048]{1,0:T(8,128)(2,1)S(1)} %join.3.refs_1_), channel_id=1, source_target_pairs={{0,6},{1,7},{2,0},{3,1},{4,2},{5,3},{6,4},{7,5},{8,14},{9,15},{10,... | collective-permute-start | bytes 1572872 | tf_op jit(solution)/shard_map/ppermute | solution.py:43
  75.6 31.2 %collective-permute-start.14 = (bf16[128,2048]{1,0:T(8,128)(2,1)S(1)}, bf16[128,2048]{1,0:T(8,128)(2,1)S(1)}, u32[]{:S(2)}, u32[]{:S(2)}) collective-permute-start(bf16[128,2048]{1,0:T(8,128)(2,1)S(1)} %join.2.refs_0_), channel_id=1, source_target_pairs={{0,2},{1,3},{2,4},{3,5},{4,6},{5,7},{6,0},{7,1},{8,10},{9,11},{10,... | collective-permute-start | bytes 1572872 | tf_op jit(solution)/shard_map/ppermute | solution.py:43
  85.7 30.8 %collective-permute-start.34 = (bf16[128,2048]{1,0:T(8,128)(2,1)S(1)}, bf16[128,2048]{1,0:T(8,128)(2,1)S(1)}, u32[]{:S(2)}, u32[]{:S(2)}) collective-permute-start(bf16[128,2048]{1,0:T(8,128)(2,1)S(1)} %copy-done.7), channel_id=1, source_target_pairs={{0,6},{1,7},{2,0},{3,1},{4,2},{5,3},{6,4},{7,5},{8,14},{9,15},{10,... | collective-permute-start | bytes 1572872 | tf_op jit(solution)/shard_map/ppermute | solution.py:43
  87.0 32.3 %collective-permute-start.35 = (bf16[128,2048]{1,0:T(8,128)(2,1)S(1)}, bf16[128,2048]{1,0:T(8,128)(2,1)S(1)}, u32[]{:S(2)}, u32[]{:S(2)}) collective-permute-start(bf16[128,2048]{1,0:T(8,128)(2,1)S(1)} %collective-permute-done.15.refs_5_), channel_id=1, source_target_pairs={{0,2},{1,3},{2,4},{3,5},{4,6},{5,7},{6,0},{7,1},{8,10},{9,11},{10,... | collective-permute-start | bytes 1572872 | tf_op jit(solution)/shard_map/ppermute | solution.py:43
  95.7 23.6 %collective-permute-start.36 = (bf16[128,2048]{1,0:T(8,128)(2,1)S(1)}, bf16[128,2048]{1,0:T(8,128)(2,1)S(1)}, u32[]{:S(2)}, u32[]{:S(2)}) collective-permute-start(bf16[128,2048]{1,0:T(8,128)(2,1)S(1)} %collective-permute-done.23.refs_0_), channel_id=1, source_target_pairs={{0,6},{1,7},{2,0},{3,1},{4,2},{5,3},{6,4},{7,5},{8,14},{9,15},{10,... | collective-permute-start | bytes 1572872 | tf_op jit(solution)/shard_map/ppermute | solution.py:43
  104.5 24.8 %collective-permute-start.37 = (bf16[128,2048]{1,0:T(8,128)(2,1)}, bf16[128,2048]{1,0:T(8,128)(2,1)S(1)}, u32[]{:S(2)}, u32[]{:S(2)}) collective-permute-start(bf16[128,2048]{1,0:T(8,128)(2,1)} %collective-permute-done.26.refs_3_), channel_id=1, source_target_pairs={{0,2},{1,3},{2,4},{3,5},{4,6},{5,7},{6,0},{7,1},{8,10},{9,11},{10,... | collective-permute-start | bytes 1572872 | tf_op jit(solution)/shard_map/ppermute | solution.py:43
  106.9 29.9 %collective-permute-start.6 = (bf16[64,2048]{1,0:T(8,128)(2,1)S(1)}, bf16[64,2048]{1,0:T(8,128)(2,1)S(1)}, u32[]{:S(2)}, u32[]{:S(2)}) collective-permute-start(bf16[64,2048]{1,0:T(8,128)(2,1)S(1)} %get-tuple-element.64), channel_id=1, source_target_pairs={{0,32},{1,33},{2,34},{3,35},{4,36},{5,37},{6,38},{7,39},{8,40},{9,... | collective-permute-start | bytes 786440 | tf_op jit(solution)/shard_map/ppermute | solution.py:43
  116.5 51.0 %collective-permute-start.7 = (bf16[64,2048]{1,0:T(8,128)(2,1)S(1)}, bf16[64,2048]{1,0:T(8,128)(2,1)S(1)}, u32[]{:S(2)}, u32[]{:S(2)}) collective-permute-start(bf16[64,2048]{1,0:T(8,128)(2,1)S(1)} %get-tuple-element.65), channel_id=1, source_target_pairs={{0,96},{1,97},{2,98},{3,99},{4,100},{5,101},{6,102},{7,103},{8,104... | collective-permute-start | bytes 786440 | tf_op jit(solution)/shard_map/ppermute | solution.py:43
  119.3 38.2 %collective-permute-start.16 = (bf16[192,2048]{1,0:T(8,128)(2,1)S(1)}, bf16[192,2048]{1,0:T(8,128)(2,1)S(1)}, u32[]{:S(2)}, u32[]{:S(2)}) collective-permute-start(bf16[192,2048]{1,0:T(8,128)(2,1)S(1)} %get-tuple-element.70), channel_id=1, source_target_pairs={{0,32},{1,33},{2,34},{3,35},{4,36},{5,37},{6,38},{7,39},{8,40},{9,... | collective-permute-start | bytes 2359304 | tf_op jit(solution)/shard_map/ppermute | solution.py:43
  119.3 26.9 %collective-permute-start.27 = (bf16[128,2048]{1,0:T(8,128)(2,1)S(1)}, bf16[128,2048]{1,0:T(8,128)(2,1)S(1)}, u32[]{:S(2)}, u32[]{:S(2)}) collective-permute-start(bf16[128,2048]{1,0:T(8,128)(2,1)S(1)} %get-tuple-element.80), channel_id=1, source_target_pairs={{0,32},{1,33},{2,34},{3,35},{4,36},{5,37},{6,38},{7,39},{8,40},{9,... | collective-permute-start | bytes 1572872 | tf_op jit(solution)/shard_map/ppermute | solution.py:43
  136.7 20.7 %collective-permute-start.38 = (bf16[128,2048]{1,0:T(8,128)(2,1)S(1)}, bf16[128,2048]{1,0:T(8,128)(2,1)S(1)}, u32[]{:S(2)}, u32[]{:S(2)}) collective-permute-start(bf16[128,2048]{1,0:T(8,128)(2,1)S(1)} %get-tuple-element.90), channel_id=1, source_target_pairs={{0,32},{1,33},{2,34},{3,35},{4,36},{5,37},{6,38},{7,39},{8,40},{9,... | collective-permute-start | bytes 1572872 | tf_op jit(solution)/shard_map/ppermute | solution.py:43
  167.6 39.0 %collective-permute-start.40 = (bf16[128,1024]{1,0:T(8,128)(2,1)S(1)}, bf16[128,1024]{1,0:T(8,128)(2,1)S(1)}, u32[]{:S(2)}, u32[]{:S(2)}) collective-permute-start(bf16[128,1024]{1,0:T(8,128)(2,1)S(1)} %add_convert_fusion.3), channel_id=1, source_target_pairs={{0,32},{1,33},{2,34},{3,35},{4,36},{5,37},{6,38},{7,39},{8,40},{9,... | collective-permute-start | bytes 786440 | tf_op jit(solution)/shard_map/ppermute | solution.py:43
  167.7 38.9 %collective-permute-start.41 = (bf16[128,1024]{1,0:T(8,128)(2,1)S(1)}, bf16[128,1024]{1,0:T(8,128)(2,1)S(1)}, u32[]{:S(2)}, u32[]{:S(2)}) collective-permute-start(bf16[128,1024]{1,0:T(8,128)(2,1)S(1)} %add_convert_fusion.2), channel_id=1, source_target_pairs={{0,96},{1,97},{2,98},{3,99},{4,100},{5,101},{6,102},{7,103},{8,104... | collective-permute-start | bytes 786440 | tf_op jit(solution)/shard_map/ppermute | solution.py:43
  171.6 29.2 %collective-permute-start.8 = (bf16[64,1024]{1,0:T(8,128)(2,1)S(1)}, bf16[64,1024]{1,0:T(8,128)(2,1)S(1)}, u32[]{:S(2)}, u32[]{:S(2)}) collective-permute-start(bf16[64,1024]{1,0:T(8,128)(2,1)S(1)} %add_convert_fusion.7), channel_id=1, source_target_pairs={{0,32},{1,33},{2,34},{3,35},{4,36},{5,37},{6,38},{7,39},{8,40},{9,... | collective-permute-start | bytes 393224 | tf_op jit(solution)/shard_map/ppermute | solution.py:43
  171.6 29.2 %collective-permute-start.9 = (bf16[64,1024]{1,0:T(8,128)(2,1)S(1)}, bf16[64,1024]{1,0:T(8,128)(2,1)S(1)}, u32[]{:S(2)}, u32[]{:S(2)}) collective-permute-start(bf16[64,1024]{1,0:T(8,128)(2,1)S(1)} %add_convert_fusion.6), channel_id=1, source_target_pairs={{0,96},{1,97},{2,98},{3,99},{4,100},{5,101},{6,102},{7,103},{8,104... | collective-permute-start | bytes 393224 | tf_op jit(solution)/shard_map/ppermute | solution.py:43
  184.4 41.5 %collective-permute-start.32 = (f32[128,1024]{1,0:T(8,128)}, f32[128,1024]{1,0:T(8,128)S(1)}, u32[]{:S(2)}, u32[]{:S(2)}) collective-permute-start(f32[128,1024]{1,0:T(8,128)} %get-tuple-element.86), channel_id=1, source_target_pairs={{0,1},{1,0},{2,3},{3,2},{4,5},{5,4},{6,7},{7,6},{8,9},{9,8},{10,11... | collective-permute-start | bytes 1572872 | tf_op jit(solution)/shard_map/ppermute | solution.py:43
  233.2 25.9 %all-to-all-start = ((bf16[128,32,128]{2,1,0:T(8,128)(2,1)}), bf16[128,32,128]{2,1,0:T(8,128)(2,1)S(1)}, u32[]{:S(2)}, u32[]{:S(2)}) async-start(bf16[128,32,128]{2,1,0:T(8,128)(2,1)} %get-tuple-element.98), calls=%async_computation | async-start | bytes 2097152 | tf_op jit(solution)/shard_map/all_to_all | solution.py:552
  (45 other events, 525.4 us)
